TPU v7x, 32 devices: a whole 2x2x4 slice. The times are simulated.
32 devices in a mesh: groups: 2 (over y), space: 4 (over z), chan: 2 (over x), rep: 2 (over core).
Axes of the slice: x: 2, y: 2, z: 4, core: 2. Of those that a mesh axis runs over, the one named last changes fastest.
Arguments:
- volume: bfloat16 [4, 8, 32, 8, 128], P(('groups', 'rep'), 'space', 'chan'), parts along dimension 0, may hold values from -6 to 6
- early_weight: bfloat16 [3, 3, 3, 128, 128], replicated, may hold values from -0.109375 to 0.109375
- late_weight: bfloat16 [3, 3, 3, 128, 512], P(None, None, None, None, 'chan'), may hold values from -0.109375 to 0.109375
- cotangent: bfloat16 [4, 4, 16, 4, 512], P(('groups', 'rep'), 'space', None, None, 'chan'), parts along dimension 0, may hold values from -6 to 6
Outputs:
- grad_early: bfloat16 [6, 3, 3, 128, 128], P('groups'), parts along dimension 0
- grad_late: bfloat16 [6, 3, 3, 128, 512], P('groups', None, None, None, 'chan'), parts along dimension 0
- grad_volume: bfloat16 [4, 8, 32, 8, 128], P(('groups', 'rep'), 'space', 'chan'), parts along dimension 0
There are 2 independent parts, one for each index of `groups`. A program takes and returns all parts, laid end to end along the dimension named above; an argument that names none is the same for every part. Nothing has to cross between parts.
All inputs are finite; a program needn't handle non-finite values.
Results may differ from a plain program's by a relative error of at most 0.0065.
Values may be sent and summed in bfloat16 or wider, within the bound.
No kernel may reach another device: no remote copies, remote signals or barrier semaphores. Data moves between devices by JAX's collectives and lax.ppermute only.
A program may use at most 64 MiB of HBM per device.

v0:
```python
import math

import jax
import jax.numpy as jnp
from jax import lax
from jax.sharding import PartitionSpec as P


def padded_2(block, sides, width):
    for axis, dim in sides:
        count = lax.axis_size(axis)
        forward = [(i, i + 1) for i in range(count - 1)]
        backward = [(target, source) for source, target in forward]
        low = lax.ppermute(
            lax.slice_in_dim(block, block.shape[dim] - width, None, axis=dim), axis, forward
        )
        high = lax.ppermute(lax.slice_in_dim(block, 0, width, axis=dim), axis, backward)
        block = jnp.concatenate([low, block, high], axis=dim)
    return block


def gelu_tanh(value):
    return jax.nn.gelu(value, approximate=True)


def conv_padded(padded, weight):
    depth = padded.shape[1] - 2
    height = padded.shape[2] - 2
    length = padded.shape[3] - 2
    total = None
    for first in range(3):
        for second in range(3):
            for third in range(3):
                window = padded[
                    :, first : first + depth, second : second + height, third : third + length
                ]
                term = jnp.einsum(
                    "sxyzc,co->sxyzo",
                    window,
                    weight[first, second, third],
                    preferred_element_type=jnp.float32,
                )
                total = term if total is None else total + term
    return total


def kernel_grad(padded, delta):
    depth = delta.shape[1]
    height = delta.shape[2]
    length = delta.shape[3]
    planes = []
    for first in range(3):
        for second in range(3):
            for third in range(3):
                window = padded[
                    :, first : first + depth, second : second + height, third : third + length
                ]
                planes.append(
                    jnp.einsum("sxyzc,sxyzo->co", window, delta, preferred_element_type=jnp.float32)
                )
    stacked = jnp.stack(planes, axis=0)
    return stacked.reshape((3, 3, 3) + stacked.shape[1:])


def flipped(weight):
    return jnp.swapaxes(weight[::-1, ::-1, ::-1], 3, 4)


def pad_dims(field, dims):
    widths = [(1, 1) if place in dims else (0, 0) for place in range(field.ndim)]
    return jnp.pad(field, widths)


def pool_cells(field):
    s, x, y, z, c = field.shape
    return jnp.mean(field.reshape(s, x // 2, 2, y // 2, 2, z // 2, 2, c), axis=(2, 4, 6))


def spread_cells(field):
    s, x, y, z, c = field.shape
    wide = jnp.broadcast_to(field[:, :, None, :, None, :, None, :], (s, x, 2, y, 2, z, 2, c))
    return wide.reshape(s, 2 * x, 2 * y, 2 * z, c) * 0.125


def late_layer(joined, late_weight, cotangent):
    rim = padded_2(joined, (("space", 1),), 1)
    late_pad = pad_dims(rim, (2, 3))
    pre_late = conv_padded(late_pad, late_weight)
    delta_late = jax.vjp(gelu_tanh, pre_late)[1](cotangent.astype(jnp.float32))[0].astype(
        jnp.bfloat16
    )
    late_part = kernel_grad(late_pad, delta_late)
    delta_rim = padded_2(delta_late, (("space", 1),), 1)
    back_partial = conv_padded(pad_dims(delta_rim, (2, 3)), flipped(late_weight))
    return (back_partial, late_part)


def per_device(volume, early_weight, late_weight, cotangent):
    count = (
        cotangent.shape[0]
        * lax.axis_size("rep")
        * cotangent.shape[1]
        * lax.axis_size("space")
        * cotangent.shape[2]
        * cotangent.shape[3]
    )
    scale = 1.0 / math.sqrt(count)
    haloed = padded_2(volume, (("space", 1), ("chan", 2)), 1)
    padded_in = pad_dims(haloed, (3,))
    pre_early = conv_padded(padded_in, early_weight)
    pooled = pool_cells(gelu_tanh(pre_early)).astype(jnp.bfloat16)
    joined = lax.all_gather(pooled, "chan", axis=2, tiled=True)
    back_partial, late_part = late_layer(joined, late_weight, cotangent)
    back_rows = lax.psum_scatter(back_partial, "chan", scatter_dimension=2, tiled=True)
    delta_early = jax.vjp(gelu_tanh, pre_early)[1](spread_cells(back_rows))[0].astype(jnp.bfloat16)
    early_part = kernel_grad(padded_in, delta_early)
    delta_halo = padded_2(delta_early, (("space", 1), ("chan", 2)), 1)
    grad_volume = conv_padded(pad_dims(delta_halo, (3,)), flipped(early_weight)).astype(
        jnp.bfloat16
    )
    early_total = lax.psum(early_part, ("space", "chan", "rep"))
    grad_early = (early_total * scale).astype(jnp.bfloat16)
    late_total = lax.psum(late_part, ("space", "rep"))
    grad_late = (late_total * scale).astype(jnp.bfloat16)
    return (grad_early, grad_late, grad_volume)


def solution(mesh):
    return jax.shard_map(
        per_device,
        mesh=mesh,
        in_specs=(
            P(("groups", "rep"), "space", "chan", None, None),
            P(),
            P(None, None, None, None, "chan"),
            P(("groups", "rep"), "space", None, None, "chan"),
        ),
        out_specs=(
            P("groups", None, None, None, None),
            P("groups", None, None, None, "chan"),
            P(("groups", "rep"), "space", "chan", None, None),
        ),
        check_vma=False,
    )
```

profile of v0, /device:TPU:0, one launch (start us, length us, event | category | flops | bytes accessed | tf_op | source)
XLA Modules:
  0.0 279.8 jit_solution(17251219886939649005)
XLA Ops:
  7.2 0.8 fusion.308
  8.0 4.9 %collective-permute-start = (bf16[1,1,16,8,128]{4,3,2,1,0:T(8,128)(2,1)S(1)}, bf16[1,1,16,8,128]{4,3,2,1,0:T(8,128)(2,1)S(1)}, u32[]{:S(2)}, u32[]{:S(2)}) collective-permute-start(bf16[1,1,16,8,128]{4,3,2,1,0:T(8,128)(2,1)S(1)} %get-tuple-element.12), channel_id=1, source_target_pairs={{0,4},{4,8},{8,12},{1,5},{5,9},{9,13},{2,6},{6,10},{10,14},{3,7},{... | collective-permute-start | bytes 98312 | tf_op jit(solution)/shard_map/ppermute | solution.py:14
  12.9 1.4 collective-permute-start.1
  14.4 3.8 %copy.129 = bf16[3,3,3,128,256]{3,4,2,1,0:T(8,128)(2,1)} copy(bf16[3,3,3,128,256]{4,3,2,1,0:T(8,128)(2,1)} %param.6) | data formatting | bytes 3538944 | tf_op args[2]
  18.2 0.6 collective-permute-done.1
  18.9 3.4 %collective-permute-start.2 = (bf16[1,4,1,8,128]{4,3,2,1,0:T(8,128)(2,1)S(1)}, bf16[1,4,1,8,128]{4,3,2,1,0:T(8,128)(2,1)S(1)}, u32[]{:S(2)}, u32[]{:S(2)}) collective-permute-start(bf16[1,4,1,8,128]{4,3,2,1,0:T(8,128)(2,1)S(1)} %get-tuple-element.7), channel_id=1, source_target_pairs={{0,2},{1,3},{4,6},{5,7},{8,10},{9,11},{12,14},{13,15},{16,18},{17,... | collective-permute-start | bytes 24584 | tf_op jit(solution)/shard_map/ppermute | solution.py:14
  22.3 1.4 collective-permute-start.3
  23.7 1.6 reverse_bitcast_fusion
  25.3 1.7 copy.133
  27.0 1.0 collective-permute-done.3
  32.5 4.5 %all-gather = bf16[16,4,128]{2,0,1:T(8,128)(2,1)S(1)} all-gather(bf16[8,4,128]{2,0,1:T(8,128)(2,1)S(1)} %fusion.279), channel_id=2, replica_groups=mesh['groups'=2,'space'=4,'chan'=2,'rep'=2] {'chan'}, dimensions={0}, use_global_device_ids=true | all-gather | bytes 24576 | tf_op jit(solution)/shard_map/all_gather | solution.py:112
  37.0 3.9 %collective-permute-start.4 = (bf16[1,1,16,4,128]{4,2,3,1,0:T(8,128)(2,1)S(1)}, bf16[1,1,16,4,128]{4,2,3,1,0:T(8,128)(2,1)S(1)}, u32[]{:S(2)}, u32[]{:S(2)}) collective-permute-start(bf16[1,1,16,4,128]{4,2,3,1,0:T(8,128)(2,1)S(1)} %bitcast.1506), channel_id=1, source_target_pairs={{0,4},{4,8},{8,12},{1,5},{5,9},{9,13},{2,6},{6,10},{10,14},{3,7},{... | collective-permute-start | bytes 49160 | tf_op jit(solution)/shard_map/ppermute | solution.py:14
  41.0 1.3 collective-permute-start.5
  42.3 1.2 reverse_bitcast_fusion.1
  43.5 3.1 %collective-permute-done.5 = bf16[1,1,16,4,128]{4,2,3,1,0:T(8,128)(2,1)S(1)} collective-permute-done((bf16[1,1,16,4,128]{4,2,3,1,0:T(8,128)(2,1)S(1)}, bf16[1,1,16,4,128]{4,2,3,1,0:T(8,128)(2,1)S(1)}, u32[]{:S(2)}, u32[]{:S(2)}) %collective-permute-start.5) | collective-permute-done | bytes 16416 | tf_op jit(solution)/shard_map/ppermute | solution.py:17
  50.5 3.5 %collective-permute-start.6 = (bf16[1,1,16,4,256]{4,2,3,1,0:T(8,128)(2,1)S(1)}, bf16[1,1,16,4,256]{4,2,3,1,0:T(8,128)(2,1)S(1)}, u32[]{:S(2)}, u32[]{:S(2)}) collective-permute-start(bf16[1,1,16,4,256]{4,2,3,1,0:T(8,128)(2,1)S(1)} %fusion.92), channel_id=1, source_target_pairs={{0,4},{4,8},{8,12},{1,5},{5,9},{9,13},{2,6},{6,10},{10,14},{3,7},{... | collective-permute-start | bytes 98312 | tf_op jit(solution)/shard_map/ppermute | solution.py:14
  54.0 1.3 collective-permute-start.7
  60.1 1.8 copy-done.1
  65.6 0.8 fusion.64
  66.5 0.9 fusion.2
  67.3 10.6 %reduce-scatter.2.cloned.1.call-done = f32[1,1,8,4,128]{4,2,3,1,0:T(8,128)} async-done(((f32[1,1,16,4,128]{4,2,3,1,0:T(8,128)}), f32[1,1,8,4,128]{4,2,3,1,0:T(8,128)}) %reduce-scatter.2.cloned.1.call-update) | async-done | bytes 16400 | tf_op jit(solution)/shard_map/reduce_scatter | solution.py:114
  77.9 0.7 multiply_bitcast_fusion.1
  79.1 0.9 fusion.60
  80.0 0.2 fusion.59
  80.4 0.2 fusion.57
  80.7 0.2 fusion.56
  81.8 0.2 fusion.51
  82.0 0.2 fusion.50
  82.7 0.2 fusion.47
  83.4 0.2 fusion.44
  83.8 0.2 fusion.42
  84.0 0.2 fusion.41
  84.5 0.2 fusion.39
  84.7 0.2 fusion.38
  85.6 1.2 copy-done.4
  87.0 3.4 %collective-permute-start.8 = (bf16[1,1,16,8,128]{4,3,2,1,0:T(8,128)(2,1)S(1)}, bf16[1,1,16,8,128]{4,3,2,1,0:T(8,128)(2,1)S(1)}, u32[]{:S(2)}, u32[]{:S(2)}) collective-permute-start(bf16[1,1,16,8,128]{4,3,2,1,0:T(8,128)(2,1)S(1)} %get-tuple-element.9), channel_id=1, source_target_pairs={{0,4},{4,8},{8,12},{1,5},{5,9},{9,13},{2,6},{6,10},{10,14},{3,7},{... | collective-permute-start | bytes 98312 | tf_op jit(solution)/shard_map/ppermute | solution.py:14
  90.4 1.3 collective-permute-start.9
  91.7 0.9 fusion.1
  92.6 3.8 %collective-permute-done.9 = bf16[1,1,16,8,128]{4,3,2,1,0:T(8,128)(2,1)S(1)} collective-permute-done((bf16[1,1,16,8,128]{4,3,2,1,0:T(8,128)(2,1)S(1)}, bf16[1,1,16,8,128]{4,3,2,1,0:T(8,128)(2,1)S(1)}, u32[]{:S(2)}, u32[]{:S(2)}) %collective-permute-start.9) | collective-permute-done | bytes 32800 | tf_op jit(solution)/shard_map/ppermute | solution.py:17
  96.4 2.7 collective-permute-start.10
  99.1 1.3 collective-permute-start.11
  100.4 0.8 fusion
  101.3 3.4 %collective-permute-done.11 = bf16[1,4,1,8,128]{4,3,2,1,0:T(8,128)(2,1)S(1)} collective-permute-done((bf16[1,4,1,8,128]{4,3,2,1,0:T(8,128)(2,1)S(1)}, bf16[1,4,1,8,128]{4,3,2,1,0:T(8,128)(2,1)S(1)}, u32[]{:S(2)}, u32[]{:S(2)}) %collective-permute-start.11) | collective-permute-done | bytes 8224 | tf_op jit(solution)/shard_map/ppermute | solution.py:17
  109.0 0.8 fusion.34
  109.8 74.2 %all-reduce.7.cloned.1.call-done = f32[3,3,3,128,128]{4,3,2,1,0:T(8,128)} async-done(((f32[3,3,3,128,128]{4,3,2,1,0:T(8,128)}), f32[3,3,3,128,128]{4,3,2,1,0:T(8,128)}) %all-reduce.7.cloned.1.call-update) | async-done | bytes 1769488 | tf_op jit(solution)/shard_map/psum | solution.py:121
  184.0 2.6 multiply_convert_fusion.1
  186.6 83.0 %all-reduce.9.cloned.1.call-done = f32[3,3,3,128,256]{4,3,2,1,0:T(8,128)} async-done(((f32[3,3,3,128,256]{4,3,2,1,0:T(8,128)}), f32[3,3,3,128,256]{4,3,2,1,0:T(8,128)}) %all-reduce.9.cloned.1.call-update) | async-done | bytes 3538960 | tf_op jit(solution)/shard_map/psum | solution.py:123
  269.6 3.7 %multiply_convert_fusion = bf16[3,3,3,128,256]{4,3,2,1,0:T(8,128)(2,1)} fusion(f32[3,3,3,128,256]{4,3,2,1,0:T(8,128)} %all-reduce.9.cloned.1.call-done), kind=kLoop, calls=%fused_computation | loop fusion | flops 1769472 | bytes 5308416 | tf_op jit(solution)/shard_map/convert_element_type | solution.py:124
  (207 shorter events, 24.9 us)
Async XLA Ops:
  7.2 70.8 %reduce-scatter.2.cloned.1.call-start = ((), (), s32[]{:S(2)}) async-start(), calls=%async_computation.1 | async-start | bytes 49152 | tf_op jit(solution)/shard_map/reduce_scatter | solution.py:114
  8.0 10.2 %collective-permute-start = (bf16[1,1,16,8,128]{4,3,2,1,0:T(8,128)(2,1)S(1)}, bf16[1,1,16,8,128]{4,3,2,1,0:T(8,128)(2,1)S(1)}, u32[]{:S(2)}, u32[]{:S(2)}) collective-permute-start(bf16[1,1,16,8,128]{4,3,2,1,0:T(8,128)(2,1)S(1)} %get-tuple-element.12), channel_id=1, source_target_pairs={{0,4},{4,8},{8,12},{1,5},{5,9},{9,13},{2,6},{6,10},{10,14},{3,7},{... | collective-permute-start | bytes 98312 | tf_op jit(solution)/shard_map/ppermute | solution.py:14
  12.9 5.3 %copy-start.3 = (bf16[1,2,16,8,128]{4,3,2,1,0:T(8,128)(2,1)S(1)}, bf16[1,2,16,8,128]{4,3,2,1,0:T(8,128)(2,1)}, u32[]{:S(2)}) copy-start(bf16[1,2,16,8,128]{4,3,2,1,0:T(8,128)(2,1)} %param.4) | copy-start | bytes 196612
  12.9 5.9 %collective-permute-start.1 = (bf16[1,1,16,8,128]{4,3,2,1,0:T(8,128)(2,1)S(1)}, bf16[1,1,16,8,128]{4,3,2,1,0:T(8,128)(2,1)S(1)}, u32[]{:S(2)}, u32[]{:S(2)}) collective-permute-start(bf16[1,1,16,8,128]{4,3,2,1,0:T(8,128)(2,1)S(1)} %get-tuple-element.11), channel_id=1, source_target_pairs={{4,0},{8,4},{12,8},{5,1},{9,5},{13,9},{6,2},{10,6},{14,10},{7,3},{... | collective-permute-start | bytes 98312 | tf_op jit(solution)/shard_map/ppermute | solution.py:17
  18.2 11.2 %copy-start.13 = (bf16[1,1,16,8,128]{4,3,2,1,0:T(8,128)(2,1)}, bf16[1,1,16,8,128]{4,3,2,1,0:T(8,128)(2,1)S(1)}, u32[]{:S(2)}) copy-start(bf16[1,1,16,8,128]{4,3,2,1,0:T(8,128)(2,1)S(1)} %collective-permute-done) | copy-start | bytes 98308
  18.9 13.1 %copy-start.11 = (bf16[1,1,16,8,128]{4,3,2,1,0:T(8,128)(2,1)}, bf16[1,1,16,8,128]{4,3,2,1,0:T(8,128)(2,1)S(1)}, u32[]{:S(2)}) copy-start(bf16[1,1,16,8,128]{4,3,2,1,0:T(8,128)(2,1)S(1)} %collective-permute-done.1) | copy-start | bytes 98308
  18.9 8.1 %collective-permute-start.2 = (bf16[1,4,1,8,128]{4,3,2,1,0:T(8,128)(2,1)S(1)}, bf16[1,4,1,8,128]{4,3,2,1,0:T(8,128)(2,1)S(1)}, u32[]{:S(2)}, u32[]{:S(2)}) collective-permute-start(bf16[1,4,1,8,128]{4,3,2,1,0:T(8,128)(2,1)S(1)} %get-tuple-element.7), channel_id=1, source_target_pairs={{0,2},{1,3},{4,6},{5,7},{8,10},{9,11},{12,14},{13,15},{16,18},{17,... | collective-permute-start | bytes 24584 | tf_op jit(solution)/shard_map/ppermute | solution.py:14
  22.3 3.0 %copy-start.2 = (bf16[3,3,3,128,128]{4,3,2,1,0:T(8,128)(2,1)S(1)}, bf16[3,3,3,128,128]{4,3,2,1,0:T(8,128)(2,1)}, u32[]{:S(2)}) copy-start(bf16[3,3,3,128,128]{4,3,2,1,0:T(8,128)(2,1)} %param.5) | copy-start | bytes 2654212
  22.3 5.7 %collective-permute-start.3 = (bf16[1,4,1,8,128]{4,3,2,1,0:T(8,128)(2,1)S(1)}, bf16[1,4,1,8,128]{4,3,2,1,0:T(8,128)(2,1)S(1)}, u32[]{:S(2)}, u32[]{:S(2)}) collective-permute-start(bf16[1,4,1,8,128]{4,3,2,1,0:T(8,128)(2,1)S(1)} %get-tuple-element.8), channel_id=1, source_target_pairs={{2,0},{3,1},{6,4},{7,5},{10,8},{11,9},{14,12},{15,13},{18,16},{19,... | collective-permute-start | bytes 24584 | tf_op jit(solution)/shard_map/ppermute | solution.py:17
  27.0 4.6 %copy-start.9 = (bf16[1,4,1,8,128]{4,3,2,1,0:T(8,128)(2,1)}, bf16[1,4,1,8,128]{4,3,2,1,0:T(8,128)(2,1)S(1)}, u32[]{:S(2)}) copy-start(bf16[1,4,1,8,128]{4,3,2,1,0:T(8,128)(2,1)S(1)} %collective-permute-done.2) | copy-start | bytes 24580
  28.0 4.3 %copy-start.7 = (bf16[1,4,1,8,128]{4,3,2,1,0:T(8,128)(2,1)}, bf16[1,4,1,8,128]{4,3,2,1,0:T(8,128)(2,1)S(1)}, u32[]{:S(2)}) copy-start(bf16[1,4,1,8,128]{4,3,2,1,0:T(8,128)(2,1)S(1)} %collective-permute-done.3) | copy-start | bytes 24580
  32.5 14.1 %copy-start = (bf16[3,3,3,128,256]{4,3,2,1,0:T(8,128)(2,1)S(1)}, bf16[3,3,3,128,256]{4,3,2,1,0:T(8,128)(2,1)}, u32[]{:S(2)}) copy-start(bf16[3,3,3,128,256]{4,3,2,1,0:T(8,128)(2,1)} %param.6) | copy-start | bytes 5308420
  37.0 6.5 %collective-permute-start.4 = (bf16[1,1,16,4,128]{4,2,3,1,0:T(8,128)(2,1)S(1)}, bf16[1,1,16,4,128]{4,2,3,1,0:T(8,128)(2,1)S(1)}, u32[]{:S(2)}, u32[]{:S(2)}) collective-permute-start(bf16[1,1,16,4,128]{4,2,3,1,0:T(8,128)(2,1)S(1)} %bitcast.1506), channel_id=1, source_target_pairs={{0,4},{4,8},{8,12},{1,5},{5,9},{9,13},{2,6},{6,10},{10,14},{3,7},{... | collective-permute-start | bytes 49160 | tf_op jit(solution)/shard_map/ppermute | solution.py:14
  41.0 5.6 %collective-permute-start.5 = (bf16[1,1,16,4,128]{4,2,3,1,0:T(8,128)(2,1)S(1)}, bf16[1,1,16,4,128]{4,2,3,1,0:T(8,128)(2,1)S(1)}, u32[]{:S(2)}, u32[]{:S(2)}) collective-permute-start(bf16[1,1,16,4,128]{4,2,3,1,0:T(8,128)(2,1)S(1)} %bitcast.1507), channel_id=1, source_target_pairs={{4,0},{8,4},{12,8},{5,1},{9,5},{13,9},{6,2},{10,6},{14,10},{7,3},{... | collective-permute-start | bytes 49160 | tf_op jit(solution)/shard_map/ppermute | solution.py:17
  48.0 2.3 copy-start.15
  50.5 9.6 %collective-permute-start.6 = (bf16[1,1,16,4,256]{4,2,3,1,0:T(8,128)(2,1)S(1)}, bf16[1,1,16,4,256]{4,2,3,1,0:T(8,128)(2,1)S(1)}, u32[]{:S(2)}, u32[]{:S(2)}) collective-permute-start(bf16[1,1,16,4,256]{4,2,3,1,0:T(8,128)(2,1)S(1)} %fusion.92), channel_id=1, source_target_pairs={{0,4},{4,8},{8,12},{1,5},{5,9},{9,13},{2,6},{6,10},{10,14},{3,7},{... | collective-permute-start | bytes 98312 | tf_op jit(solution)/shard_map/ppermute | solution.py:14
  54.0 7.9 %collective-permute-start.7 = (bf16[1,1,16,4,256]{4,2,3,1,0:T(8,128)(2,1)S(1)}, bf16[1,1,16,4,256]{4,2,3,1,0:T(8,128)(2,1)S(1)}, u32[]{:S(2)}, u32[]{:S(2)}) collective-permute-start(bf16[1,1,16,4,256]{4,2,3,1,0:T(8,128)(2,1)S(1)} %fusion.92), channel_id=1, source_target_pairs={{4,0},{8,4},{12,8},{5,1},{9,5},{13,9},{6,2},{10,6},{14,10},{7,3},{... | collective-permute-start | bytes 98312 | tf_op jit(solution)/shard_map/ppermute | solution.py:17
  60.1 1.8 copy-start.1
  66.4 117.6 %all-reduce.7.cloned.1.call-start = ((), (), s32[]{:S(2)}) async-start(), calls=%async_computation.2 | async-start | bytes 3538944 | tf_op jit(solution)/shard_map/psum | solution.py:121
  78.8 6.6 %copy-start.5 = (bf16[2,16,8,128]{3,2,1,0:T(8,128)(2,1)}, bf16[2,16,8,128]{3,2,1,0:T(8,128)(2,1)S(1)}, u32[]{:S(2)}) copy-start(bf16[2,16,8,128]{3,2,1,0:T(8,128)(2,1)S(1)} %fusion.84) | copy-start | bytes 196612
  78.8 1.6 copy-start.14
  80.2 0.9 copy-start.8
  80.9 0.9 copy-start.10
  83.6 0.9 copy-start.12
  85.6 1.2 copy-start.4
  86.8 182.8 %all-reduce.9.cloned.1.call-start = ((), (), s32[]{:S(2)}) async-start(), calls=%async_computation.3 | async-start | bytes 7077888 | tf_op jit(solution)/shard_map/psum | solution.py:123
  87.0 5.6 %collective-permute-start.8 = (bf16[1,1,16,8,128]{4,3,2,1,0:T(8,128)(2,1)S(1)}, bf16[1,1,16,8,128]{4,3,2,1,0:T(8,128)(2,1)S(1)}, u32[]{:S(2)}, u32[]{:S(2)}) collective-permute-start(bf16[1,1,16,8,128]{4,3,2,1,0:T(8,128)(2,1)S(1)} %get-tuple-element.9), channel_id=1, source_target_pairs={{0,4},{4,8},{8,12},{1,5},{5,9},{9,13},{2,6},{6,10},{10,14},{3,7},{... | collective-permute-start | bytes 98312 | tf_op jit(solution)/shard_map/ppermute | solution.py:14
  90.4 6.0 %collective-permute-start.9 = (bf16[1,1,16,8,128]{4,3,2,1,0:T(8,128)(2,1)S(1)}, bf16[1,1,16,8,128]{4,3,2,1,0:T(8,128)(2,1)S(1)}, u32[]{:S(2)}, u32[]{:S(2)}) collective-permute-start(bf16[1,1,16,8,128]{4,3,2,1,0:T(8,128)(2,1)S(1)} %get-tuple-element.10), channel_id=1, source_target_pairs={{4,0},{8,4},{12,8},{5,1},{9,5},{13,9},{6,2},{10,6},{14,10},{7,3},{... | collective-permute-start | bytes 98312 | tf_op jit(solution)/shard_map/ppermute | solution.py:17
  96.4 4.9 %collective-permute-start.10 = (bf16[1,4,1,8,128]{4,3,2,1,0:T(8,128)(2,1)S(1)}, bf16[1,4,1,8,128]{4,3,2,1,0:T(8,128)(2,1)S(1)}, u32[]{:S(2)}, u32[]{:S(2)}) collective-permute-start(bf16[1,4,1,8,128]{4,3,2,1,0:T(8,128)(2,1)S(1)} %get-tuple-element.5), channel_id=1, source_target_pairs={{0,2},{1,3},{4,6},{5,7},{8,10},{9,11},{12,14},{13,15},{16,18},{17,... | collective-permute-start | bytes 24584 | tf_op jit(solution)/shard_map/ppermute | solution.py:14
  99.1 5.5 %collective-permute-start.11 = (bf16[1,4,1,8,128]{4,3,2,1,0:T(8,128)(2,1)S(1)}, bf16[1,4,1,8,128]{4,3,2,1,0:T(8,128)(2,1)S(1)}, u32[]{:S(2)}, u32[]{:S(2)}) collective-permute-start(bf16[1,4,1,8,128]{4,3,2,1,0:T(8,128)(2,1)S(1)} %get-tuple-element.6), channel_id=1, source_target_pairs={{2,0},{3,1},{6,4},{7,5},{10,8},{11,9},{14,12},{15,13},{18,16},{19,... | collective-permute-start | bytes 24584 | tf_op jit(solution)/shard_map/ppermute | solution.py:17
  105.5 1.4 copy-start.6
Sparse Core Ops, SparseCore 0:
  66.6 11.3 reduce-scatter.1
  87.0 96.9 all-reduce.6
  186.5 83.0 all-reduce.8
where the time goes:
time: 281 us; the launch traced here: 280 us
  waiting for transfers between devices  180 us (64%)
  matrix products  31.2 us (11%)
  starting transfers between devices  30 us (11%)
  between operations  14.4 us (5%)
  local copies, waits for them, and re-layouts  12.3 us (4%)
  other arithmetic  7.75 us (3%)
  blocking collectives  4.48 us (2%)
    psum x1, waiting for transfers between devices, per_device(): late_total = lax.psum(late_part, ('space', 'rep'))  83 us
    psum x1, waiting for transfers between devices, per_device(): early_total = lax.psum(early_part, ('space', 'chan', 'rep'))  74.2 us
    ppermute x6, starting transfers between devices, padded_2(): lax.ppermute(lax.slice_in_dim(block, block.shape[dim] - width, None, axis...  21.8 us
    dot_general x108, matrix products, conv_padded(): jnp.einsum('sxyzc,co->sxyzo', window, weight[first, second, third], prefe...  17.4 us
    dot_general x54, matrix products, kernel_grad(): jnp.einsum('sxyzc,sxyzo->co', window, delta, preferred_element_type=jnp.f...  13.9 us
    ppermute x6, waiting for transfers between devices, padded_2(): lax.ppermute(lax.slice_in_dim(block, 0, width, axis=dim), axis, backward)  11.9 us
    reduce_scatter x1, waiting for transfers between devices, per_device(): lax.psum_scatter(back_partial, 'chan', scatter_dimension=2, tiled=True)  10.6 us
    unnamed x36, local copies, waits for them, and re-layouts  8.58 us
  transfers between devices with their start and end apart: 15, of which 8 were waited for; matrix products, arithmetic and copies ran while one was open for 8% of the time, Pallas kernels for 0%

commit v1 on v0

--- a/solution.py
+++ b/solution.py
@@ -1,9 +1,17 @@
+import functools
 import math
 
 import jax
 import jax.numpy as jnp
 from jax import lax
+from jax.experimental import pallas as pl
+from jax.experimental.pallas import tpu as pltpu
 from jax.sharding import PartitionSpec as P
+
+BF = jnp.bfloat16
+F32 = jnp.float32
+VMEM_BYTES = 56 * 2**20
+GATHER_BLOCKS = 8
 
 
 def padded_2(block, sides, width):
@@ -125,9 +133,314 @@
     return (grad_early, grad_late, grad_volume)
 
 
+NT = (((1,), (1,)), ((), ()))
+
+
+def gelu_and_slope(v):
+    k = 0.7978845608028654
+    sq = v * v
+    t = jnp.tanh(k * (v + 0.044715 * (v * sq)))
+    half = 0.5 * (1.0 + t)
+    return v * half, half + 0.5 * v * (1.0 - t * t) * (k * (1.0 + 0.134145 * sq))
+
+
+def depth_of(rows, period):
+    return lax.broadcasted_iota(jnp.int32, (rows, 128), 0) % period
+
+
+def shifted(ref, lead, start, rows, cell, period, step):
+    dy, dz = step
+    got = ref[lead + (pl.ds(start + dy * period + dz, rows), slice(None))]
+    if dz == 0:
+        return got
+    lanes = got.shape[1] // 128
+    edge = (cell == 0) if dz < 0 else (cell == period - 1)
+    edge = jnp.concatenate([edge] * lanes, axis=1) if lanes > 1 else edge
+    return jnp.where(edge, 0.0, got)
+
+
+STEPS = [(b, c) for b in (-1, 0, 1) for c in (-1, 0, 1)]
+
+
+def prep_kernel(we_ref, wcat_ref, wt_ref):
+    for n in range(9):
+        b, c = divmod(n, 3)
+        for a in range(3):
+            w = we_ref[a, b, c]
+            wcat_ref[pl.ds(n * 128, 128), pl.ds(a * 128, 128)] = w
+            wt_ref[a, pl.ds(n * 128, 128), :] = w.astype(F32).T.astype(BF)
+
+
+def forward_kernel(
+    pos_ref, *refs, nk, nj, dims
+):
+    gx, gy, gz, lx, ly, lz, bx, by = dims
+    blocks = refs[: nk * nj]
+    wcat_ref, wl_ref = refs[nk * nj : nk * nj + 2]
+    col_ref, slope_ref, pd_ref, back_ref = refs[nk * nj + 2 : nk * nj + 6]
+    vol_ref, p_ref, h_ref, pool_ref, lcol_ref, dl_ref = refs[nk * nj + 6 :]
+    k, j = pos_ref[0], pos_ref[1]
+    plane, lplane = gy * gz, ly * lz
+    brows = by * gz
+    cl = wl_ref.shape[-1]
+    crow = bx // 2 * lplane
+
+    vol_ref[:, pl.ds(0, 16), :] = jnp.zeros((gx, 16, 128), F32)
+    vol_ref[:, pl.ds(16 + plane, 16), :] = jnp.zeros((gx, 16, 128), F32)
+    for dj in range(nj):
+        for dk in range(nk):
+            src = blocks[dj * nk + dk]
+            kk = lax.rem(k + nk - dk, nk)
+            jj = lax.rem(j + nj - dj, nj)
+            row = pl.multiple_of(16 + jj * brows, 8)
+            for q in range(bx):
+                vol_ref[kk * bx + q, pl.ds(row, brows), :] = src[pl.ds(q * brows, brows), :].astype(F32)
+
+    cell = depth_of(plane, gz)
+    for x in range(gx):
+        for n, step in enumerate(STEPS):
+            col_ref[pl.ds(x * plane, plane), pl.ds(n * 128, 128)] = shifted(
+                vol_ref, (x,), 16, plane, cell, gz, step
+            ).astype(BF)
+
+    p_ref[...] = jnp.dot(col_ref[...], wcat_ref[...], preferred_element_type=F32)
+
+    for lq in range(lx):
+        pair = None
+        for x in (2 * lq, 2 * lq + 1):
+            pre = p_ref[pl.ds(x * plane, plane), pl.ds(128, 128)]
+            if x > 0:
+                pre = pre + p_ref[pl.ds((x - 1) * plane, plane), pl.ds(0, 128)]
+            if x < gx - 1:
+                pre = pre + p_ref[pl.ds((x + 1) * plane, plane), pl.ds(256, 128)]
+            h, slope = gelu_and_slope(pre)
+            slope_ref[pl.ds(x * plane, plane), :] = slope
+            pair = h if pair is None else pair + h
+        wide = pair.reshape(ly, 2, gz, 128)
+        h_ref[...] = (wide[:, 0] + wide[:, 1]).reshape(ly * gz, 128)
+        pooled = (h_ref[pl.ds(0, lplane, stride=2), :] + h_ref[pl.ds(1, lplane, stride=2), :]) * 0.125
+        pooled = pooled.astype(BF)
+        pd_ref[pl.ds(lq * lplane, lplane), pl.ds(0, 128)] = pooled
+        pool_ref[lq, pl.ds(0, 8), :] = jnp.zeros((8, 128), F32)
+        pool_ref[lq, pl.ds(8 + lplane, 8), :] = jnp.zeros((8, 128), F32)
+        pool_ref[lq, pl.ds(8, lplane), :] = pooled.astype(F32)
+
+    lcell = depth_of(lplane, lz)
+    for x in range(lx):
+        for n, step in enumerate(STEPS):
+            lcol_ref[pl.ds(x * lplane, lplane), pl.ds(n * 128, 128)] = shifted(
+                pool_ref, (x,), 8, lplane, lcell, lz, step
+            ).astype(BF)
+    lcol = lcol_ref[...]
+    parts = [
+        jnp.dot(lcol, wl_ref[a].reshape(9 * 128, cl), preferred_element_type=F32) for a in range(3)
+    ]
+    for x in range(lx):
+        dl_ref[x, pl.ds(0, 8), :] = jnp.zeros((8, cl), F32)
+        dl_ref[x, pl.ds(8 + lplane, 8), :] = jnp.zeros((8, cl), F32)
+    zero = jnp.zeros((lplane, cl), F32)
+    pre = parts[1]
+    pre = pre + jnp.concatenate([zero, parts[0][:-lplane]], axis=0)
+    pre = pre + jnp.concatenate([parts[2][lplane:], zero], axis=0)
+    slope = gelu_and_slope(pre)[1]
+    for dk in range(nk):
+        src = blocks[dk]
+        kk = lax.rem(k + nk - dk, nk)
+        start = pl.multiple_of(kk * crow, 8)
+        for g in range(cl // 128):
+            h_ref2 = src[pl.ds(bx * brows + g * crow, crow), :].astype(F32)
+            p_ref[pl.ds(start, crow), pl.ds(g * 128, 128)] = h_ref2
+    cot = p_ref[pl.ds(0, lx * lplane), pl.ds(0, cl)]
+    delta = (cot * slope).astype(BF)
+    pd_ref[:, pl.ds(128, cl)] = delta
+    wide = delta.astype(F32)
+    for x in range(lx):
+        dl_ref[x, pl.ds(8, lplane), :] = wide[x * lplane : (x + 1) * lplane]
+    total = None
+    for n, (b, c) in enumerate(STEPS):
+        part = jnp.concatenate(
+            [shifted(dl_ref, (x,), 8, lplane, lcell, lz, (-b, -c)) for x in range(lx)], axis=0
+        ).astype(BF)
+        w = wl_ref[:, b + 1, c + 1].reshape(3 * 128, cl)
+        term = lax.dot_general(part, w, NT, preferred_element_type=F32)
+        total = term if total is None else total + term
+    zero = jnp.zeros((lplane, 128), F32)
+    back = total[:, 128:256]
+    back = back + jnp.concatenate([total[lplane:, 0:128], zero], axis=0)
+    back = back + jnp.concatenate([zero, total[:-lplane, 256:384]], axis=0)
+    back_ref[...] = back
+
+
+def late_grad_kernel(mine_ref, other_ref, out_ref, pool_ref, lcol_ref, *, dims, scale):
+    lx, ly, lz = dims
+    lplane = ly * lz
+    rows = lx * lplane
+    lcell = depth_of(lplane, lz)
+    pool_ref[...] = jnp.zeros(pool_ref.shape, F32)
+    for s, ref in enumerate((mine_ref, other_ref)):
+        for x in range(lx):
+            pool_ref[s, x + 1, pl.ds(8, lplane), :] = ref[pl.ds(x * lplane, lplane), pl.ds(0, 128)].astype(F32)
+        for x in range(lx + 2):
+            for n, step in enumerate(STEPS):
+                lcol_ref[s, pl.ds(x * lplane, lplane), pl.ds(n * 128, 128)] = shifted(
+                    pool_ref, (s, x), 8, lplane, lcell, lz, step
+                ).astype(BF)
+    cl = mine_ref.shape[1] - 128
+    delta = jnp.concatenate([mine_ref[:, pl.ds(128, cl)], other_ref[:, pl.ds(128, cl)]], axis=0)
+    for a in range(3):
+        left = jnp.concatenate([lcol_ref[s, pl.ds(a * lplane, rows), :] for s in (0, 1)], axis=0)
+        got = lax.dot_general(left, delta, (((0,), (0,)), ((), ())), preferred_element_type=F32)
+        out_ref[pl.ds(a * 9 * 128, 9 * 128), :] = (got * scale).astype(BF)
+
+
+def early_back_kernel(
+    pos_ref, mine_ref, other_ref, slope_ref, col_ref, wt_ref, grad_ref, gv_ref,
+    wide_ref, d_ref, dt_ref, win_ref, vcol_ref, *, dims
+):
+    gx, gy, gz, lx, ly, lz, bx, by = dims
+    plane, lplane = gy * gz, ly * lz
+    k, j = pos_ref[0], pos_ref[1]
+    brows = by * gz
+    for q in (0, gx + 1):
+        d_ref[q] = jnp.zeros(d_ref.shape[1:], F32)
+    d_ref[:, pl.ds(0, 16), :] = jnp.zeros((gx + 2, 16, 128), F32)
+    d_ref[:, pl.ds(16 + plane, 16), :] = jnp.zeros((gx + 2, 16, 128), F32)
+    dt_ref[:, pl.ds(0, plane)] = jnp.zeros((128, plane), BF)
+    dt_ref[:, pl.ds((gx + 1) * plane, plane)] = jnp.zeros((128, plane), BF)
+    back = (mine_ref[...] + other_ref[...].astype(F32)) * 0.125
+    wide_ref[pl.ds(0, lx * lplane, stride=2), :] = back
+    wide_ref[pl.ds(1, lx * lplane, stride=2), :] = back
+    for lq in range(lx):
+        rows = wide_ref[pl.ds(lq * ly * gz, ly * gz), :].reshape(ly, 1, gz, 128)
+        rows = jnp.broadcast_to(rows, (ly, 2, gz, 128)).reshape(plane, 128)
+        for x in (2 * lq, 2 * lq + 1):
+            delta = (rows * slope_ref[pl.ds(x * plane, plane), :]).astype(BF).astype(F32)
+            d_ref[x + 1, pl.ds(16, plane), :] = delta
+            dt_ref[:, pl.ds((x + 1) * plane, plane)] = delta.T.astype(BF)
+    left = jnp.concatenate([dt_ref[:, pl.ds((2 - a) * plane, gx * plane)] for a in range(3)], axis=0)
+    got = jnp.dot(left, col_ref[...], preferred_element_type=F32)
+    for a in range(3):
+        for n in range(9):
+            grad_ref[pl.ds((a * 9 + n) * 128, 128), :] = got[
+                a * 128 : (a + 1) * 128, n * 128 : (n + 1) * 128
+            ].T.astype(grad_ref.dtype)
+    cell = depth_of(brows, gz)
+    row = pl.multiple_of(j * brows, 8)
+    for q in range(bx + 2):
+        win_ref[q] = d_ref[k * bx + q, pl.ds(row, brows + 32), :]
+    for q in range(bx + 2):
+        for n, (b, c) in enumerate(STEPS):
+            vcol_ref[pl.ds(q * brows, brows), pl.ds(n * 128, 128)] = shifted(
+                win_ref, (q,), 16, brows, cell, gz, (-b, -c)
+            ).astype(BF)
+    total = None
+    for a in range(3):
+        term = jnp.dot(vcol_ref[pl.ds((2 - a) * brows, bx * brows), :], wt_ref[a], preferred_element_type=F32)
+        total = term if total is None else total + term
+    gv_ref[...] = total.astype(BF)
+
+
+def finish_kernel(mine_ref, other_ref, out_ref, *, scale):
+    out_ref[...] = ((mine_ref[...].astype(F32) + other_ref[...].astype(F32)) * scale).astype(BF)
+
+
+def turned(value, axis, by):
+    count = lax.axis_size(axis)
+    return lax.ppermute(value, axis, [(i, (i + by) % count) for i in range(count)])
+
+
+def call(kernel, outs, scratch, args, name, smem=0):
+    specs = [pl.BlockSpec(memory_space=pltpu.SMEM)] * smem
+    specs += [pl.BlockSpec(memory_space=pltpu.VMEM)] * (len(args) - smem)
+    return pl.pallas_call(
+        kernel,
+        out_shape=outs,
+        in_specs=specs,
+        out_specs=[pl.BlockSpec(memory_space=pltpu.VMEM)] * len(outs),
+        scratch_shapes=scratch,
+        compiler_params=pltpu.CompilerParams(vmem_limit_bytes=VMEM_BYTES),
+        name=name,
+    )(*args)
+
+
+def whole_sample(volume, early_weight, late_weight, cotangent):
+    nk, nj, nr = (lax.axis_size(axis) for axis in ("space", "chan", "rep"))
+    _, bx, by, gz, _ = volume.shape
+    _, cx, ly, lz, cl = cotangent.shape
+    gx, gy, lx = bx * nk, by * nj, cx * nk
+    plane, lplane, brows = gy * gz, ly * lz, by * gz
+    rows, lrows = gx * plane, lx * lplane
+    scale = 1.0 / math.sqrt(nr * lrows)
+    pos = jnp.stack([lax.axis_index("space"), lax.axis_index("chan")]).astype(jnp.int32)
+    sds = jax.ShapeDtypeStruct
+
+    cot = cotangent.reshape(cx * lplane, cl)
+    payload = jnp.concatenate(
+        [volume.reshape(bx * brows, 128)] + [cot[:, g : g + 128] for g in range(0, cl, 128)], axis=0
+    )
+    line = [payload] + [turned(payload, "space", dk) for dk in range(1, nk)]
+    blocks = list(line)
+    for dj in range(1, nj):
+        blocks += [turned(block, "chan", dj) for block in line]
+
+    wcat, wt = call(
+        prep_kernel, [sds((9 * 128, 3 * 128), BF), sds((3, 9 * 128, 128), BF)], [], [early_weight], "prep"
+    )
+    dims = (gx, gy, gz, lx, ly, lz, bx, by)
+    col, slope, pooled_delta, back = call(
+        functools.partial(forward_kernel, nk=nk, nj=nj, dims=dims),
+        [sds((rows, 9 * 128), BF), sds((rows, 128), F32), sds((lrows, 128 + cl), BF), sds((lrows, 128), F32)],
+        [
+            pltpu.VMEM((gx, plane + 32, 128), F32),
+            pltpu.VMEM((rows, 3 * 128), F32),
+            pltpu.VMEM((ly * gz, 128), F32),
+            pltpu.VMEM((lx, lplane + 16, 128), F32),
+            pltpu.VMEM((lrows, 9 * 128), BF),
+            pltpu.VMEM((lx, lplane + 16, cl), F32),
+        ],
+        [pos] + blocks + [wcat, late_weight],
+        "forward",
+        smem=1,
+    )
+    back_other = turned(back.astype(BF), "chan", 1)
+    pd_other = turned(pooled_delta, "rep", 1)
+    (late,) = call(
+        functools.partial(late_grad_kernel, dims=(lx, ly, lz), scale=scale),
+        [sds((27 * 128, cl), BF)],
+        [pltpu.VMEM((2, lx + 2, lplane + 16, 128), F32), pltpu.VMEM((2, (lx + 2) * lplane, 9 * 128), BF)],
+        [pooled_delta, pd_other],
+        "late_grad",
+    )
+    part, gv = call(
+        functools.partial(early_back_kernel, dims=dims),
+        [sds((27 * 128, 128), BF), sds((bx * brows, 128), BF)],
+        [
+            pltpu.VMEM((lx * ly * gz, 128), F32),
+            pltpu.VMEM((gx + 2, plane + 32, 128), F32),
+            pltpu.VMEM((128, (gx + 2) * plane), BF),
+            pltpu.VMEM((bx + 2, brows + 32, 128), F32),
+            pltpu.VMEM(((bx + 2) * brows, 9 * 128), BF),
+        ],
+        [pos, back, back_other, slope, col, wt],
+        "early_back",
+        smem=1,
+    )
+    part_other = turned(part, "rep", 1)
+    (early,) = call(
+        functools.partial(finish_kernel, scale=scale), [sds((27 * 128, 128), BF)], [], [part, part_other], "finish"
+    )
+    return (
+        early.reshape(3, 3, 3, 128, 128),
+        late.reshape(3, 3, 3, 128, cl),
+        gv.reshape(1, bx, by, gz, 128),
+    )
+
+
 def solution(mesh):
+    few = mesh.shape["space"] * mesh.shape["chan"] <= GATHER_BLOCKS
+    alone = mesh.shape["rep"] == 2 and mesh.shape["chan"] == 2
     return jax.shard_map(
-        per_device,
+        whole_sample if few and alone else per_device,
         mesh=mesh,
         in_specs=(
             P(("groups", "rep"), "space", "chan", None, None),

time: 281 us -> 55.1 us (0.20)
  waiting for transfers between devices: 180 us -> 11.8 us
  matrix products: 31.2 us -> 0 us
  Pallas kernels: 0 us -> 24.2 us
  starting transfers between devices: 30 us -> 12 us
  between operations: 14.4 us -> 0.71 us
  local copies, waits for them, and re-layouts: 12.3 us -> 3.62 us
  other arithmetic: 7.75 us -> 2.38 us
  blocking collectives: 4.48 us -> 0 us
    psum x2 -> x0, waiting for transfers between devices: 157 us -> none  [the longest x1 83 us: per_device(): late_total = lax.psum(late_part, ('space', 'rep'))]
    dot_general x162 -> x0, matrix products: 31.2 us -> none  [the longest x108 17.4 us: conv_padded(): jnp.einsum('sxyzc,co->sxyzo', window, weight[first, second, third], prefe...]
    pallas_call x0 -> x5, Pallas kernels: none -> 24.2 us  [call(): pl.pallas_call(kernel, out_shape=outs, in_specs=specs, out_specs=[pl.Bloc...]
    ppermute x12 -> x10, starting transfers between devices: 29.9 us -> 12 us  [turned(): lax.ppermute(value, axis, [(i, (i + by) % count) for i in range(count)])]
    reduce_scatter x1 -> x0, waiting for transfers between devices: 10.6 us -> none  [per_device(): lax.psum_scatter(back_partial, 'chan', scatter_dimension=2, tiled=True)]
    unnamed x36 -> x24, local copies, waits for them, and re-layouts: 8.58 us -> 2.84 us
    convert_element_type x5 -> x1, other arithmetic: 6.51 us -> 0.91 us  [whole_sample(): back_other = turned(back.astype(BF), 'chan', 1)]
    all_gather x1 -> x0, blocking collectives: 4.48 us -> none  [per_device(): joined = lax.all_gather(pooled, 'chan', axis=2, tiled=True)]
  transfers between devices with their start and end apart: 15 -> 10, of which waited for: 8 -> 5; matrix products, arithmetic and copies ran while one was open for 8% -> 1% of each run, Pallas kernels for 0% -> 11%
where the time goes in v1:
time: 55.1 us; the launch traced here: 54.7 us
  Pallas kernels  24.2 us (44%)
  starting transfers between devices  12 us (22%)
  waiting for transfers between devices  11.8 us (21%)
  local copies, waits for them, and re-layouts  3.62 us (7%)
  other arithmetic  2.38 us (4%)
  between operations  0.71 us (1%)
    pallas_call x5, Pallas kernels, call(): pl.pallas_call(kernel, out_shape=outs, in_specs=specs, out_specs=[pl.Bloc...  24.2 us
    ppermute x10, starting transfers between devices, turned(): lax.ppermute(value, axis, [(i, (i + by) % count) for i in range(count)])  12 us
    ppermute x10, waiting for transfers between devices, turned(): lax.ppermute(value, axis, [(i, (i + by) % count) for i in range(count)])  11.8 us
    unnamed x24, local copies, waits for them, and re-layouts  2.84 us
  transfers between devices with their start and end apart: 10, of which 5 were waited for; matrix products, arithmetic and copies ran while one was open for 1% of the time, Pallas kernels for 11%

profile of v1, /device:TPU:0, one launch (start us, length us, event | category | flops | bytes accessed | tf_op | source)
XLA Modules:
  0.0 54.7 jit_solution(9539742421532303888)
XLA Ops:
  0.6 0.8 %reshape.22 = bf16[64,256]{1,0:T(8,128)(2,1)S(1)} reshape(bf16[1,1,16,4,256]{4,3,2,1,0:T(4,128)(2,1)} %param.7) | data formatting | bytes 65536 | tf_op jit(solution)/shard_map/reshape | solution.py:377
  1.4 0.8 %pad_maximum_fusion.refs_0_ = bf16[384,128]{1,0:T(8,128)(2,1)S(1)} fusion(bf16[64,128]{1,0:T(8,128)(2,1)S(1)} %get-tuple-element.20, bf16[64,128]{1,0:T(8,128)(2,1)S(1)} %get-tuple-element.19, bf16[256,128]{1,0:T(8,128)(2,1)} %bitcast.8), kind=kLoop, calls=%fused_computation | loop fusion | flops 294912 | bytes 196608 | tf_op jit(solution)/shard_map/concatenate | solution.py:378
  2.3 0.0 copy-start.1
  2.3 5.1 %collective-permute-start.2 = (bf16[384,128]{1,0:T(8,128)(2,1)S(1)}, bf16[384,128]{1,0:T(8,128)(2,1)S(1)}, u32[]{:S(2)}, u32[]{:S(2)}) collective-permute-start(bf16[384,128]{1,0:T(8,128)(2,1)S(1)} %pad_maximum_fusion.refs_0_), channel_id=1, source_target_pairs={{0,12},{4,0},{8,4},{12,8},{1,13},{5,1},{9,5},{13,9},{2,14},{6,2},{... | collective-permute-start | bytes 294920 | tf_op jit(solution)/shard_map/ppermute | solution.py:349
  7.4 0.0 collective-permute-start.1
  7.4 1.0 %collective-permute-start = (bf16[384,128]{1,0:T(8,128)(2,1)S(1)}, bf16[384,128]{1,0:T(8,128)(2,1)S(1)}, u32[]{:S(2)}, u32[]{:S(2)}) collective-permute-start(bf16[384,128]{1,0:T(8,128)(2,1)S(1)} %pad_maximum_fusion.refs_0_), channel_id=1, source_target_pairs={{0,4},{4,8},{8,12},{12,0},{1,5},{5,9},{9,13},{13,1},{2,6},{6,10},{... | collective-permute-start | bytes 294920 | tf_op jit(solution)/shard_map/ppermute | solution.py:349
  8.4 1.5 %collective-permute-start.3 = (bf16[384,128]{1,0:T(8,128)(2,1)S(1)}, bf16[384,128]{1,0:T(8,128)(2,1)S(1)}, u32[]{:S(2)}, u32[]{:S(2)}) collective-permute-start(bf16[384,128]{1,0:T(8,128)(2,1)S(1)} %pad_maximum_fusion.refs_0_), channel_id=1, source_target_pairs={{0,2},{2,0},{1,3},{3,1},{4,6},{6,4},{5,7},{7,5},{8,10},{10,8},{9,1... | collective-permute-start | bytes 294920 | tf_op jit(solution)/shard_map/ppermute | solution.py:349
  9.9 2.6 %prep.1 = (bf16[1152,384]{1,0:T(8,128)(2,1)}, bf16[3,1152,128]{2,1,0:T(8,128)(2,1)}) custom-call(bf16[3,3,3,128,128]{4,3,2,1,0:T(8,128)(2,1)} %we_ref.1), custom_call_target="tpu_custom_call" | custom-call | tf_op jit(solution)/shard_map/prep/pallas_call | solution.py:355
  12.5 0.0 collective-permute-done.2.refs_3_
  12.5 0.5 collective-permute-start.6
  13.0 3.1 %collective-permute-done.1.refs_2_ = bf16[384,128]{1,0:T(8,128)(2,1)S(1)} collective-permute-done((bf16[384,128]{1,0:T(8,128)(2,1)S(1)}, bf16[384,128]{1,0:T(8,128)(2,1)S(1)}, u32[]{:S(2)}, u32[]{:S(2)}) %collective-permute-start.1) | collective-permute-done | bytes 98336 | tf_op jit(solution)/shard_map/ppermute | solution.py:349
  16.1 1.5 %collective-permute-start.5 = (bf16[384,128]{1,0:T(8,128)(2,1)S(1)}, bf16[384,128]{1,0:T(8,128)(2,1)S(1)}, u32[]{:S(2)}, u32[]{:S(2)}) collective-permute-start(bf16[384,128]{1,0:T(8,128)(2,1)S(1)} %collective-permute-done.1.refs_2_), channel_id=1, source_target_pairs={{0,2},{2,0},{1,3},{3,1},{4,6},{6,4},{5,7},{7,5},{8,10},{10,8},{9,1... | collective-permute-start | bytes 294920 | tf_op jit(solution)/shard_map/ppermute | solution.py:349
  17.6 0.0 collective-permute-done.refs_1_
  17.6 0.0 copy-start.6
  17.6 0.5 collective-permute-start.4
  18.2 0.6 %pad_add_fusion.pos_ref = s32[2]{0:T(128)} fusion(s32[1]{0:T(128)} %bitcast.1, s32[1]{0:T(128)} %bitcast), kind=kLoop, calls=%fused_computation.1 | loop fusion | flops 2 | bytes 16 | tf_op jit(solution)/shard_map/stack | solution.py:374
  18.8 0.0 collective-permute-done.3.refs_4_
  18.8 0.0 copy-start.7
  18.8 0.0 collective-permute-done.6.refs_7_
  18.8 0.0 copy-start.8
  18.8 2.8 %collective-permute-done.5.refs_6_ = bf16[384,128]{1,0:T(8,128)(2,1)S(1)} collective-permute-done((bf16[384,128]{1,0:T(8,128)(2,1)S(1)}, bf16[384,128]{1,0:T(8,128)(2,1)S(1)}, u32[]{:S(2)}, u32[]{:S(2)}) %collective-permute-start.5) | collective-permute-done | bytes 98336 | tf_op jit(solution)/shard_map/ppermute | solution.py:349
  21.6 0.0 copy-start.9
  21.6 1.1 %collective-permute-done.4.refs_5_ = bf16[384,128]{1,0:T(8,128)(2,1)S(1)} collective-permute-done((bf16[384,128]{1,0:T(8,128)(2,1)S(1)}, bf16[384,128]{1,0:T(8,128)(2,1)S(1)}, u32[]{:S(2)}, u32[]{:S(2)}) %collective-permute-start.4) | collective-permute-done | bytes 98336 | tf_op jit(solution)/shard_map/ppermute | solution.py:349
  22.6 0.0 copy-start.10
  22.6 0.0 copy-done.1
  22.6 0.0 copy-done.4
  22.6 0.0 copy-done.5
  22.6 0.0 copy-done.6
  22.6 0.0 copy-done.7
  22.7 0.0 copy-done.8
  22.7 0.0 copy-done.9
  22.7 0.6 %copy-done.10 = bf16[384,128]{1,0:T(8,128)(2,1)} copy-done((bf16[384,128]{1,0:T(8,128)(2,1)}, bf16[384,128]{1,0:T(8,128)(2,1)S(1)}, u32[]{:S(2)}) %copy-start.10) | copy-done | bytes 98328
  23.2 8.8 %forward.1 = (bf16[2048,1152]{1,0:T(8,128)(2,1)}, f32[2048,128]{1,0:T(8,128)}, bf16[256,384]{1,0:T(8,128)(2,1)}, f32[256,128]{1,0:T(8,128)}) custom-call(s32[2]{0:T(128)} %pad_add_fusion.pos_ref, bf16[384,128]{1,0:T(8,128)(2,1)} %copy-done.1, bf16[384,128]{1,0:T(8,128)(2,1)} %copy-done.6, bf16[384,128]{1,0:T(8,128)(2,1)} %copy-done.5, ...), custom_call_target="tpu_custom_call" | custom-call | tf_op jit(solution)/shard_map/forward/pallas_call | solution.py:355
  32.0 0.9 %convert_element_type.3 = bf16[256,128]{1,0:T(8,128)(2,1)S(1)} convert(f32[256,128]{1,0:T(8,128)} %get-tuple-element.12.mine_ref) | non-fusion elementwise | flops 32768 | bytes 196608 | tf_op jit(solution)/shard_map/convert_element_type | solution.py:405
  32.9 1.3 %collective-permute-start.7 = (bf16[256,128]{1,0:T(8,128)(2,1)S(1)}, bf16[256,128]{1,0:T(8,128)(2,1)S(1)}, u32[]{:S(2)}, u32[]{:S(2)}) collective-permute-start(bf16[256,128]{1,0:T(8,128)(2,1)S(1)} %convert_element_type.3), channel_id=1, source_target_pairs={{0,2},{2,0},{1,3},{3,1},{4,6},{6,4},{5,7},{7,5},{8,10},{10,8},{9,1... | collective-permute-start | bytes 196616 | tf_op jit(solution)/shard_map/ppermute | solution.py:349
  34.3 2.9 %collective-permute-done.7.other_ref = bf16[256,128]{1,0:T(8,128)(2,1)S(1)} collective-permute-done((bf16[256,128]{1,0:T(8,128)(2,1)S(1)}, bf16[256,128]{1,0:T(8,128)(2,1)S(1)}, u32[]{:S(2)}, u32[]{:S(2)}) %collective-permute-start.7) | collective-permute-done | bytes 65568 | tf_op jit(solution)/shard_map/ppermute | solution.py:349
  37.2 0.0 copy-start.11
  37.2 0.6 %copy-done.11 = bf16[256,128]{1,0:T(8,128)(2,1)} copy-done((bf16[256,128]{1,0:T(8,128)(2,1)}, bf16[256,128]{1,0:T(8,128)(2,1)S(1)}, u32[]{:S(2)}) %copy-start.11) | copy-done | bytes 65560
  37.8 6.8 %early_back.1 = (bf16[3456,128]{1,0:T(8,128)(2,1)}, bf16[256,128]{1,0:T(8,128)(2,1)}) custom-call(s32[2]{0:T(128)} %pad_add_fusion.pos_ref, f32[256,128]{1,0:T(8,128)} %get-tuple-element.12.mine_ref, bf16[256,128]{1,0:T(8,128)(2,1)} %copy-done.11, f32[2048,128]{1,0:T(8,128)} %get-tuple-element.13.slope_ref, bf16[2048,1152]{1,0:T(8,128)(2,1)} %get-tuple-element.14.col_ref, ...), custom_call_target="tpu_custom_call" | custom-call | tf_op jit(solution)/shard_map/early_back/pallas_call | solution.py:355
  44.6 0.0 collective-permute-start.8
  44.6 0.0 copy-done.2
  44.6 0.5 collective-permute-start.9
  45.1 2.0 %collective-permute-done.9.other_ref = bf16[256,384]{1,0:T(8,128)(2,1)S(1)} collective-permute-done((bf16[256,384]{1,0:T(8,128)(2,1)S(1)}, bf16[256,384]{1,0:T(8,128)(2,1)S(1)}, u32[]{:S(2)}, u32[]{:S(2)}) %collective-permute-start.9) | collective-permute-done | bytes 196640 | tf_op jit(solution)/shard_map/ppermute | solution.py:349
  47.0 0.7 %copy-done.3 = bf16[256,384]{1,0:T(8,128)(2,1)} copy-done((bf16[256,384]{1,0:T(8,128)(2,1)}, bf16[256,384]{1,0:T(8,128)(2,1)S(1)}, u32[]{:S(2)}) %copy-start.3) | copy-done | bytes 196632
  47.7 3.4 %late_grad.1 = bf16[3456,256]{1,0:T(8,128)(2,1)} custom-call(bf16[256,384]{1,0:T(8,128)(2,1)} %get-tuple-element.17.mine_ref, bf16[256,384]{1,0:T(8,128)(2,1)} %copy-done.3), custom_call_target="tpu_custom_call" | custom-call | tf_op jit(solution)/shard_map/late_grad/pallas_call | solution.py:355
  51.2 0.0 collective-permute-done.8.other_ref
  51.2 0.9 %copy-done = bf16[3456,128]{1,0:T(8,128)(2,1)} copy-done((bf16[3456,128]{1,0:T(8,128)(2,1)}, bf16[3456,128]{1,0:T(8,128)(2,1)S(1)}, u32[]{:S(2)}) %copy-start) | copy-done | bytes 884760
  52.1 2.6 %finish.1 = bf16[3456,128]{1,0:T(8,128)(2,1)} custom-call(bf16[3456,128]{1,0:T(8,128)(2,1)} %get-tuple-element.16.mine_ref, bf16[3456,128]{1,0:T(8,128)(2,1)} %copy-done), custom_call_target="tpu_custom_call" | custom-call | tf_op jit(solution)/shard_map/finish/pallas_call | solution.py:355
  (6 shorter events, 0.0 us)
Async XLA Ops:
  2.3 20.4 %copy-start.1 = (bf16[384,128]{1,0:T(8,128)(2,1)}, bf16[384,128]{1,0:T(8,128)(2,1)S(1)}, u32[]{:S(2)}) copy-start(bf16[384,128]{1,0:T(8,128)(2,1)S(1)} %pad_maximum_fusion.refs_0_) | copy-start | bytes 294916
  2.3 10.2 %collective-permute-start.2 = (bf16[384,128]{1,0:T(8,128)(2,1)S(1)}, bf16[384,128]{1,0:T(8,128)(2,1)S(1)}, u32[]{:S(2)}, u32[]{:S(2)}) collective-permute-start(bf16[384,128]{1,0:T(8,128)(2,1)S(1)} %pad_maximum_fusion.refs_0_), channel_id=1, source_target_pairs={{0,12},{4,0},{8,4},{12,8},{1,13},{5,1},{9,5},{13,9},{2,14},{6,2},{... | collective-permute-start | bytes 294920 | tf_op jit(solution)/shard_map/ppermute | solution.py:349
  7.4 8.7 %collective-permute-start.1 = (bf16[384,128]{1,0:T(8,128)(2,1)S(1)}, bf16[384,128]{1,0:T(8,128)(2,1)S(1)}, u32[]{:S(2)}, u32[]{:S(2)}) collective-permute-start(bf16[384,128]{1,0:T(8,128)(2,1)S(1)} %pad_maximum_fusion.refs_0_), channel_id=1, source_target_pairs={{0,8},{4,12},{8,0},{12,4},{1,9},{5,13},{9,1},{13,5},{2,10},{6,14},... | collective-permute-start | bytes 294920 | tf_op jit(solution)/shard_map/ppermute | solution.py:349
  7.4 10.2 %collective-permute-start = (bf16[384,128]{1,0:T(8,128)(2,1)S(1)}, bf16[384,128]{1,0:T(8,128)(2,1)S(1)}, u32[]{:S(2)}, u32[]{:S(2)}) collective-permute-start(bf16[384,128]{1,0:T(8,128)(2,1)S(1)} %pad_maximum_fusion.refs_0_), channel_id=1, source_target_pairs={{0,4},{4,8},{8,12},{12,0},{1,5},{5,9},{9,13},{13,1},{2,6},{6,10},{... | collective-permute-start | bytes 294920 | tf_op jit(solution)/shard_map/ppermute | solution.py:349
  8.4 10.4 %collective-permute-start.3 = (bf16[384,128]{1,0:T(8,128)(2,1)S(1)}, bf16[384,128]{1,0:T(8,128)(2,1)S(1)}, u32[]{:S(2)}, u32[]{:S(2)}) collective-permute-start(bf16[384,128]{1,0:T(8,128)(2,1)S(1)} %pad_maximum_fusion.refs_0_), channel_id=1, source_target_pairs={{0,2},{2,0},{1,3},{3,1},{4,6},{6,4},{5,7},{7,5},{8,10},{10,8},{9,1... | collective-permute-start | bytes 294920 | tf_op jit(solution)/shard_map/ppermute | solution.py:349
  12.5 10.1 %copy-start.4 = (bf16[384,128]{1,0:T(8,128)(2,1)}, bf16[384,128]{1,0:T(8,128)(2,1)S(1)}, u32[]{:S(2)}) copy-start(bf16[384,128]{1,0:T(8,128)(2,1)S(1)} %collective-permute-done.2.refs_3_) | copy-start | bytes 294916
  12.5 6.3 %collective-permute-start.6 = (bf16[384,128]{1,0:T(8,128)(2,1)S(1)}, bf16[384,128]{1,0:T(8,128)(2,1)S(1)}, u32[]{:S(2)}, u32[]{:S(2)}) collective-permute-start(bf16[384,128]{1,0:T(8,128)(2,1)S(1)} %collective-permute-done.2.refs_3_), channel_id=1, source_target_pairs={{0,2},{2,0},{1,3},{3,1},{4,6},{6,4},{5,7},{7,5},{8,10},{10,8},{9,1... | collective-permute-start | bytes 294920 | tf_op jit(solution)/shard_map/ppermute | solution.py:349
  16.1 6.5 %copy-start.5 = (bf16[384,128]{1,0:T(8,128)(2,1)}, bf16[384,128]{1,0:T(8,128)(2,1)S(1)}, u32[]{:S(2)}) copy-start(bf16[384,128]{1,0:T(8,128)(2,1)S(1)} %collective-permute-done.1.refs_2_) | copy-start | bytes 294916
  16.1 5.4 %collective-permute-start.5 = (bf16[384,128]{1,0:T(8,128)(2,1)S(1)}, bf16[384,128]{1,0:T(8,128)(2,1)S(1)}, u32[]{:S(2)}, u32[]{:S(2)}) collective-permute-start(bf16[384,128]{1,0:T(8,128)(2,1)S(1)} %collective-permute-done.1.refs_2_), channel_id=1, source_target_pairs={{0,2},{2,0},{1,3},{3,1},{4,6},{6,4},{5,7},{7,5},{8,10},{10,8},{9,1... | collective-permute-start | bytes 294920 | tf_op jit(solution)/shard_map/ppermute | solution.py:349
  17.6 5.0 %copy-start.6 = (bf16[384,128]{1,0:T(8,128)(2,1)}, bf16[384,128]{1,0:T(8,128)(2,1)S(1)}, u32[]{:S(2)}) copy-start(bf16[384,128]{1,0:T(8,128)(2,1)S(1)} %collective-permute-done.refs_1_) | copy-start | bytes 294916
  17.6 5.0 %collective-permute-start.4 = (bf16[384,128]{1,0:T(8,128)(2,1)S(1)}, bf16[384,128]{1,0:T(8,128)(2,1)S(1)}, u32[]{:S(2)}, u32[]{:S(2)}) collective-permute-start(bf16[384,128]{1,0:T(8,128)(2,1)S(1)} %collective-permute-done.refs_1_), channel_id=1, source_target_pairs={{0,2},{2,0},{1,3},{3,1},{4,6},{6,4},{5,7},{7,5},{8,10},{10,8},{9,1... | collective-permute-start | bytes 294920 | tf_op jit(solution)/shard_map/ppermute | solution.py:349
  18.8 3.9 %copy-start.7 = (bf16[384,128]{1,0:T(8,128)(2,1)}, bf16[384,128]{1,0:T(8,128)(2,1)S(1)}, u32[]{:S(2)}) copy-start(bf16[384,128]{1,0:T(8,128)(2,1)S(1)} %collective-permute-done.3.refs_4_) | copy-start | bytes 294916
  18.8 3.9 %copy-start.8 = (bf16[384,128]{1,0:T(8,128)(2,1)}, bf16[384,128]{1,0:T(8,128)(2,1)S(1)}, u32[]{:S(2)}) copy-start(bf16[384,128]{1,0:T(8,128)(2,1)S(1)} %collective-permute-done.6.refs_7_) | copy-start | bytes 294916
  21.6 1.1 %copy-start.9 = (bf16[384,128]{1,0:T(8,128)(2,1)}, bf16[384,128]{1,0:T(8,128)(2,1)S(1)}, u32[]{:S(2)}) copy-start(bf16[384,128]{1,0:T(8,128)(2,1)S(1)} %collective-permute-done.5.refs_6_) | copy-start | bytes 294916
  22.6 0.6 %copy-start.10 = (bf16[384,128]{1,0:T(8,128)(2,1)}, bf16[384,128]{1,0:T(8,128)(2,1)S(1)}, u32[]{:S(2)}) copy-start(bf16[384,128]{1,0:T(8,128)(2,1)S(1)} %collective-permute-done.4.refs_5_) | copy-start | bytes 294916
  32.9 4.3 %collective-permute-start.7 = (bf16[256,128]{1,0:T(8,128)(2,1)S(1)}, bf16[256,128]{1,0:T(8,128)(2,1)S(1)}, u32[]{:S(2)}, u32[]{:S(2)}) collective-permute-start(bf16[256,128]{1,0:T(8,128)(2,1)S(1)} %convert_element_type.3), channel_id=1, source_target_pairs={{0,2},{2,0},{1,3},{3,1},{4,6},{6,4},{5,7},{7,5},{8,10},{10,8},{9,1... | collective-permute-start | bytes 196616 | tf_op jit(solution)/shard_map/ppermute | solution.py:349
  37.2 0.6 %copy-start.11 = (bf16[256,128]{1,0:T(8,128)(2,1)}, bf16[256,128]{1,0:T(8,128)(2,1)S(1)}, u32[]{:S(2)}) copy-start(bf16[256,128]{1,0:T(8,128)(2,1)S(1)} %collective-permute-done.7.other_ref) | copy-start | bytes 196612
  37.8 6.8 %copy-start.2 = (bf16[256,384]{1,0:T(8,128)(2,1)S(1)}, bf16[256,384]{1,0:T(8,128)(2,1)}, u32[]{:S(2)}) copy-start(bf16[256,384]{1,0:T(8,128)(2,1)} %get-tuple-element.17.mine_ref) | copy-start | bytes 589828
  44.6 6.6 %collective-permute-start.8 = (bf16[3456,128]{1,0:T(8,128)(2,1)}, bf16[3456,128]{1,0:T(8,128)(2,1)S(1)}, u32[]{:S(2)}, u32[]{:S(2)}) collective-permute-start(bf16[3456,128]{1,0:T(8,128)(2,1)} %get-tuple-element.16.mine_ref), channel_id=1, source_target_pairs={{0,1},{1,0},{2,3},{3,2},{4,5},{5,4},{6,7},{7,6},{8,9},{9,8},{10,11... | collective-permute-start | bytes 2654216 | tf_op jit(solution)/shard_map/ppermute | solution.py:349
  44.6 2.5 %collective-permute-start.9 = (bf16[256,384]{1,0:T(8,128)(2,1)S(1)}, bf16[256,384]{1,0:T(8,128)(2,1)S(1)}, u32[]{:S(2)}, u32[]{:S(2)}) collective-permute-start(bf16[256,384]{1,0:T(8,128)(2,1)S(1)} %copy-done.2), channel_id=1, source_target_pairs={{0,1},{1,0},{2,3},{3,2},{4,5},{5,4},{6,7},{7,6},{8,9},{9,8},{10,11... | collective-permute-start | bytes 589832 | tf_op jit(solution)/shard_map/ppermute | solution.py:349
  47.0 0.7 %copy-start.3 = (bf16[256,384]{1,0:T(8,128)(2,1)}, bf16[256,384]{1,0:T(8,128)(2,1)S(1)}, u32[]{:S(2)}) copy-start(bf16[256,384]{1,0:T(8,128)(2,1)S(1)} %collective-permute-done.9.other_ref) | copy-start | bytes 589828
  51.2 0.9 %copy-start = (bf16[3456,128]{1,0:T(8,128)(2,1)}, bf16[3456,128]{1,0:T(8,128)(2,1)S(1)}, u32[]{:S(2)}) copy-start(bf16[3456,128]{1,0:T(8,128)(2,1)S(1)} %collective-permute-done.8.other_ref) | copy-start | bytes 2654212

commit v2 on v1

--- a/solution.py
+++ b/solution.py
@@ -10,7 +10,7 @@
 
 BF = jnp.bfloat16
 F32 = jnp.float32
-VMEM_BYTES = 56 * 2**20
+VMEM_BYTES = 24 * 2**20
 GATHER_BLOCKS = 8
 
 
@@ -171,15 +171,13 @@
             wt_ref[a, pl.ds(n * 128, 128), :] = w.astype(F32).T.astype(BF)
 
 
-def forward_kernel(
-    pos_ref, *refs, nk, nj, dims
-):
+def forward_kernel(*refs, nk, nj, dims):
     gx, gy, gz, lx, ly, lz, bx, by = dims
-    blocks = refs[: nk * nj]
-    wcat_ref, wl_ref = refs[nk * nj : nk * nj + 2]
-    col_ref, slope_ref, pd_ref, back_ref = refs[nk * nj + 2 : nk * nj + 6]
-    vol_ref, p_ref, h_ref, pool_ref, lcol_ref, dl_ref = refs[nk * nj + 6 :]
-    k, j = pos_ref[0], pos_ref[1]
+    blocks, refs = refs[: nk * nj], refs[nk * nj :]
+    cots, refs = refs[:nk], refs[nk:]
+    wcat_ref, wl_ref, col_ref, slope_ref, pd_ref, back_ref, mine_ref = refs[:7]
+    vol_ref, p_ref, h_ref, pool_ref, lcol_ref, dl_ref = refs[7:]
+    k, j = lax.axis_index("space"), lax.axis_index("chan")
     plane, lplane = gy * gz, ly * lz
     brows = by * gz
     cl = wl_ref.shape[-1]
@@ -244,12 +242,9 @@
     pre = pre + jnp.concatenate([parts[2][lplane:], zero], axis=0)
     slope = gelu_and_slope(pre)[1]
     for dk in range(nk):
-        src = blocks[dk]
         kk = lax.rem(k + nk - dk, nk)
         start = pl.multiple_of(kk * crow, 8)
-        for g in range(cl // 128):
-            h_ref2 = src[pl.ds(bx * brows + g * crow, crow), :].astype(F32)
-            p_ref[pl.ds(start, crow), pl.ds(g * 128, 128)] = h_ref2
+        p_ref[pl.ds(start, crow), pl.ds(0, cl)] = cots[dk][...].astype(F32)
     cot = p_ref[pl.ds(0, lx * lplane), pl.ds(0, cl)]
     delta = (cot * slope).astype(BF)
     pd_ref[:, pl.ds(128, cl)] = delta
@@ -268,7 +263,8 @@
     back = total[:, 128:256]
     back = back + jnp.concatenate([total[lplane:, 0:128], zero], axis=0)
     back = back + jnp.concatenate([zero, total[:-lplane, 256:384]], axis=0)
-    back_ref[...] = back
+    back_ref[...] = back.astype(BF)
+    mine_ref[...] = back
 
 
 def late_grad_kernel(mine_ref, other_ref, out_ref, pool_ref, lcol_ref, *, dims, scale):
@@ -293,13 +289,12 @@
         out_ref[pl.ds(a * 9 * 128, 9 * 128), :] = (got * scale).astype(BF)
 
 
-def early_back_kernel(
-    pos_ref, mine_ref, other_ref, slope_ref, col_ref, wt_ref, grad_ref, gv_ref,
-    wide_ref, d_ref, dt_ref, win_ref, vcol_ref, *, dims
+def early_grad_kernel(
+    mine_ref, other_ref, slope_ref, col_ref, part_ref, win_ref, wide_ref, d_ref, dt_ref, *, dims
 ):
     gx, gy, gz, lx, ly, lz, bx, by = dims
     plane, lplane = gy * gz, ly * lz
-    k, j = pos_ref[0], pos_ref[1]
+    k, j = lax.axis_index("space"), lax.axis_index("chan")
     brows = by * gz
     for q in (0, gx + 1):
         d_ref[q] = jnp.zeros(d_ref.shape[1:], F32)
@@ -321,13 +316,16 @@
     got = jnp.dot(left, col_ref[...], preferred_element_type=F32)
     for a in range(3):
         for n in range(9):
-            grad_ref[pl.ds((a * 9 + n) * 128, 128), :] = got[
+            part_ref[pl.ds((a * 9 + n) * 128, 128), :] = got[
                 a * 128 : (a + 1) * 128, n * 128 : (n + 1) * 128
-            ].T.astype(grad_ref.dtype)
-    cell = depth_of(brows, gz)
+            ].T.astype(part_ref.dtype)
     row = pl.multiple_of(j * brows, 8)
     for q in range(bx + 2):
         win_ref[q] = d_ref[k * bx + q, pl.ds(row, brows + 32), :]
+
+
+def grad_volume_kernel(win_ref, wt_ref, gv_ref, vcol_ref, *, bx, brows, gz):
+    cell = depth_of(brows, gz)
     for q in range(bx + 2):
         for n, (b, c) in enumerate(STEPS):
             vcol_ref[pl.ds(q * brows, brows), pl.ds(n * 128, 128)] = shifted(
@@ -340,22 +338,18 @@
     gv_ref[...] = total.astype(BF)
 
 
-def finish_kernel(mine_ref, other_ref, out_ref, *, scale):
-    out_ref[...] = ((mine_ref[...].astype(F32) + other_ref[...].astype(F32)) * scale).astype(BF)
-
-
 def turned(value, axis, by):
     count = lax.axis_size(axis)
     return lax.ppermute(value, axis, [(i, (i + by) % count) for i in range(count)])
 
 
-def call(kernel, outs, scratch, args, name, smem=0):
-    specs = [pl.BlockSpec(memory_space=pltpu.SMEM)] * smem
-    specs += [pl.BlockSpec(memory_space=pltpu.VMEM)] * (len(args) - smem)
+def call(kernel, outs, scratch, args, name, far=()):
+    args = [pltpu.with_memory_space_constraint(arg, pltpu.VMEM) for arg in args]
+    outs = [out if n in far else pltpu.VMEM(out.shape, out.dtype) for n, out in enumerate(outs)]
     return pl.pallas_call(
         kernel,
         out_shape=outs,
-        in_specs=specs,
+        in_specs=[pl.BlockSpec(memory_space=pltpu.VMEM)] * len(args),
         out_specs=[pl.BlockSpec(memory_space=pltpu.VMEM)] * len(outs),
         scratch_shapes=scratch,
         compiler_params=pltpu.CompilerParams(vmem_limit_bytes=VMEM_BYTES),
@@ -371,25 +365,29 @@
     plane, lplane, brows = gy * gz, ly * lz, by * gz
     rows, lrows = gx * plane, lx * lplane
     scale = 1.0 / math.sqrt(nr * lrows)
-    pos = jnp.stack([lax.axis_index("space"), lax.axis_index("chan")]).astype(jnp.int32)
     sds = jax.ShapeDtypeStruct
 
-    cot = cotangent.reshape(cx * lplane, cl)
-    payload = jnp.concatenate(
-        [volume.reshape(bx * brows, 128)] + [cot[:, g : g + 128] for g in range(0, cl, 128)], axis=0
-    )
-    line = [payload] + [turned(payload, "space", dk) for dk in range(1, nk)]
+    mine = volume.reshape(bx * brows, 128)
+    line = [mine] + [turned(mine, "space", dk) for dk in range(1, nk)]
     blocks = list(line)
     for dj in range(1, nj):
         blocks += [turned(block, "chan", dj) for block in line]
+    cot = cotangent.reshape(cx * lplane, cl)
+    cots = [cot] + [turned(cot, "space", dk) for dk in range(1, nk)]
 
     wcat, wt = call(
         prep_kernel, [sds((9 * 128, 3 * 128), BF), sds((3, 9 * 128, 128), BF)], [], [early_weight], "prep"
     )
     dims = (gx, gy, gz, lx, ly, lz, bx, by)
-    col, slope, pooled_delta, back = call(
+    col, slope, pooled_delta, back, back_mine = call(
         functools.partial(forward_kernel, nk=nk, nj=nj, dims=dims),
-        [sds((rows, 9 * 128), BF), sds((rows, 128), F32), sds((lrows, 128 + cl), BF), sds((lrows, 128), F32)],
+        [
+            sds((rows, 9 * 128), BF),
+            sds((rows, 128), F32),
+            sds((lrows, 128 + cl), BF),
+            sds((lrows, 128), BF),
+            sds((lrows, 128), F32),
+        ],
         [
             pltpu.VMEM((gx, plane + 32, 128), F32),
             pltpu.VMEM((rows, 3 * 128), F32),
@@ -398,37 +396,41 @@
             pltpu.VMEM((lrows, 9 * 128), BF),
             pltpu.VMEM((lx, lplane + 16, cl), F32),
         ],
-        [pos] + blocks + [wcat, late_weight],
+        blocks + cots + [wcat, late_weight],
         "forward",
-        smem=1,
-    )
-    back_other = turned(back.astype(BF), "chan", 1)
+    )
     pd_other = turned(pooled_delta, "rep", 1)
+    back_other = turned(back, "chan", 1)
     (late,) = call(
         functools.partial(late_grad_kernel, dims=(lx, ly, lz), scale=scale),
         [sds((27 * 128, cl), BF)],
         [pltpu.VMEM((2, lx + 2, lplane + 16, 128), F32), pltpu.VMEM((2, (lx + 2) * lplane, 9 * 128), BF)],
         [pooled_delta, pd_other],
         "late_grad",
-    )
-    part, gv = call(
-        functools.partial(early_back_kernel, dims=dims),
-        [sds((27 * 128, 128), BF), sds((bx * brows, 128), BF)],
+        far=(0,),
+    )
+    back_mine, late = lax.optimization_barrier((back_mine, late))
+    part, win = call(
+        functools.partial(early_grad_kernel, dims=dims),
+        [sds((27 * 128, 128), BF), sds((bx + 2, brows + 32, 128), F32)],
         [
             pltpu.VMEM((lx * ly * gz, 128), F32),
             pltpu.VMEM((gx + 2, plane + 32, 128), F32),
             pltpu.VMEM((128, (gx + 2) * plane), BF),
-            pltpu.VMEM((bx + 2, brows + 32, 128), F32),
-            pltpu.VMEM(((bx + 2) * brows, 9 * 128), BF),
         ],
-        [pos, back, back_other, slope, col, wt],
-        "early_back",
-        smem=1,
+        [back_mine, back_other, slope, col],
+        "early_grad",
     )
     part_other = turned(part, "rep", 1)
-    (early,) = call(
-        functools.partial(finish_kernel, scale=scale), [sds((27 * 128, 128), BF)], [], [part, part_other], "finish"
-    )
+    (gv,) = call(
+        functools.partial(grad_volume_kernel, bx=bx, brows=brows, gz=gz),
+        [sds((bx * brows, 128), BF)],
+        [pltpu.VMEM(((bx + 2) * brows, 9 * 128), BF)],
+        [win, wt],
+        "grad_volume",
+        far=(0,),
+    )
+    early = ((part.astype(F32) + part_other.astype(F32)) * scale).astype(BF)
     return (
         early.reshape(3, 3, 3, 128, 128),
         late.reshape(3, 3, 3, 128, cl),

time: 55.1 us -> 42.3 us (0.77)
  Pallas kernels: 24.2 us -> 12.5 us
  waiting for transfers between devices: 11.8 us -> 6.26 us
  starting transfers between devices: 12 us -> 17.1 us
  other arithmetic: 2.38 us -> 1.2 us
  local copies, waits for them, and re-layouts: 3.62 us -> 4.25 us
    pallas_call x5, Pallas kernels: 24.2 us -> 12.5 us  [call(): pl.pallas_call(kernel, out_shape=outs, in_specs=[pl.BlockSpec(memory_spac...]
    ppermute x10 -> x13, waiting for transfers between devices: 11.8 us -> 6.26 us  [turned(): lax.ppermute(value, axis, [(i, (i + by) % count) for i in range(count)])]
    ppermute x10 -> x13, starting transfers between devices: 12 us -> 17.1 us  [turned(): lax.ppermute(value, axis, [(i, (i + by) % count) for i in range(count)])]
    concatenate x1 -> x0, other arithmetic: 0.85 us -> none  [whole_sample(): jnp.concatenate([volume.reshape(bx * brows, 128)] + [cot[:, g:g + 128] fo...]
    unnamed x24 -> x6, local copies, waits for them, and re-layouts: 2.84 us -> 3.48 us
    another operation x1 -> x0, other arithmetic: 0.62 us -> none  [whole_sample(): jnp.stack([lax.axis_index('space'), lax.axis_index('chan')])]
  transfers between devices with their start and end apart: 10 -> 13, of which waited for: 5 -> 4; matrix products, arithmetic and copies ran while one was open for 1% -> 2% of each run, Pallas kernels for 11% -> 10%
where the time goes in v2:
time: 42.3 us; the launch traced here: 42 us
  starting transfers between devices  17.1 us (40%)
  Pallas kernels  12.5 us (30%)
  waiting for transfers between devices  6.26 us (15%)
  local copies, waits for them, and re-layouts  4.25 us (10%)
  other arithmetic  1.2 us (3%)
  between operations  0.7 us (2%)
    ppermute x13, starting transfers between devices, turned(): lax.ppermute(value, axis, [(i, (i + by) % count) for i in range(count)])  17.1 us
    pallas_call x5, Pallas kernels, call(): pl.pallas_call(kernel, out_shape=outs, in_specs=[pl.BlockSpec(memory_spac...  12.5 us
    ppermute x13, waiting for transfers between devices, turned(): lax.ppermute(value, axis, [(i, (i + by) % count) for i in range(count)])  6.26 us
    unnamed x6, local copies, waits for them, and re-layouts  3.48 us
    convert_element_type x1, other arithmetic, whole_sample(): early = ((part.astype(F32) + part_other.astype(F32)) * scale).astype(BF)  1.2 us
  transfers between devices with their start and end apart: 13, of which 4 were waited for; matrix products, arithmetic and copies ran while one was open for 2% of the time, Pallas kernels for 10%

profile of v2, /device:TPU:0, one launch (start us, length us, event | category | flops | bytes accessed | tf_op | source)
XLA Modules:
  0.0 42.0 jit_solution(16998475674267155251)
XLA Ops:
  0.6 5.1 %collective-permute-start.2 = (bf16[256,128]{1,0:T(8,128)(2,1)}, bf16[256,128]{1,0:T(8,128)(2,1)S(1)}, u32[]{:S(2)}, u32[]{:S(2)}) collective-permute-start(bf16[256,128]{1,0:T(8,128)(2,1)} %bitcast.4), channel_id=1, source_target_pairs={{0,12},{4,0},{8,4},{12,8},{1,13},{5,1},{9,5},{13,9},{2,14},{6,2},{... | collective-permute-start | bytes 196616 | tf_op jit(solution)/shard_map/ppermute | solution.py:343
  5.7 0.0 collective-permute-start.1
  5.7 1.0 %collective-permute-start = (bf16[256,128]{1,0:T(8,128)(2,1)}, bf16[256,128]{1,0:T(8,128)(2,1)S(1)}, u32[]{:S(2)}, u32[]{:S(2)}) collective-permute-start(bf16[256,128]{1,0:T(8,128)(2,1)} %bitcast.6), channel_id=1, source_target_pairs={{0,4},{4,8},{8,12},{12,0},{1,5},{5,9},{9,13},{13,1},{2,6},{6,10},{... | collective-permute-start | bytes 196616 | tf_op jit(solution)/shard_map/ppermute | solution.py:343
  6.7 0.8 %reshape.22.refs_8_ = bf16[64,256]{1,0:T(8,128)(2,1)S(1)} reshape(bf16[1,1,16,4,256]{4,3,2,1,0:T(4,128)(2,1)} %param.7) | data formatting | bytes 65536 | tf_op jit(solution)/shard_map/reshape | solution.py:375
  7.5 2.9 %collective-permute-start.9 = (bf16[64,256]{1,0:T(8,128)(2,1)S(1)}, bf16[64,256]{1,0:T(8,128)(2,1)S(1)}, u32[]{:S(2)}, u32[]{:S(2)}) collective-permute-start(bf16[64,256]{1,0:T(8,128)(2,1)S(1)} %reshape.22.refs_8_), channel_id=1, source_target_pairs={{0,12},{4,0},{8,4},{12,8},{1,13},{5,1},{9,5},{13,9},{2,14},{6,2},{... | collective-permute-start | bytes 98312 | tf_op jit(solution)/shard_map/ppermute | solution.py:343
  10.4 1.1 %collective-permute-start.8 = (bf16[64,256]{1,0:T(8,128)(2,1)S(1)}, bf16[64,256]{1,0:T(8,128)(2,1)S(1)}, u32[]{:S(2)}, u32[]{:S(2)}) collective-permute-start(bf16[64,256]{1,0:T(8,128)(2,1)S(1)} %reshape.22.refs_8_), channel_id=1, source_target_pairs={{0,8},{4,12},{8,0},{12,4},{1,9},{5,13},{9,1},{13,5},{2,10},{6,14},... | collective-permute-start | bytes 98312 | tf_op jit(solution)/shard_map/ppermute | solution.py:343
  11.5 1.6 %collective-permute-done.9.refs_11_ = bf16[64,256]{1,0:T(8,128)(2,1)S(1)} collective-permute-done((bf16[64,256]{1,0:T(8,128)(2,1)S(1)}, bf16[64,256]{1,0:T(8,128)(2,1)S(1)}, u32[]{:S(2)}, u32[]{:S(2)}) %collective-permute-start.9) | collective-permute-done | bytes 32800 | tf_op jit(solution)/shard_map/ppermute | solution.py:343
  13.1 1.5 %collective-permute-start.3 = (bf16[256,128]{1,0:T(8,128)(2,1)}, bf16[256,128]{1,0:T(8,128)(2,1)S(1)}, u32[]{:S(2)}, u32[]{:S(2)}) collective-permute-start(bf16[256,128]{1,0:T(8,128)(2,1)} %bitcast.7), channel_id=1, source_target_pairs={{0,2},{2,0},{1,3},{3,1},{4,6},{6,4},{5,7},{7,5},{8,10},{10,8},{9,1... | collective-permute-start | bytes 196616 | tf_op jit(solution)/shard_map/ppermute | solution.py:343
  14.6 0.0 collective-permute-done.2.refs_3_
  14.6 0.5 %collective-permute-start.6 = (bf16[256,128]{1,0:T(8,128)(2,1)S(1)}, bf16[256,128]{1,0:T(8,128)(2,1)S(1)}, u32[]{:S(2)}, u32[]{:S(2)}) collective-permute-start(bf16[256,128]{1,0:T(8,128)(2,1)S(1)} %collective-permute-done.2.refs_3_), channel_id=1, source_target_pairs={{0,2},{2,0},{1,3},{3,1},{4,6},{6,4},{5,7},{7,5},{8,10},{10,8},{9,1... | collective-permute-start | bytes 196616 | tf_op jit(solution)/shard_map/ppermute | solution.py:343
  15.1 0.0 collective-permute-done.1.refs_2_
  15.1 1.5 %collective-permute-start.5 = (bf16[256,128]{1,0:T(8,128)(2,1)S(1)}, bf16[256,128]{1,0:T(8,128)(2,1)S(1)}, u32[]{:S(2)}, u32[]{:S(2)}) collective-permute-start(bf16[256,128]{1,0:T(8,128)(2,1)S(1)} %collective-permute-done.1.refs_2_), channel_id=1, source_target_pairs={{0,2},{2,0},{1,3},{3,1},{4,6},{6,4},{5,7},{7,5},{8,10},{10,8},{9,1... | collective-permute-start | bytes 196616 | tf_op jit(solution)/shard_map/ppermute | solution.py:343
  16.6 0.0 collective-permute-done.refs_1_
  16.6 0.5 %collective-permute-start.4 = (bf16[256,128]{1,0:T(8,128)(2,1)S(1)}, bf16[256,128]{1,0:T(8,128)(2,1)S(1)}, u32[]{:S(2)}, u32[]{:S(2)}) collective-permute-start(bf16[256,128]{1,0:T(8,128)(2,1)S(1)} %collective-permute-done.refs_1_), channel_id=1, source_target_pairs={{0,2},{2,0},{1,3},{3,1},{4,6},{6,4},{5,7},{7,5},{8,10},{10,8},{9,1... | collective-permute-start | bytes 196616 | tf_op jit(solution)/shard_map/ppermute | solution.py:343
  17.2 0.0 collective-permute-done.8.refs_10_
  17.2 1.2 %collective-permute-start.7 = (bf16[64,256]{1,0:T(8,128)(2,1)S(1)}, bf16[64,256]{1,0:T(8,128)(2,1)S(1)}, u32[]{:S(2)}, u32[]{:S(2)}) collective-permute-start(bf16[64,256]{1,0:T(8,128)(2,1)S(1)} %reshape.22.refs_8_), channel_id=1, source_target_pairs={{0,4},{4,8},{8,12},{12,0},{1,5},{5,9},{9,13},{13,1},{2,6},{6,10},{... | collective-permute-start | bytes 98312 | tf_op jit(solution)/shard_map/ppermute | solution.py:343
  18.4 0.0 copy-start.1
  18.4 1.2 %copy-done.1 = bf16[3,3,3,128,128]{4,3,2,1,0:T(8,128)(2,1)S(1)} copy-done((bf16[3,3,3,128,128]{4,3,2,1,0:T(8,128)(2,1)S(1)}, bf16[3,3,3,128,128]{4,3,2,1,0:T(8,128)(2,1)}, u32[]{:S(2)}) %copy-start.1) | copy-done | bytes 884760
  19.6 0.3 prep.1
  19.9 3.0 %collective-permute-done.7.refs_9_ = bf16[64,256]{1,0:T(8,128)(2,1)S(1)} collective-permute-done((bf16[64,256]{1,0:T(8,128)(2,1)S(1)}, bf16[64,256]{1,0:T(8,128)(2,1)S(1)}, u32[]{:S(2)}, u32[]{:S(2)}) %collective-permute-start.7) | collective-permute-done | bytes 32800 | tf_op jit(solution)/shard_map/ppermute | solution.py:343
  22.9 0.0 collective-permute-done.3.refs_4_
  22.9 0.0 collective-permute-done.6.refs_7_
  22.9 0.0 collective-permute-done.5.refs_6_
  22.9 0.0 collective-permute-done.4.refs_5_
  22.9 0.0 copy-start
  22.9 1.5 %copy-done = bf16[3,3,3,128,256]{4,3,2,1,0:T(8,128)(2,1)S(1)} copy-done((bf16[3,3,3,128,256]{4,3,2,1,0:T(8,128)(2,1)S(1)}, bf16[3,3,3,128,256]{4,3,2,1,0:T(8,128)(2,1)}, u32[]{:S(2)}) %copy-start) | copy-done | bytes 1769496
  24.4 0.0 copy-start.2
  24.4 0.8 %copy-done.2 = bf16[1,2,16,8,128]{4,3,2,1,0:T(8,128)(2,1)S(1)} copy-done((bf16[1,2,16,8,128]{4,3,2,1,0:T(8,128)(2,1)S(1)}, bf16[1,2,16,8,128]{4,3,2,1,0:T(8,128)(2,1)}, u32[]{:S(2)}) %copy-start.2) | copy-done | bytes 65560
  25.2 6.0 %forward.1 = (bf16[2048,1152]{1,0:T(8,128)(2,1)S(1)}, f32[2048,128]{1,0:T(8,128)S(1)}, bf16[256,384]{1,0:T(8,128)(2,1)S(1)}, bf16[256,128]{1,0:T(8,128)(2,1)S(1)}, f32[256,128]{1,0:T(8,128)S(1)}) custom-call(bf16[256,128]{1,0:T(8,128)(2,1)S(1)} %bitcast.8, bf16[256,128]{1,0:T(8,128)(2,1)S(1)} %collective-permute-done.refs_1_, ...), custom_call_target="tpu_custom_call" | custom-call | tf_op jit(solution)/shard_map/forward/pallas_call | solution.py:349
  31.2 0.1 collective-permute-start.10
  31.3 1.6 %collective-permute-start.11 = (bf16[256,128]{1,0:T(8,128)(2,1)S(1)}, bf16[256,128]{1,0:T(8,128)(2,1)S(1)}, u32[]{:S(2)}, u32[]{:S(2)}) collective-permute-start(bf16[256,128]{1,0:T(8,128)(2,1)S(1)} %get-tuple-element.18), channel_id=1, source_target_pairs={{0,2},{2,0},{1,3},{3,1},{4,6},{6,4},{5,7},{7,5},{8,10},{10,8},{9,1... | collective-permute-start | bytes 196616 | tf_op jit(solution)/shard_map/ppermute | solution.py:343
  32.9 0.0 collective-permute-done.10.other_ref
  32.9 2.4 %late_grad.1 = bf16[3456,256]{1,0:T(8,128)(2,1)} custom-call(bf16[256,384]{1,0:T(8,128)(2,1)S(1)} %get-tuple-element.16.mine_ref, bf16[256,384]{1,0:T(8,128)(2,1)S(1)} %collective-permute-done.10.other_ref), custom_call_target="tpu_custom_call" | custom-call | tf_op jit(solution)/shard_map/late_grad/pallas_call | solution.py:349
  35.3 0.5 %collective-permute-done.11.other_ref = bf16[256,128]{1,0:T(8,128)(2,1)S(1)} collective-permute-done((bf16[256,128]{1,0:T(8,128)(2,1)S(1)}, bf16[256,128]{1,0:T(8,128)(2,1)S(1)}, u32[]{:S(2)}, u32[]{:S(2)}) %collective-permute-start.11) | collective-permute-done | bytes 65568 | tf_op jit(solution)/shard_map/ppermute | solution.py:343
  35.8 2.4 %early_grad.1 = (bf16[3456,128]{1,0:T(8,128)(2,1)S(1)}, f32[4,160,128]{2,1,0:T(8,128)S(1)}) custom-call(f32[256,128]{1,0:T(8,128)S(1)} %get-tuple-element.17.mine_ref, bf16[256,128]{1,0:T(8,128)(2,1)S(1)} %collective-permute-done.11.other_ref, f32[2048,128]{1,0:T(8,128)S(1)} %get-tuple-element.19.slope_ref, bf16[2048,1152]{1,0:T(8,128)(2,1)S(1)} %get-tuple-element.20.col_ref), custom_call_target="tpu_custom_call" | custom-call | tf_op jit(solution)/shard_map/early_grad/pallas_call | solution.py:349
  38.3 0.1 collective-permute-start.12
  38.4 1.3 %grad_volume.1 = bf16[256,128]{1,0:T(8,128)(2,1)} custom-call(f32[4,160,128]{2,1,0:T(8,128)S(1)} %get-tuple-element.23.win_ref, bf16[3,1152,128]{2,1,0:T(8,128)(2,1)S(1)} %get-tuple-element.24.wt_ref), custom_call_target="tpu_custom_call" | custom-call | tf_op jit(solution)/shard_map/grad_volume/pallas_call | solution.py:349
  39.6 1.2 %collective-permute-done.12 = bf16[3456,128]{1,0:T(8,128)(2,1)S(1)} collective-permute-done((bf16[3456,128]{1,0:T(8,128)(2,1)S(1)}, bf16[3456,128]{1,0:T(8,128)(2,1)S(1)}, u32[]{:S(2)}, u32[]{:S(2)}) %collective-permute-start.12) | collective-permute-done | bytes 884768 | tf_op jit(solution)/shard_map/ppermute | solution.py:343
  40.8 1.2 %multiply_convert_fusion = bf16[3456,128]{1,0:T(8,128)(2,1)} fusion(bf16[3456,128]{1,0:T(8,128)(2,1)S(1)} %collective-permute-done.12, bf16[3456,128]{1,0:T(8,128)(2,1)S(1)} %get-tuple-element.21), kind=kLoop, calls=%fused_computation | loop fusion | flops 2211840 | bytes 2654208 | tf_op jit(solution)/shard_map/convert_element_type | solution.py:433
Async XLA Ops:
  0.6 14.0 %collective-permute-start.2 = (bf16[256,128]{1,0:T(8,128)(2,1)}, bf16[256,128]{1,0:T(8,128)(2,1)S(1)}, u32[]{:S(2)}, u32[]{:S(2)}) collective-permute-start(bf16[256,128]{1,0:T(8,128)(2,1)} %bitcast.4), channel_id=1, source_target_pairs={{0,12},{4,0},{8,4},{12,8},{1,13},{5,1},{9,5},{13,9},{2,14},{6,2},{... | collective-permute-start | bytes 196616 | tf_op jit(solution)/shard_map/ppermute | solution.py:343
  5.7 9.4 %collective-permute-start.1 = (bf16[256,128]{1,0:T(8,128)(2,1)}, bf16[256,128]{1,0:T(8,128)(2,1)S(1)}, u32[]{:S(2)}, u32[]{:S(2)}) collective-permute-start(bf16[256,128]{1,0:T(8,128)(2,1)} %bitcast.5), channel_id=1, source_target_pairs={{0,8},{4,12},{8,0},{12,4},{1,9},{5,13},{9,1},{13,5},{2,10},{6,14},... | collective-permute-start | bytes 196616 | tf_op jit(solution)/shard_map/ppermute | solution.py:343
  5.7 10.9 %collective-permute-start = (bf16[256,128]{1,0:T(8,128)(2,1)}, bf16[256,128]{1,0:T(8,128)(2,1)S(1)}, u32[]{:S(2)}, u32[]{:S(2)}) collective-permute-start(bf16[256,128]{1,0:T(8,128)(2,1)} %bitcast.6), channel_id=1, source_target_pairs={{0,4},{4,8},{8,12},{12,0},{1,5},{5,9},{9,13},{13,1},{2,6},{6,10},{... | collective-permute-start | bytes 196616 | tf_op jit(solution)/shard_map/ppermute | solution.py:343
  7.5 5.6 %collective-permute-start.9 = (bf16[64,256]{1,0:T(8,128)(2,1)S(1)}, bf16[64,256]{1,0:T(8,128)(2,1)S(1)}, u32[]{:S(2)}, u32[]{:S(2)}) collective-permute-start(bf16[64,256]{1,0:T(8,128)(2,1)S(1)} %reshape.22.refs_8_), channel_id=1, source_target_pairs={{0,12},{4,0},{8,4},{12,8},{1,13},{5,1},{9,5},{13,9},{2,14},{6,2},{... | collective-permute-start | bytes 98312 | tf_op jit(solution)/shard_map/ppermute | solution.py:343
  10.4 6.8 %collective-permute-start.8 = (bf16[64,256]{1,0:T(8,128)(2,1)S(1)}, bf16[64,256]{1,0:T(8,128)(2,1)S(1)}, u32[]{:S(2)}, u32[]{:S(2)}) collective-permute-start(bf16[64,256]{1,0:T(8,128)(2,1)S(1)} %reshape.22.refs_8_), channel_id=1, source_target_pairs={{0,8},{4,12},{8,0},{12,4},{1,9},{5,13},{9,1},{13,5},{2,10},{6,14},... | collective-permute-start | bytes 98312 | tf_op jit(solution)/shard_map/ppermute | solution.py:343
  13.1 9.8 %collective-permute-start.3 = (bf16[256,128]{1,0:T(8,128)(2,1)}, bf16[256,128]{1,0:T(8,128)(2,1)S(1)}, u32[]{:S(2)}, u32[]{:S(2)}) collective-permute-start(bf16[256,128]{1,0:T(8,128)(2,1)} %bitcast.7), channel_id=1, source_target_pairs={{0,2},{2,0},{1,3},{3,1},{4,6},{6,4},{5,7},{7,5},{8,10},{10,8},{9,1... | collective-permute-start | bytes 196616 | tf_op jit(solution)/shard_map/ppermute | solution.py:343
  14.6 8.3 %collective-permute-start.6 = (bf16[256,128]{1,0:T(8,128)(2,1)S(1)}, bf16[256,128]{1,0:T(8,128)(2,1)S(1)}, u32[]{:S(2)}, u32[]{:S(2)}) collective-permute-start(bf16[256,128]{1,0:T(8,128)(2,1)S(1)} %collective-permute-done.2.refs_3_), channel_id=1, source_target_pairs={{0,2},{2,0},{1,3},{3,1},{4,6},{6,4},{5,7},{7,5},{8,10},{10,8},{9,1... | collective-permute-start | bytes 196616 | tf_op jit(solution)/shard_map/ppermute | solution.py:343
  15.1 7.8 %collective-permute-start.5 = (bf16[256,128]{1,0:T(8,128)(2,1)S(1)}, bf16[256,128]{1,0:T(8,128)(2,1)S(1)}, u32[]{:S(2)}, u32[]{:S(2)}) collective-permute-start(bf16[256,128]{1,0:T(8,128)(2,1)S(1)} %collective-permute-done.1.refs_2_), channel_id=1, source_target_pairs={{0,2},{2,0},{1,3},{3,1},{4,6},{6,4},{5,7},{7,5},{8,10},{10,8},{9,1... | collective-permute-start | bytes 196616 | tf_op jit(solution)/shard_map/ppermute | solution.py:343
  16.6 6.3 %collective-permute-start.4 = (bf16[256,128]{1,0:T(8,128)(2,1)S(1)}, bf16[256,128]{1,0:T(8,128)(2,1)S(1)}, u32[]{:S(2)}, u32[]{:S(2)}) collective-permute-start(bf16[256,128]{1,0:T(8,128)(2,1)S(1)} %collective-permute-done.refs_1_), channel_id=1, source_target_pairs={{0,2},{2,0},{1,3},{3,1},{4,6},{6,4},{5,7},{7,5},{8,10},{10,8},{9,1... | collective-permute-start | bytes 196616 | tf_op jit(solution)/shard_map/ppermute | solution.py:343
  17.2 5.7 %collective-permute-start.7 = (bf16[64,256]{1,0:T(8,128)(2,1)S(1)}, bf16[64,256]{1,0:T(8,128)(2,1)S(1)}, u32[]{:S(2)}, u32[]{:S(2)}) collective-permute-start(bf16[64,256]{1,0:T(8,128)(2,1)S(1)} %reshape.22.refs_8_), channel_id=1, source_target_pairs={{0,4},{4,8},{8,12},{12,0},{1,5},{5,9},{9,13},{13,1},{2,6},{6,10},{... | collective-permute-start | bytes 98312 | tf_op jit(solution)/shard_map/ppermute | solution.py:343
  18.4 1.2 %copy-start.1 = (bf16[3,3,3,128,128]{4,3,2,1,0:T(8,128)(2,1)S(1)}, bf16[3,3,3,128,128]{4,3,2,1,0:T(8,128)(2,1)}, u32[]{:S(2)}) copy-start(bf16[3,3,3,128,128]{4,3,2,1,0:T(8,128)(2,1)} %we_ref.1) | copy-start | bytes 2654212
  22.9 1.5 %copy-start = (bf16[3,3,3,128,256]{4,3,2,1,0:T(8,128)(2,1)S(1)}, bf16[3,3,3,128,256]{4,3,2,1,0:T(8,128)(2,1)}, u32[]{:S(2)}) copy-start(bf16[3,3,3,128,256]{4,3,2,1,0:T(8,128)(2,1)} %refs_13_.1) | copy-start | bytes 5308420
  24.4 0.8 %copy-start.2 = (bf16[1,2,16,8,128]{4,3,2,1,0:T(8,128)(2,1)S(1)}, bf16[1,2,16,8,128]{4,3,2,1,0:T(8,128)(2,1)}, u32[]{:S(2)}) copy-start(bf16[1,2,16,8,128]{4,3,2,1,0:T(8,128)(2,1)} %param.4) | copy-start | bytes 196612
  31.2 1.6 %collective-permute-start.10 = (bf16[256,384]{1,0:T(8,128)(2,1)S(1)}, bf16[256,384]{1,0:T(8,128)(2,1)S(1)}, u32[]{:S(2)}, u32[]{:S(2)}) collective-permute-start(bf16[256,384]{1,0:T(8,128)(2,1)S(1)} %get-tuple-element.16.mine_ref), channel_id=1, source_target_pairs={{0,1},{1,0},{2,3},{3,2},{4,5},{5,4},{6,7},{7,6},{8,9},{9,8},{10,11... | collective-permute-start | bytes 589832 | tf_op jit(solution)/shard_map/ppermute | solution.py:343
  31.3 4.5 %collective-permute-start.11 = (bf16[256,128]{1,0:T(8,128)(2,1)S(1)}, bf16[256,128]{1,0:T(8,128)(2,1)S(1)}, u32[]{:S(2)}, u32[]{:S(2)}) collective-permute-start(bf16[256,128]{1,0:T(8,128)(2,1)S(1)} %get-tuple-element.18), channel_id=1, source_target_pairs={{0,2},{2,0},{1,3},{3,1},{4,6},{6,4},{5,7},{7,5},{8,10},{10,8},{9,1... | collective-permute-start | bytes 196616 | tf_op jit(solution)/shard_map/ppermute | solution.py:343
  38.3 2.5 %collective-permute-start.12 = (bf16[3456,128]{1,0:T(8,128)(2,1)S(1)}, bf16[3456,128]{1,0:T(8,128)(2,1)S(1)}, u32[]{:S(2)}, u32[]{:S(2)}) collective-permute-start(bf16[3456,128]{1,0:T(8,128)(2,1)S(1)} %get-tuple-element.21), channel_id=1, source_target_pairs={{0,1},{1,0},{2,3},{3,2},{4,5},{5,4},{6,7},{7,6},{8,9},{9,8},{10,11... | collective-permute-start | bytes 2654216 | tf_op jit(solution)/shard_map/ppermute | solution.py:343

commit v3 on v2

--- a/solution.py
+++ b/solution.py
@@ -162,37 +162,33 @@
 STEPS = [(b, c) for b in (-1, 0, 1) for c in (-1, 0, 1)]
 
 
-def prep_kernel(we_ref, wcat_ref, wt_ref):
-    for n in range(9):
-        b, c = divmod(n, 3)
-        for a in range(3):
-            w = we_ref[a, b, c]
-            wcat_ref[pl.ds(n * 128, 128), pl.ds(a * 128, 128)] = w
-            wt_ref[a, pl.ds(n * 128, 128), :] = w.astype(F32).T.astype(BF)
-
-
-def forward_kernel(*refs, nk, nj, dims):
+def early_kernel(*refs, nk, nj, dims):
     gx, gy, gz, lx, ly, lz, bx, by = dims
     blocks, refs = refs[: nk * nj], refs[nk * nj :]
-    cots, refs = refs[:nk], refs[nk:]
-    wcat_ref, wl_ref, col_ref, slope_ref, pd_ref, back_ref, mine_ref = refs[:7]
-    vol_ref, p_ref, h_ref, pool_ref, lcol_ref, dl_ref = refs[7:]
+    we_hbm, wl_hbm, we_ref, wl_ref, col_ref, slope_ref, pooled_ref = refs[:7]
+    vol_ref, own_ref, wcat_ref, p_ref, h_ref, sems = refs[7:]
     k, j = lax.axis_index("space"), lax.axis_index("chan")
     plane, lplane = gy * gz, ly * lz
     brows = by * gz
-    cl = wl_ref.shape[-1]
-    crow = bx // 2 * lplane
+    own_copy = pltpu.make_async_copy(blocks[0], own_ref, sems.at[0])
+    we_copy = pltpu.make_async_copy(we_hbm, we_ref, sems.at[1])
+    wl_copy = pltpu.make_async_copy(wl_hbm, wl_ref, sems.at[2])
+    own_copy.start()
+    we_copy.start()
+    wl_copy.start()
 
     vol_ref[:, pl.ds(0, 16), :] = jnp.zeros((gx, 16, 128), F32)
     vol_ref[:, pl.ds(16 + plane, 16), :] = jnp.zeros((gx, 16, 128), F32)
-    for dj in range(nj):
-        for dk in range(nk):
-            src = blocks[dj * nk + dk]
-            kk = lax.rem(k + nk - dk, nk)
-            jj = lax.rem(j + nj - dj, nj)
-            row = pl.multiple_of(16 + jj * brows, 8)
-            for q in range(bx):
-                vol_ref[kk * bx + q, pl.ds(row, brows), :] = src[pl.ds(q * brows, brows), :].astype(F32)
+    for n in [*range(1, nk * nj), 0]:
+        dj, dk = divmod(n, nk)
+        if n == 0:
+            own_copy.wait()
+        src = blocks[n] if n else own_ref
+        kk = lax.rem(k + nk - dk, nk)
+        jj = lax.rem(j + nj - dj, nj)
+        row = pl.multiple_of(16 + jj * brows, 8)
+        for q in range(bx):
+            vol_ref[kk * bx + q, pl.ds(row, brows), :] = src[pl.ds(q * brows, brows), :].astype(F32)
 
     cell = depth_of(plane, gz)
     for x in range(gx):
@@ -201,6 +197,11 @@
                 vol_ref, (x,), 16, plane, cell, gz, step
             ).astype(BF)
 
+    we_copy.wait()
+    for n in range(9):
+        b, c = divmod(n, 3)
+        for a in range(3):
+            wcat_ref[pl.ds(n * 128, 128), pl.ds(a * 128, 128)] = we_ref[a, b, c]
     p_ref[...] = jnp.dot(col_ref[...], wcat_ref[...], preferred_element_type=F32)
 
     for lq in range(lx):
@@ -217,11 +218,23 @@
         wide = pair.reshape(ly, 2, gz, 128)
         h_ref[...] = (wide[:, 0] + wide[:, 1]).reshape(ly * gz, 128)
         pooled = (h_ref[pl.ds(0, lplane, stride=2), :] + h_ref[pl.ds(1, lplane, stride=2), :]) * 0.125
-        pooled = pooled.astype(BF)
-        pd_ref[pl.ds(lq * lplane, lplane), pl.ds(0, 128)] = pooled
-        pool_ref[lq, pl.ds(0, 8), :] = jnp.zeros((8, 128), F32)
-        pool_ref[lq, pl.ds(8 + lplane, 8), :] = jnp.zeros((8, 128), F32)
-        pool_ref[lq, pl.ds(8, lplane), :] = pooled.astype(F32)
+        pooled_ref[pl.ds(lq * lplane, lplane), :] = pooled.astype(BF)
+    wl_copy.wait()
+
+
+def late_kernel(*refs, nk, dims):
+    lx, ly, lz, cx = dims
+    pooled_ref, cots, refs = refs[0], refs[1 : nk + 1], refs[nk + 1 :]
+    wl_ref, pd_ref, back_ref, mine_ref, pool_ref, lcol_ref, dl_ref, cot_ref = refs
+    lplane = ly * lz
+    cl = wl_ref.shape[-1]
+    crow = cx * lplane
+    k = lax.axis_index("space")
+    for x in range(lx):
+        pool_ref[x, pl.ds(0, 8), :] = jnp.zeros((8, 128), F32)
+        pool_ref[x, pl.ds(8 + lplane, 8), :] = jnp.zeros((8, 128), F32)
+        pool_ref[x, pl.ds(8, lplane), :] = pooled_ref[pl.ds(x * lplane, lplane), :].astype(F32)
+    pd_ref[:, pl.ds(0, 128)] = pooled_ref[...]
 
     lcell = depth_of(lplane, lz)
     for x in range(lx):
@@ -244,9 +257,8 @@
     for dk in range(nk):
         kk = lax.rem(k + nk - dk, nk)
         start = pl.multiple_of(kk * crow, 8)
-        p_ref[pl.ds(start, crow), pl.ds(0, cl)] = cots[dk][...].astype(F32)
-    cot = p_ref[pl.ds(0, lx * lplane), pl.ds(0, cl)]
-    delta = (cot * slope).astype(BF)
+        cot_ref[pl.ds(start, crow), :] = cots[dk][...].astype(F32)
+    delta = (cot_ref[...] * slope).astype(BF)
     pd_ref[:, pl.ds(128, cl)] = delta
     wide = delta.astype(F32)
     for x in range(lx):
@@ -324,7 +336,11 @@
         win_ref[q] = d_ref[k * bx + q, pl.ds(row, brows + 32), :]
 
 
-def grad_volume_kernel(win_ref, wt_ref, gv_ref, vcol_ref, *, bx, brows, gz):
+def grad_volume_kernel(win_ref, we_ref, gv_ref, vcol_ref, wt_ref, *, bx, brows, gz):
+    for n in range(9):
+        b, c = divmod(n, 3)
+        for a in range(3):
+            wt_ref[a, pl.ds(n * 128, 128), :] = we_ref[a, b, c].astype(F32).T.astype(BF)
     cell = depth_of(brows, gz)
     for q in range(bx + 2):
         for n, (b, c) in enumerate(STEPS):
@@ -343,13 +359,18 @@
     return lax.ppermute(value, axis, [(i, (i + by) % count) for i in range(count)])
 
 
-def call(kernel, outs, scratch, args, name, far=()):
-    args = [pltpu.with_memory_space_constraint(arg, pltpu.VMEM) for arg in args]
+def call(kernel, outs, scratch, args, name, far=(), raw=()):
+    args = [
+        pltpu.with_memory_space_constraint(arg, pltpu.HBM if n in raw else pltpu.VMEM)
+        for n, arg in enumerate(args)
+    ]
     outs = [out if n in far else pltpu.VMEM(out.shape, out.dtype) for n, out in enumerate(outs)]
     return pl.pallas_call(
         kernel,
         out_shape=outs,
-        in_specs=[pl.BlockSpec(memory_space=pltpu.VMEM)] * len(args),
+        in_specs=[
+            pl.BlockSpec(memory_space=pltpu.HBM if n in raw else pltpu.VMEM) for n in range(len(args))
+        ],
         out_specs=[pl.BlockSpec(memory_space=pltpu.VMEM)] * len(outs),
         scratch_shapes=scratch,
         compiler_params=pltpu.CompilerParams(vmem_limit_bytes=VMEM_BYTES),
@@ -373,31 +394,42 @@
     for dj in range(1, nj):
         blocks += [turned(block, "chan", dj) for block in line]
     cot = cotangent.reshape(cx * lplane, cl)
-    cots = [cot] + [turned(cot, "space", dk) for dk in range(1, nk)]
-
-    wcat, wt = call(
-        prep_kernel, [sds((9 * 128, 3 * 128), BF), sds((3, 9 * 128, 128), BF)], [], [early_weight], "prep"
-    )
-    dims = (gx, gy, gz, lx, ly, lz, bx, by)
-    col, slope, pooled_delta, back, back_mine = call(
-        functools.partial(forward_kernel, nk=nk, nj=nj, dims=dims),
+    held = lax.optimization_barrier((cot, *line[1:]))[0]
+    cots = [cot] + [turned(held, "space", dk) for dk in range(1, nk)]
+
+    count = nk * nj
+    we, wl, col, slope, pooled = call(
+        functools.partial(early_kernel, nk=nk, nj=nj, dims=(gx, gy, gz, lx, ly, lz, bx, by)),
         [
+            sds(early_weight.shape, BF),
+            sds(late_weight.shape, BF),
             sds((rows, 9 * 128), BF),
             sds((rows, 128), F32),
-            sds((lrows, 128 + cl), BF),
             sds((lrows, 128), BF),
-            sds((lrows, 128), F32),
         ],
         [
             pltpu.VMEM((gx, plane + 32, 128), F32),
+            pltpu.VMEM((bx * brows, 128), BF),
+            pltpu.VMEM((9 * 128, 3 * 128), BF),
             pltpu.VMEM((rows, 3 * 128), F32),
             pltpu.VMEM((ly * gz, 128), F32),
+            pltpu.SemaphoreType.DMA((3,)),
+        ],
+        blocks + [early_weight, late_weight],
+        "early",
+        raw=(0, count, count + 1),
+    )
+    pooled_delta, back, back_mine = call(
+        functools.partial(late_kernel, nk=nk, dims=(lx, ly, lz, cx)),
+        [sds((lrows, 128 + cl), BF), sds((lrows, 128), BF), sds((lrows, 128), F32)],
+        [
             pltpu.VMEM((lx, lplane + 16, 128), F32),
             pltpu.VMEM((lrows, 9 * 128), BF),
             pltpu.VMEM((lx, lplane + 16, cl), F32),
+            pltpu.VMEM((lrows, cl), F32),
         ],
-        blocks + cots + [wcat, late_weight],
-        "forward",
+        [pooled] + cots + [wl],
+        "late",
     )
     pd_other = turned(pooled_delta, "rep", 1)
     back_other = turned(back, "chan", 1)
@@ -411,7 +443,7 @@
     )
     back_mine, late = lax.optimization_barrier((back_mine, late))
     part, win = call(
-        functools.partial(early_grad_kernel, dims=dims),
+        functools.partial(early_grad_kernel, dims=(gx, gy, gz, lx, ly, lz, bx, by)),
         [sds((27 * 128, 128), BF), sds((bx + 2, brows + 32, 128), F32)],
         [
             pltpu.VMEM((lx * ly * gz, 128), F32),
@@ -425,8 +457,8 @@
     (gv,) = call(
         functools.partial(grad_volume_kernel, bx=bx, brows=brows, gz=gz),
         [sds((bx * brows, 128), BF)],
-        [pltpu.VMEM(((bx + 2) * brows, 9 * 128), BF)],
-        [win, wt],
+        [pltpu.VMEM(((bx + 2) * brows, 9 * 128), BF), pltpu.VMEM((3, 9 * 128, 128), BF)],
+        [win, we],
         "grad_volume",
         far=(0,),
     )

time: 42.3 us -> 37.3 us (0.88)
  local copies, waits for them, and re-layouts: 4.25 us -> 0.77 us
  starting transfers between devices: 17.1 us -> 15.4 us
  Pallas kernels: 12.5 us -> 14.1 us
  waiting for transfers between devices: 6.26 us -> 4.95 us
    unnamed x6 -> x0, local copies, waits for them, and re-layouts: 3.48 us -> none
    ppermute x13, starting transfers between devices: 17.1 us -> 15.4 us  [turned(): lax.ppermute(value, axis, [(i, (i + by) % count) for i in range(count)])]
    pallas_call x5, Pallas kernels: 12.5 us -> 14.1 us  [call(): pl.pallas_call(kernel, out_shape=outs, in_specs=[pl.BlockSpec(memory_spac...]
    ppermute x13, waiting for transfers between devices: 6.26 us -> 4.95 us  [turned(): lax.ppermute(value, axis, [(i, (i + by) % count) for i in range(count)])]
  transfers between devices with their start and end apart: 13 -> 13, of which waited for: 4 -> 5; matrix products, arithmetic and copies ran while one was open for 2% -> 2% of each run, Pallas kernels for 10% -> 25%
where the time goes in v3:
time: 37.3 us; the launch traced here: 37.1 us
  starting transfers between devices  15.4 us (41%)
  Pallas kernels  14.1 us (38%)
  waiting for transfers between devices  4.95 us (13%)
  other arithmetic  1.2 us (3%)
  local copies, waits for them, and re-layouts  0.77 us (2%)
  between operations  0.71 us (2%)
    ppermute x13, starting transfers between devices, turned(): lax.ppermute(value, axis, [(i, (i + by) % count) for i in range(count)])  15.4 us
    pallas_call x5, Pallas kernels, call(): pl.pallas_call(kernel, out_shape=outs, in_specs=[pl.BlockSpec(memory_spac...  14.1 us
    ppermute x13, waiting for transfers between devices, turned(): lax.ppermute(value, axis, [(i, (i + by) % count) for i in range(count)])  4.95 us
    convert_element_type x1, other arithmetic, whole_sample(): early = ((part.astype(F32) + part_other.astype(F32)) * scale).astype(BF)  1.2 us
    reshape x1, local copies, waits for them, and re-layouts, whole_sample(): cot = cotangent.reshape(cx * lplane, cl)  0.77 us
  transfers between devices with their start and end apart: 13, of which 5 were waited for; matrix products, arithmetic and copies ran while one was open for 2% of the time, Pallas kernels for 25%

profile of v3, /device:TPU:0, one launch (start us, length us, event | category | flops | bytes accessed | tf_op | source)
XLA Modules:
  0.0 37.1 jit_solution(8806055801202535253)
XLA Ops:
  0.6 5.1 %collective-permute-start.2 = (bf16[256,128]{1,0:T(8,128)(2,1)}, bf16[256,128]{1,0:T(8,128)(2,1)S(1)}, u32[]{:S(2)}, u32[]{:S(2)}) collective-permute-start(bf16[256,128]{1,0:T(8,128)(2,1)} %bitcast.6), channel_id=1, source_target_pairs={{0,12},{4,0},{8,4},{12,8},{1,13},{5,1},{9,5},{13,9},{2,14},{6,2},{... | collective-permute-start | bytes 196616 | tf_op jit(solution)/shard_map/ppermute | solution.py:359
  5.7 0.0 collective-permute-start.1
  5.7 1.0 %collective-permute-start = (bf16[256,128]{1,0:T(8,128)(2,1)}, bf16[256,128]{1,0:T(8,128)(2,1)S(1)}, u32[]{:S(2)}, u32[]{:S(2)}) collective-permute-start(bf16[256,128]{1,0:T(8,128)(2,1)} %bitcast.8), channel_id=1, source_target_pairs={{0,4},{4,8},{8,12},{12,0},{1,5},{5,9},{9,13},{13,1},{2,6},{6,10},{... | collective-permute-start | bytes 196616 | tf_op jit(solution)/shard_map/ppermute | solution.py:359
  6.7 1.5 %collective-permute-start.3 = (bf16[256,128]{1,0:T(8,128)(2,1)}, bf16[256,128]{1,0:T(8,128)(2,1)S(1)}, u32[]{:S(2)}, u32[]{:S(2)}) collective-permute-start(bf16[256,128]{1,0:T(8,128)(2,1)} %bitcast.9), channel_id=1, source_target_pairs={{0,2},{2,0},{1,3},{3,1},{4,6},{6,4},{5,7},{7,5},{8,10},{10,8},{9,1... | collective-permute-start | bytes 196616 | tf_op jit(solution)/shard_map/ppermute | solution.py:359
  8.2 0.3 collective-permute-done.2.refs_3_
  8.5 1.5 %collective-permute-start.6 = (bf16[256,128]{1,0:T(8,128)(2,1)S(1)}, bf16[256,128]{1,0:T(8,128)(2,1)S(1)}, u32[]{:S(2)}, u32[]{:S(2)}) collective-permute-start(bf16[256,128]{1,0:T(8,128)(2,1)S(1)} %collective-permute-done.2.refs_3_), channel_id=1, source_target_pairs={{0,2},{2,0},{1,3},{3,1},{4,6},{6,4},{5,7},{7,5},{8,10},{10,8},{9,1... | collective-permute-start | bytes 196616 | tf_op jit(solution)/shard_map/ppermute | solution.py:359
  10.0 2.4 %collective-permute-done.1.refs_2_ = bf16[256,128]{1,0:T(8,128)(2,1)S(1)} collective-permute-done((bf16[256,128]{1,0:T(8,128)(2,1)}, bf16[256,128]{1,0:T(8,128)(2,1)S(1)}, u32[]{:S(2)}, u32[]{:S(2)}) %collective-permute-start.1) | collective-permute-done | bytes 65568 | tf_op jit(solution)/shard_map/ppermute | solution.py:359
  12.4 1.5 %collective-permute-start.5 = (bf16[256,128]{1,0:T(8,128)(2,1)S(1)}, bf16[256,128]{1,0:T(8,128)(2,1)S(1)}, u32[]{:S(2)}, u32[]{:S(2)}) collective-permute-start(bf16[256,128]{1,0:T(8,128)(2,1)S(1)} %collective-permute-done.1.refs_2_), channel_id=1, source_target_pairs={{0,2},{2,0},{1,3},{3,1},{4,6},{6,4},{5,7},{7,5},{8,10},{10,8},{9,1... | collective-permute-start | bytes 196616 | tf_op jit(solution)/shard_map/ppermute | solution.py:359
  13.9 0.0 collective-permute-done.refs_1_
  13.9 0.5 %collective-permute-start.4 = (bf16[256,128]{1,0:T(8,128)(2,1)S(1)}, bf16[256,128]{1,0:T(8,128)(2,1)S(1)}, u32[]{:S(2)}, u32[]{:S(2)}) collective-permute-start(bf16[256,128]{1,0:T(8,128)(2,1)S(1)} %collective-permute-done.refs_1_), channel_id=1, source_target_pairs={{0,2},{2,0},{1,3},{3,1},{4,6},{6,4},{5,7},{7,5},{8,10},{10,8},{9,1... | collective-permute-start | bytes 196616 | tf_op jit(solution)/shard_map/ppermute | solution.py:359
  14.4 0.8 %reshape.22.refs_1_ = bf16[64,256]{1,0:T(8,128)(2,1)S(1)} reshape(bf16[1,1,16,4,256]{4,3,2,1,0:T(4,128)(2,1)} %param.7) | data formatting | bytes 65536 | tf_op jit(solution)/shard_map/reshape | solution.py:396
  15.2 1.9 %collective-permute-start.9 = (bf16[64,256]{1,0:T(8,128)(2,1)S(1)}, bf16[64,256]{1,0:T(8,128)(2,1)S(1)}, u32[]{:S(2)}, u32[]{:S(2)}) collective-permute-start(bf16[64,256]{1,0:T(8,128)(2,1)S(1)} %reshape.22.refs_1_), channel_id=1, source_target_pairs={{0,12},{4,0},{8,4},{12,8},{1,13},{5,1},{9,5},{13,9},{2,14},{6,2},{... | collective-permute-start | bytes 98312 | tf_op jit(solution)/shard_map/ppermute | solution.py:359
  17.2 0.0 collective-permute-done.3.refs_4_
  17.2 0.0 collective-permute-start.8
  17.2 0.0 collective-permute-done.6.refs_7_
  17.2 1.4 %collective-permute-start.7 = (bf16[64,256]{1,0:T(8,128)(2,1)S(1)}, bf16[64,256]{1,0:T(8,128)(2,1)S(1)}, u32[]{:S(2)}, u32[]{:S(2)}) collective-permute-start(bf16[64,256]{1,0:T(8,128)(2,1)S(1)} %reshape.22.refs_1_), channel_id=1, source_target_pairs={{0,4},{4,8},{8,12},{12,0},{1,5},{5,9},{9,13},{13,1},{2,6},{6,10},{... | collective-permute-start | bytes 98312 | tf_op jit(solution)/shard_map/ppermute | solution.py:359
  18.5 0.0 collective-permute-done.5.refs_6_
  18.5 0.0 collective-permute-done.4.refs_5_
  18.5 5.3 %early.1 = (bf16[3,3,3,128,128]{4,3,2,1,0:T(8,128)(2,1)S(1)}, bf16[3,3,3,128,256]{4,3,2,1,0:T(8,128)(2,1)S(1)}, bf16[2048,1152]{1,0:T(8,128)(2,1)S(1)}, f32[2048,128]{1,0:T(8,128)S(1)}, bf16[256,128]{1,0:T(8,128)(2,1)S(1)}) custom-call(bf16[256,128]{1,0:T(8,128)(2,1)} %bitcast.10, bf16[256,128]{1,0:T(8,128)(2,1)S(1)} %collective-permute-done.refs_1_, ...), custom_call_target="tpu_custom_call" | custom-call | tf_op jit(solution)/shard_map/early/pallas_call | solution.py:368
  23.8 0.0 collective-permute-done.9.refs_4_
  23.8 0.0 collective-permute-done.8.refs_3_
  23.9 0.0 collective-permute-done.7.refs_2_
  23.9 2.5 %late.1 = (bf16[256,384]{1,0:T(8,128)(2,1)S(1)}, bf16[256,128]{1,0:T(8,128)(2,1)S(1)}, f32[256,128]{1,0:T(8,128)S(1)}) custom-call(bf16[256,128]{1,0:T(8,128)(2,1)S(1)} %get-tuple-element.16.refs_0_, bf16[64,256]{1,0:T(8,128)(2,1)S(1)} %reshape.22.refs_1_, bf16[64,256]{1,0:T(8,128)(2,1)S(1)} %collective-permute-done.7.refs_2_, ...), custom_call_target="tpu_custom_call" | custom-call | tf_op jit(solution)/shard_map/late/pallas_call | solution.py:368
  26.4 0.1 collective-permute-start.10
  26.5 0.8 %collective-permute-start.11 = (bf16[256,128]{1,0:T(8,128)(2,1)S(1)}, bf16[256,128]{1,0:T(8,128)(2,1)S(1)}, u32[]{:S(2)}, u32[]{:S(2)}) collective-permute-start(bf16[256,128]{1,0:T(8,128)(2,1)S(1)} %get-tuple-element.22), channel_id=1, source_target_pairs={{0,2},{2,0},{1,3},{3,1},{4,6},{6,4},{5,7},{7,5},{8,10},{10,8},{9,1... | collective-permute-start | bytes 196616 | tf_op jit(solution)/shard_map/ppermute | solution.py:359
  27.3 0.6 %collective-permute-done.10.other_ref = bf16[256,384]{1,0:T(8,128)(2,1)S(1)} collective-permute-done((bf16[256,384]{1,0:T(8,128)(2,1)S(1)}, bf16[256,384]{1,0:T(8,128)(2,1)S(1)}, u32[]{:S(2)}, u32[]{:S(2)}) %collective-permute-start.10) | collective-permute-done | bytes 196640 | tf_op jit(solution)/shard_map/ppermute | solution.py:359
  27.9 2.4 %late_grad.1 = bf16[3456,256]{1,0:T(8,128)(2,1)} custom-call(bf16[256,384]{1,0:T(8,128)(2,1)S(1)} %get-tuple-element.20.mine_ref, bf16[256,384]{1,0:T(8,128)(2,1)S(1)} %collective-permute-done.10.other_ref), custom_call_target="tpu_custom_call" | custom-call | tf_op jit(solution)/shard_map/late_grad/pallas_call | solution.py:368
  30.3 0.7 %collective-permute-done.11.other_ref = bf16[256,128]{1,0:T(8,128)(2,1)S(1)} collective-permute-done((bf16[256,128]{1,0:T(8,128)(2,1)S(1)}, bf16[256,128]{1,0:T(8,128)(2,1)S(1)}, u32[]{:S(2)}, u32[]{:S(2)}) %collective-permute-start.11) | collective-permute-done | bytes 65568 | tf_op jit(solution)/shard_map/ppermute | solution.py:359
  31.0 2.4 %early_grad.1 = (bf16[3456,128]{1,0:T(8,128)(2,1)S(1)}, f32[4,160,128]{2,1,0:T(8,128)S(1)}) custom-call(f32[256,128]{1,0:T(8,128)S(1)} %get-tuple-element.21.mine_ref, bf16[256,128]{1,0:T(8,128)(2,1)S(1)} %collective-permute-done.11.other_ref, f32[2048,128]{1,0:T(8,128)S(1)} %get-tuple-element.23.slope_ref, bf16[2048,1152]{1,0:T(8,128)(2,1)S(1)} %get-tuple-element.24.col_ref), custom_call_target="tpu_custom_call" | custom-call | tf_op jit(solution)/shard_map/early_grad/pallas_call | solution.py:368
  33.4 0.1 collective-permute-start.12
  33.5 1.4 %grad_volume.1 = bf16[256,128]{1,0:T(8,128)(2,1)} custom-call(f32[4,160,128]{2,1,0:T(8,128)S(1)} %get-tuple-element.27.win_ref, bf16[3,3,3,128,128]{4,3,2,1,0:T(8,128)(2,1)S(1)} %get-tuple-element.28.we_ref), custom_call_target="tpu_custom_call" | custom-call | tf_op jit(solution)/shard_map/grad_volume/pallas_call | solution.py:368
  34.9 1.0 %collective-permute-done.12 = bf16[3456,128]{1,0:T(8,128)(2,1)S(1)} collective-permute-done((bf16[3456,128]{1,0:T(8,128)(2,1)S(1)}, bf16[3456,128]{1,0:T(8,128)(2,1)S(1)}, u32[]{:S(2)}, u32[]{:S(2)}) %collective-permute-start.12) | collective-permute-done | bytes 884768 | tf_op jit(solution)/shard_map/ppermute | solution.py:359
  35.9 1.2 %multiply_convert_fusion = bf16[3456,128]{1,0:T(8,128)(2,1)} fusion(bf16[3456,128]{1,0:T(8,128)(2,1)S(1)} %collective-permute-done.12, bf16[3456,128]{1,0:T(8,128)(2,1)S(1)} %get-tuple-element.25), kind=kLoop, calls=%fused_computation | loop fusion | flops 2211840 | bytes 2654208 | tf_op jit(solution)/shard_map/convert_element_type | solution.py:465
Async XLA Ops:
  0.6 7.9 %collective-permute-start.2 = (bf16[256,128]{1,0:T(8,128)(2,1)}, bf16[256,128]{1,0:T(8,128)(2,1)S(1)}, u32[]{:S(2)}, u32[]{:S(2)}) collective-permute-start(bf16[256,128]{1,0:T(8,128)(2,1)} %bitcast.6), channel_id=1, source_target_pairs={{0,12},{4,0},{8,4},{12,8},{1,13},{5,1},{9,5},{13,9},{2,14},{6,2},{... | collective-permute-start | bytes 196616 | tf_op jit(solution)/shard_map/ppermute | solution.py:359
  5.7 6.7 %collective-permute-start.1 = (bf16[256,128]{1,0:T(8,128)(2,1)}, bf16[256,128]{1,0:T(8,128)(2,1)S(1)}, u32[]{:S(2)}, u32[]{:S(2)}) collective-permute-start(bf16[256,128]{1,0:T(8,128)(2,1)} %bitcast.7), channel_id=1, source_target_pairs={{0,8},{4,12},{8,0},{12,4},{1,9},{5,13},{9,1},{13,5},{2,10},{6,14},... | collective-permute-start | bytes 196616 | tf_op jit(solution)/shard_map/ppermute | solution.py:359
  5.7 8.2 %collective-permute-start = (bf16[256,128]{1,0:T(8,128)(2,1)}, bf16[256,128]{1,0:T(8,128)(2,1)S(1)}, u32[]{:S(2)}, u32[]{:S(2)}) collective-permute-start(bf16[256,128]{1,0:T(8,128)(2,1)} %bitcast.8), channel_id=1, source_target_pairs={{0,4},{4,8},{8,12},{12,0},{1,5},{5,9},{9,13},{13,1},{2,6},{6,10},{... | collective-permute-start | bytes 196616 | tf_op jit(solution)/shard_map/ppermute | solution.py:359
  6.7 10.4 %collective-permute-start.3 = (bf16[256,128]{1,0:T(8,128)(2,1)}, bf16[256,128]{1,0:T(8,128)(2,1)S(1)}, u32[]{:S(2)}, u32[]{:S(2)}) collective-permute-start(bf16[256,128]{1,0:T(8,128)(2,1)} %bitcast.9), channel_id=1, source_target_pairs={{0,2},{2,0},{1,3},{3,1},{4,6},{6,4},{5,7},{7,5},{8,10},{10,8},{9,1... | collective-permute-start | bytes 196616 | tf_op jit(solution)/shard_map/ppermute | solution.py:359
  8.5 8.6 %collective-permute-start.6 = (bf16[256,128]{1,0:T(8,128)(2,1)S(1)}, bf16[256,128]{1,0:T(8,128)(2,1)S(1)}, u32[]{:S(2)}, u32[]{:S(2)}) collective-permute-start(bf16[256,128]{1,0:T(8,128)(2,1)S(1)} %collective-permute-done.2.refs_3_), channel_id=1, source_target_pairs={{0,2},{2,0},{1,3},{3,1},{4,6},{6,4},{5,7},{7,5},{8,10},{10,8},{9,1... | collective-permute-start | bytes 196616 | tf_op jit(solution)/shard_map/ppermute | solution.py:359
  12.4 6.1 %collective-permute-start.5 = (bf16[256,128]{1,0:T(8,128)(2,1)S(1)}, bf16[256,128]{1,0:T(8,128)(2,1)S(1)}, u32[]{:S(2)}, u32[]{:S(2)}) collective-permute-start(bf16[256,128]{1,0:T(8,128)(2,1)S(1)} %collective-permute-done.1.refs_2_), channel_id=1, source_target_pairs={{0,2},{2,0},{1,3},{3,1},{4,6},{6,4},{5,7},{7,5},{8,10},{10,8},{9,1... | collective-permute-start | bytes 196616 | tf_op jit(solution)/shard_map/ppermute | solution.py:359
  13.9 4.6 %collective-permute-start.4 = (bf16[256,128]{1,0:T(8,128)(2,1)S(1)}, bf16[256,128]{1,0:T(8,128)(2,1)S(1)}, u32[]{:S(2)}, u32[]{:S(2)}) collective-permute-start(bf16[256,128]{1,0:T(8,128)(2,1)S(1)} %collective-permute-done.refs_1_), channel_id=1, source_target_pairs={{0,2},{2,0},{1,3},{3,1},{4,6},{6,4},{5,7},{7,5},{8,10},{10,8},{9,1... | collective-permute-start | bytes 196616 | tf_op jit(solution)/shard_map/ppermute | solution.py:359
  15.2 8.6 %collective-permute-start.9 = (bf16[64,256]{1,0:T(8,128)(2,1)S(1)}, bf16[64,256]{1,0:T(8,128)(2,1)S(1)}, u32[]{:S(2)}, u32[]{:S(2)}) collective-permute-start(bf16[64,256]{1,0:T(8,128)(2,1)S(1)} %reshape.22.refs_1_), channel_id=1, source_target_pairs={{0,12},{4,0},{8,4},{12,8},{1,13},{5,1},{9,5},{13,9},{2,14},{6,2},{... | collective-permute-start | bytes 98312 | tf_op jit(solution)/shard_map/ppermute | solution.py:359
  17.2 6.7 %collective-permute-start.8 = (bf16[64,256]{1,0:T(8,128)(2,1)S(1)}, bf16[64,256]{1,0:T(8,128)(2,1)S(1)}, u32[]{:S(2)}, u32[]{:S(2)}) collective-permute-start(bf16[64,256]{1,0:T(8,128)(2,1)S(1)} %reshape.22.refs_1_), channel_id=1, source_target_pairs={{0,8},{4,12},{8,0},{12,4},{1,9},{5,13},{9,1},{13,5},{2,10},{6,14},... | collective-permute-start | bytes 98312 | tf_op jit(solution)/shard_map/ppermute | solution.py:359
  17.2 6.7 %collective-permute-start.7 = (bf16[64,256]{1,0:T(8,128)(2,1)S(1)}, bf16[64,256]{1,0:T(8,128)(2,1)S(1)}, u32[]{:S(2)}, u32[]{:S(2)}) collective-permute-start(bf16[64,256]{1,0:T(8,128)(2,1)S(1)} %reshape.22.refs_1_), channel_id=1, source_target_pairs={{0,4},{4,8},{8,12},{12,0},{1,5},{5,9},{9,13},{13,1},{2,6},{6,10},{... | collective-permute-start | bytes 98312 | tf_op jit(solution)/shard_map/ppermute | solution.py:359
  26.4 1.5 %collective-permute-start.10 = (bf16[256,384]{1,0:T(8,128)(2,1)S(1)}, bf16[256,384]{1,0:T(8,128)(2,1)S(1)}, u32[]{:S(2)}, u32[]{:S(2)}) collective-permute-start(bf16[256,384]{1,0:T(8,128)(2,1)S(1)} %get-tuple-element.20.mine_ref), channel_id=1, source_target_pairs={{0,1},{1,0},{2,3},{3,2},{4,5},{5,4},{6,7},{7,6},{8,9},{9,8},{10,11... | collective-permute-start | bytes 589832 | tf_op jit(solution)/shard_map/ppermute | solution.py:359
  26.5 4.5 %collective-permute-start.11 = (bf16[256,128]{1,0:T(8,128)(2,1)S(1)}, bf16[256,128]{1,0:T(8,128)(2,1)S(1)}, u32[]{:S(2)}, u32[]{:S(2)}) collective-permute-start(bf16[256,128]{1,0:T(8,128)(2,1)S(1)} %get-tuple-element.22), channel_id=1, source_target_pairs={{0,2},{2,0},{1,3},{3,1},{4,6},{6,4},{5,7},{7,5},{8,10},{10,8},{9,1... | collective-permute-start | bytes 196616 | tf_op jit(solution)/shard_map/ppermute | solution.py:359
  33.4 2.5 %collective-permute-start.12 = (bf16[3456,128]{1,0:T(8,128)(2,1)S(1)}, bf16[3456,128]{1,0:T(8,128)(2,1)S(1)}, u32[]{:S(2)}, u32[]{:S(2)}) collective-permute-start(bf16[3456,128]{1,0:T(8,128)(2,1)S(1)} %get-tuple-element.25), channel_id=1, source_target_pairs={{0,1},{1,0},{2,3},{3,2},{4,5},{5,4},{6,7},{7,6},{8,9},{9,8},{10,11... | collective-permute-start | bytes 2654216 | tf_op jit(solution)/shard_map/ppermute | solution.py:359

commit v4 on v3

--- a/solution.py
+++ b/solution.py
@@ -10,7 +10,7 @@
 
 BF = jnp.bfloat16
 F32 = jnp.float32
-VMEM_BYTES = 24 * 2**20
+VMEM_BYTES = 14 * 2**20
 GATHER_BLOCKS = 8
 
 
@@ -162,79 +162,139 @@
 STEPS = [(b, c) for b in (-1, 0, 1) for c in (-1, 0, 1)]
 
 
-def early_kernel(*refs, nk, nj, dims):
+def fold(parts, rows):
+    zero = jnp.zeros((rows, parts[0].shape[1]), F32)
+    return (
+        parts[1]
+        + jnp.concatenate([zero, parts[0][:-rows]], axis=0)
+        + jnp.concatenate([parts[2][rows:], zero], axis=0)
+    )
+
+
+def early_kernel(*refs, nk, dims):
     gx, gy, gz, lx, ly, lz, bx, by = dims
-    blocks, refs = refs[: nk * nj], refs[nk * nj :]
-    we_hbm, wl_hbm, we_ref, wl_ref, col_ref, slope_ref, pooled_ref = refs[:7]
-    vol_ref, own_ref, wcat_ref, p_ref, h_ref, sems = refs[7:]
+    blocks, refs = refs[:nk], refs[nk:]
+    we_hbm, wl_hbm, we_ref, wl_ref, wcat_ref, half_ref, slope_ref, send_ref, edge_ref = refs[:9]
+    vol_ref, own_ref, col_ref, p_ref, pre_ref, h_ref, row_ref, sems = refs[9:]
     k, j = lax.axis_index("space"), lax.axis_index("chan")
-    plane, lplane = gy * gz, ly * lz
-    brows = by * gz
+    brows, hl, line = by * gz, by // 2 * lz, gx * gz
     own_copy = pltpu.make_async_copy(blocks[0], own_ref, sems.at[0])
     we_copy = pltpu.make_async_copy(we_hbm, we_ref, sems.at[1])
     wl_copy = pltpu.make_async_copy(wl_hbm, wl_ref, sems.at[2])
+    we_copy.start()
     own_copy.start()
-    we_copy.start()
-    wl_copy.start()
 
     vol_ref[:, pl.ds(0, 16), :] = jnp.zeros((gx, 16, 128), F32)
-    vol_ref[:, pl.ds(16 + plane, 16), :] = jnp.zeros((gx, 16, 128), F32)
-    for n in [*range(1, nk * nj), 0]:
-        dj, dk = divmod(n, nk)
+    vol_ref[:, pl.ds(16 + brows, 16), :] = jnp.zeros((gx, 16, 128), F32)
+    for n, dk in [*enumerate(far_first(nk), 1), (0, 0)]:
         if n == 0:
             own_copy.wait()
         src = blocks[n] if n else own_ref
-        kk = lax.rem(k + nk - dk, nk)
-        jj = lax.rem(j + nj - dj, nj)
-        row = pl.multiple_of(16 + jj * brows, 8)
+        kk = partner(k, dk, nk)
         for q in range(bx):
-            vol_ref[kk * bx + q, pl.ds(row, brows), :] = src[pl.ds(q * brows, brows), :].astype(F32)
-
-    cell = depth_of(plane, gz)
+            got = src[pl.ds(q * brows, brows), :]
+            vol_ref[kk * bx + q, pl.ds(16, brows), :] = got.astype(F32)
+            half_ref[pl.ds(pl.multiple_of((kk * bx + q) * brows, brows), brows), :] = got
+
+    cell = depth_of(brows, gz)
     for x in range(gx):
         for n, step in enumerate(STEPS):
-            col_ref[pl.ds(x * plane, plane), pl.ds(n * 128, 128)] = shifted(
-                vol_ref, (x,), 16, plane, cell, gz, step
+            col_ref[pl.ds(x * brows, brows), pl.ds(n * 128, 128)] = shifted(
+                vol_ref, (x,), 16, brows, cell, gz, step
             ).astype(BF)
 
     we_copy.wait()
+    wl_copy.start()
     for n in range(9):
         b, c = divmod(n, 3)
         for a in range(3):
             wcat_ref[pl.ds(n * 128, 128), pl.ds(a * 128, 128)] = we_ref[a, b, c]
     p_ref[...] = jnp.dot(col_ref[...], wcat_ref[...], preferred_element_type=F32)
 
+    outer = pl.multiple_of((brows - gz) * (1 - j), gz)
+    inner = pl.multiple_of((brows - 2 * gz) * (1 - j) + gz * j, gz)
+    for x in range(gx):
+        row_ref[pl.ds(x * gz, gz), :] = vol_ref[x, pl.ds(16 + outer, gz), :]
+    row = row_ref[...]
+    rcell = depth_of(line, gz)
+    trio = [
+        jnp.where(rcell == 0, 0.0, pltpu.roll(row, 1, 0)),
+        row,
+        jnp.where(rcell == gz - 1, 0.0, pltpu.roll(row, line - 1, 0)),
+    ]
+    taps = wcat_ref[pl.ds(pl.multiple_of(j * (6 * 128), 128), 3 * 128), :]
+    given = jnp.dot(jnp.concatenate(trio, axis=1).astype(BF), taps, preferred_element_type=F32)
+    given = fold([given[:, a * 128 : (a + 1) * 128] for a in range(3)], gz)
+
     for lq in range(lx):
         pair = None
         for x in (2 * lq, 2 * lq + 1):
-            pre = p_ref[pl.ds(x * plane, plane), pl.ds(128, 128)]
+            pre = p_ref[pl.ds(x * brows, brows), pl.ds(128, 128)]
             if x > 0:
-                pre = pre + p_ref[pl.ds((x - 1) * plane, plane), pl.ds(0, 128)]
+                pre = pre + p_ref[pl.ds((x - 1) * brows, brows), pl.ds(0, 128)]
             if x < gx - 1:
-                pre = pre + p_ref[pl.ds((x + 1) * plane, plane), pl.ds(256, 128)]
+                pre = pre + p_ref[pl.ds((x + 1) * brows, brows), pl.ds(256, 128)]
+            pre_ref[x] = pre
             h, slope = gelu_and_slope(pre)
-            slope_ref[pl.ds(x * plane, plane), :] = slope
+            slope_ref[pl.ds(x * brows, brows), :] = slope
             pair = h if pair is None else pair + h
-        wide = pair.reshape(ly, 2, gz, 128)
-        h_ref[...] = (wide[:, 0] + wide[:, 1]).reshape(ly * gz, 128)
-        pooled = (h_ref[pl.ds(0, lplane, stride=2), :] + h_ref[pl.ds(1, lplane, stride=2), :]) * 0.125
-        pooled_ref[pl.ds(lq * lplane, lplane), :] = pooled.astype(BF)
+        wide = pair.reshape(by // 2, 2, gz, 128)
+        h_ref[...] = (wide[:, 0] + wide[:, 1]).reshape(by // 2 * gz, 128)
+        pooled = (h_ref[pl.ds(0, hl, stride=2), :] + h_ref[pl.ds(1, hl, stride=2), :]) * 0.125
+        send_ref[pl.ds(lq * hl, hl), :] = pooled.astype(BF)
+    for x in range(gx):
+        edge_ref[pl.ds(x * gz, gz), :] = pre_ref[x, pl.ds(inner, gz), :]
+        edge_ref[pl.ds(line + x * gz, gz), :] = pre_ref[x, pl.ds(outer, gz), :]
+    edge_ref[pl.ds(2 * line, line), :] = given
+    send_ref[pl.ds(lx * hl, 3 * line), :] = edge_ref[...].astype(BF)
     wl_copy.wait()
 
 
+def border_pool(inner, outer, tmp_ref, tile_ref, dims):
+    lx, lz, gz = dims
+    h, slope = gelu_and_slope(outer)
+    h = (h + gelu_and_slope(inner)[0]).reshape(lx, 2, gz, 128)
+    tmp_ref[...] = (h[:, 0] + h[:, 1]).reshape(lx * gz, 128)
+    got = (tmp_ref[pl.ds(0, lx * lz, stride=2), :] + tmp_ref[pl.ds(1, lx * lz, stride=2), :]) * 0.125
+    got = got.astype(BF).astype(F32)
+    for x in range(lx):
+        for copy in range(2):
+            tile_ref[pl.ds((2 * x + copy) * lz, lz), :] = got[x * lz : (x + 1) * lz]
+    return slope
+
+
 def late_kernel(*refs, nk, dims):
-    lx, ly, lz, cx = dims
-    pooled_ref, cots, refs = refs[0], refs[1 : nk + 1], refs[nk + 1 :]
-    wl_ref, pd_ref, back_ref, mine_ref, pool_ref, lcol_ref, dl_ref, cot_ref = refs
-    lplane = ly * lz
+    gx, gz, lx, ly, lz, cx = dims
+    sent_ref, got_ref, edge_ref, cots, refs = *refs[:3], refs[3 : nk + 3], refs[nk + 3 :]
+    wl_ref, pd_ref, back_ref, mine_ref, patch_ref = refs[:5]
+    pool_ref, lcol_ref, dl_ref, cot_ref, tmp_ref, tile_ref = refs[5:]
+    lplane, hl, line = ly * lz, ly // 2 * lz, gx * gz
     cl = wl_ref.shape[-1]
     crow = cx * lplane
-    k = lax.axis_index("space")
+    k, j = lax.axis_index("space"), lax.axis_index("chan")
+    edges = got_ref[pl.ds(lx * hl, 3 * line), :].astype(F32)
+    lrow = lax.broadcasted_iota(jnp.int32, (hl, 128), 0)
     for x in range(lx):
         pool_ref[x, pl.ds(0, 8), :] = jnp.zeros((8, 128), F32)
         pool_ref[x, pl.ds(8 + lplane, 8), :] = jnp.zeros((8, 128), F32)
-        pool_ref[x, pl.ds(8, lplane), :] = pooled_ref[pl.ds(x * lplane, lplane), :].astype(F32)
-    pd_ref[:, pl.ds(0, 128)] = pooled_ref[...]
+    sides = (
+        (j, sent_ref, edge_ref[pl.ds(0, line), :], edge_ref[pl.ds(line, line), :] + edges[2 * line :]),
+        (1 - j, got_ref, edges[:line], edges[line : 2 * line] + edge_ref[pl.ds(2 * line, line), :]),
+    )
+    for n, (side, ref, inner, outer) in enumerate(sides):
+        slope = border_pool(inner, outer, tmp_ref, tile_ref, (lx, lz, gz))
+        if n == 0:
+            patch_ref[...] = slope
+        first = (hl - lz) * (1 - side)
+        border = (lrow >= first) & (lrow < first + lz)
+        for x in range(lx):
+            tiles = jnp.concatenate([tile_ref[pl.ds(x * 2 * lz, 2 * lz), :]] * (hl // (2 * lz)), axis=0)
+            start = pl.multiple_of(8 + side * hl, 8)
+            pool_ref[x, pl.ds(start, hl), :] = jnp.where(
+                border, tiles, ref[pl.ds(x * hl, hl), :].astype(F32)
+            )
+    for x in range(lx):
+        pd_ref[pl.ds(x * lplane, lplane), pl.ds(0, 128)] = pool_ref[x, pl.ds(8, lplane), :].astype(BF)
 
     lcell = depth_of(lplane, lz)
     for x in range(lx):
@@ -249,15 +309,12 @@
     for x in range(lx):
         dl_ref[x, pl.ds(0, 8), :] = jnp.zeros((8, cl), F32)
         dl_ref[x, pl.ds(8 + lplane, 8), :] = jnp.zeros((8, cl), F32)
-    zero = jnp.zeros((lplane, cl), F32)
-    pre = parts[1]
-    pre = pre + jnp.concatenate([zero, parts[0][:-lplane]], axis=0)
-    pre = pre + jnp.concatenate([parts[2][lplane:], zero], axis=0)
+    pre = fold(parts, lplane)
     slope = gelu_and_slope(pre)[1]
-    for dk in range(nk):
-        kk = lax.rem(k + nk - dk, nk)
+    for n, dk in enumerate([0, *far_first(nk)]):
+        kk = partner(k, dk, nk)
         start = pl.multiple_of(kk * crow, 8)
-        cot_ref[pl.ds(start, crow), :] = cots[dk][...].astype(F32)
+        cot_ref[pl.ds(start, crow), :] = cots[n][...].astype(F32)
     delta = (cot_ref[...] * slope).astype(BF)
     pd_ref[:, pl.ds(128, cl)] = delta
     wide = delta.astype(F32)
@@ -271,10 +328,7 @@
         w = wl_ref[:, b + 1, c + 1].reshape(3 * 128, cl)
         term = lax.dot_general(part, w, NT, preferred_element_type=F32)
         total = term if total is None else total + term
-    zero = jnp.zeros((lplane, 128), F32)
-    back = total[:, 128:256]
-    back = back + jnp.concatenate([total[lplane:, 0:128], zero], axis=0)
-    back = back + jnp.concatenate([zero, total[:-lplane, 256:384]], axis=0)
+    back = fold([total[:, (2 - a) * 128 : (3 - a) * 128] for a in range(3)], lplane)
     back_ref[...] = back.astype(BF)
     mine_ref[...] = back
 
@@ -301,30 +355,85 @@
         out_ref[pl.ds(a * 9 * 128, 9 * 128), :] = (got * scale).astype(BF)
 
 
+def other_kernel(
+    half_ref, got_ref, wcat_ref, col_ref, slope_ref, vol_ref, p_ref, *, dims
+):
+    gx, gy, gz, lx, ly, lz, bx, by = dims
+    brows = by * gz
+    j = lax.axis_index("chan")
+    vol_ref[:, :, pl.ds(0, 16), :] = jnp.zeros((2, gx, 16, 128), F32)
+    vol_ref[:, :, pl.ds(16 + brows, 16), :] = jnp.zeros((2, gx, 16, 128), F32)
+    for h, src in enumerate((half_ref, got_ref)):
+        for x in range(gx):
+            vol_ref[h, x, pl.ds(16, brows), :] = src[pl.ds(x * brows, brows), :].astype(F32)
+    for h, side in enumerate((j, 1 - j)):
+        into = pl.multiple_of((16 + brows) * (1 - side) + (16 - gz) * side, 8)
+        start = pl.multiple_of(16 + (brows - gz) * side, 8)
+        for x in range(gx):
+            vol_ref[h, x, pl.ds(into, gz), :] = vol_ref[1 - h, x, pl.ds(start, gz), :]
+    cell = depth_of(brows, gz)
+    for h in (1, 0):
+        for x in range(gx):
+            for n, step in enumerate(STEPS):
+                col_ref[pl.ds((h * gx + x) * brows, brows), pl.ds(n * 128, 128)] = shifted(
+                    vol_ref, (h, x), 16, brows, cell, gz, step
+                ).astype(BF)
+    p_ref[...] = jnp.dot(
+        col_ref[pl.ds(gx * brows, gx * brows), :], wcat_ref[...], preferred_element_type=F32
+    )
+    for x in range(gx):
+        pre = p_ref[pl.ds(x * brows, brows), pl.ds(128, 128)]
+        if x > 0:
+            pre = pre + p_ref[pl.ds((x - 1) * brows, brows), pl.ds(0, 128)]
+        if x < gx - 1:
+            pre = pre + p_ref[pl.ds((x + 1) * brows, brows), pl.ds(256, 128)]
+        slope_ref[pl.ds(x * brows, brows), :] = gelu_and_slope(pre)[1]
+
+
 def early_grad_kernel(
-    mine_ref, other_ref, slope_ref, col_ref, part_ref, win_ref, wide_ref, d_ref, dt_ref, *, dims
+    mine_ref, other_ref, slope_ref, far_ref, patch_ref, col_ref,
+    part_ref, win_ref, wide_ref, d_ref, dt_ref, *, dims
 ):
     gx, gy, gz, lx, ly, lz, bx, by = dims
     plane, lplane = gy * gz, ly * lz
     k, j = lax.axis_index("space"), lax.axis_index("chan")
     brows = by * gz
+    span = (gx + 2) * brows
     for q in (0, gx + 1):
         d_ref[q] = jnp.zeros(d_ref.shape[1:], F32)
     d_ref[:, pl.ds(0, 16), :] = jnp.zeros((gx + 2, 16, 128), F32)
     d_ref[:, pl.ds(16 + plane, 16), :] = jnp.zeros((gx + 2, 16, 128), F32)
-    dt_ref[:, pl.ds(0, plane)] = jnp.zeros((128, plane), BF)
-    dt_ref[:, pl.ds((gx + 1) * plane, plane)] = jnp.zeros((128, plane), BF)
+    for h in (0, 1):
+        dt_ref[:, pl.ds(h * span, brows)] = jnp.zeros((128, brows), BF)
+        dt_ref[:, pl.ds((h + 1) * span - brows, brows)] = jnp.zeros((128, brows), BF)
     back = (mine_ref[...] + other_ref[...].astype(F32)) * 0.125
     wide_ref[pl.ds(0, lx * lplane, stride=2), :] = back
     wide_ref[pl.ds(1, lx * lplane, stride=2), :] = back
+    first = (brows - gz) * (1 - j)
+    row = lax.broadcasted_iota(jnp.int32, (brows, 128), 0)
+    border = (row >= first) & (row < first + gz)
     for lq in range(lx):
-        rows = wide_ref[pl.ds(lq * ly * gz, ly * gz), :].reshape(ly, 1, gz, 128)
-        rows = jnp.broadcast_to(rows, (ly, 2, gz, 128)).reshape(plane, 128)
-        for x in (2 * lq, 2 * lq + 1):
-            delta = (rows * slope_ref[pl.ds(x * plane, plane), :]).astype(BF).astype(F32)
-            d_ref[x + 1, pl.ds(16, plane), :] = delta
-            dt_ref[:, pl.ds((x + 1) * plane, plane)] = delta.T.astype(BF)
-    left = jnp.concatenate([dt_ref[:, pl.ds((2 - a) * plane, gx * plane)] for a in range(3)], axis=0)
+        for h, side in enumerate((j, 1 - j)):
+            start = pl.multiple_of(lq * ly * gz + side * (by // 2 * gz), 8)
+            rows = wide_ref[pl.ds(start, by // 2 * gz), :].reshape(by // 2, 1, gz, 128)
+            rows = jnp.broadcast_to(rows, (by // 2, 2, gz, 128)).reshape(brows, 128)
+            for x in (2 * lq, 2 * lq + 1):
+                slope = (far_ref if h else slope_ref)[pl.ds(x * brows, brows), :]
+                if h == 0:
+                    tiles = jnp.concatenate([patch_ref[pl.ds(x * gz, gz), :]] * by, axis=0)
+                    slope = jnp.where(border, tiles, slope)
+                delta = (rows * slope).astype(BF).astype(F32)
+                d_ref[x + 1, pl.ds(pl.multiple_of(16 + side * brows, 8), brows), :] = delta
+                dt_ref[:, pl.ds(h * span + (x + 1) * brows, brows)] = delta.T.astype(BF)
+    left = jnp.concatenate(
+        [
+            jnp.concatenate(
+                [dt_ref[:, pl.ds(h * span + (2 - a) * brows, gx * brows)] for h in (0, 1)], axis=1
+            )
+            for a in range(3)
+        ],
+        axis=0,
+    )
     got = jnp.dot(left, col_ref[...], preferred_element_type=F32)
     for a in range(3):
         for n in range(9):
@@ -354,9 +463,20 @@
     gv_ref[...] = total.astype(BF)
 
 
+def far_first(count):
+    return range(count - 1, 0, -1)
+
+
+def partner(index, by, count):
+    if count & (count - 1) == 0:
+        return index ^ by
+    return lax.rem(index + count - by, count)
+
+
 def turned(value, axis, by):
     count = lax.axis_size(axis)
-    return lax.ppermute(value, axis, [(i, (i + by) % count) for i in range(count)])
+    pairs = count & (count - 1) == 0
+    return lax.ppermute(value, axis, [(i, i ^ by if pairs else (i + by) % count) for i in range(count)])
 
 
 def call(kernel, outs, scratch, args, name, far=(), raw=()):
@@ -389,46 +509,57 @@
     sds = jax.ShapeDtypeStruct
 
     mine = volume.reshape(bx * brows, 128)
-    line = [mine] + [turned(mine, "space", dk) for dk in range(1, nk)]
-    blocks = list(line)
-    for dj in range(1, nj):
-        blocks += [turned(block, "chan", dj) for block in line]
+    line = [mine] + [turned(mine, "space", dk) for dk in far_first(nk)]
     cot = cotangent.reshape(cx * lplane, cl)
-    held = lax.optimization_barrier((cot, *line[1:]))[0]
-    cots = [cot] + [turned(held, "space", dk) for dk in range(1, nk)]
-
-    count = nk * nj
-    we, wl, col, slope, pooled = call(
-        functools.partial(early_kernel, nk=nk, nj=nj, dims=(gx, gy, gz, lx, ly, lz, bx, by)),
+    cots = [cot] + [turned(cot, "space", dk) for dk in far_first(nk)]
+
+    dims = (gx, gy, gz, lx, ly, lz, bx, by)
+    hrows, edge = gx * brows, 3 * gx * gz
+    we, wl, wcat, half, slope, send, edges = call(
+        functools.partial(early_kernel, nk=nk, dims=dims),
         [
             sds(early_weight.shape, BF),
             sds(late_weight.shape, BF),
-            sds((rows, 9 * 128), BF),
-            sds((rows, 128), F32),
-            sds((lrows, 128), BF),
+            sds((9 * 128, 3 * 128), BF),
+            sds((hrows, 128), BF),
+            sds((hrows, 128), F32),
+            sds((lrows // 2 + edge, 128), BF),
+            sds((edge, 128), F32),
         ],
         [
-            pltpu.VMEM((gx, plane + 32, 128), F32),
+            pltpu.VMEM((gx, brows + 32, 128), F32),
             pltpu.VMEM((bx * brows, 128), BF),
-            pltpu.VMEM((9 * 128, 3 * 128), BF),
-            pltpu.VMEM((rows, 3 * 128), F32),
-            pltpu.VMEM((ly * gz, 128), F32),
+            pltpu.VMEM((hrows, 9 * 128), BF),
+            pltpu.VMEM((hrows, 3 * 128), F32),
+            pltpu.VMEM((gx, brows, 128), F32),
+            pltpu.VMEM((by // 2 * gz, 128), F32),
+            pltpu.VMEM((gx * gz, 128), F32),
             pltpu.SemaphoreType.DMA((3,)),
         ],
-        blocks + [early_weight, late_weight],
+        line + [early_weight, late_weight],
         "early",
-        raw=(0, count, count + 1),
-    )
-    pooled_delta, back, back_mine = call(
-        functools.partial(late_kernel, nk=nk, dims=(lx, ly, lz, cx)),
-        [sds((lrows, 128 + cl), BF), sds((lrows, 128), BF), sds((lrows, 128), F32)],
+        raw=(0, nk, nk + 1),
+    )
+    ready, *cots[1:] = lax.optimization_barrier((send, *cots[1:]))
+    send_other = turned(ready, "chan", 1)
+    half_other = turned(half, "chan", 1)
+    pooled_delta, back, back_mine, patch = call(
+        functools.partial(late_kernel, nk=nk, dims=(gx, gz, lx, ly, lz, cx)),
+        [
+            sds((lrows, 128 + cl), BF),
+            sds((lrows, 128), BF),
+            sds((lrows, 128), F32),
+            sds((gx * gz, 128), F32),
+        ],
         [
             pltpu.VMEM((lx, lplane + 16, 128), F32),
             pltpu.VMEM((lrows, 9 * 128), BF),
             pltpu.VMEM((lx, lplane + 16, cl), F32),
             pltpu.VMEM((lrows, cl), F32),
+            pltpu.VMEM((lx * gz, 128), F32),
+            pltpu.VMEM((lx * 2 * lz, 128), F32),
         ],
-        [pooled] + cots + [wl],
+        [send, send_other, edges] + cots + [wl],
         "late",
     )
     pd_other = turned(pooled_delta, "rep", 1)
@@ -441,16 +572,24 @@
         "late_grad",
         far=(0,),
     )
+    half_other, wcat, _ = lax.optimization_barrier((half_other, wcat, back))
+    col, far_slope = call(
+        functools.partial(other_kernel, dims=dims),
+        [sds((rows, 9 * 128), BF), sds((hrows, 128), F32)],
+        [pltpu.VMEM((2, gx, brows + 32, 128), F32), pltpu.VMEM((hrows, 3 * 128), F32)],
+        [half, half_other, wcat],
+        "other",
+    )
     back_mine, late = lax.optimization_barrier((back_mine, late))
     part, win = call(
-        functools.partial(early_grad_kernel, dims=(gx, gy, gz, lx, ly, lz, bx, by)),
+        functools.partial(early_grad_kernel, dims=dims),
         [sds((27 * 128, 128), BF), sds((bx + 2, brows + 32, 128), F32)],
         [
             pltpu.VMEM((lx * ly * gz, 128), F32),
             pltpu.VMEM((gx + 2, plane + 32, 128), F32),
             pltpu.VMEM((128, (gx + 2) * plane), BF),
         ],
-        [back_mine, back_other, slope, col],
+        [back_mine, back_other, slope, far_slope, patch, col],
         "early_grad",
     )
     part_other = turned(part, "rep", 1)

time: 37.3 us -> 36.5 us (0.979)
  starting transfers between devices: 15.4 us -> 14 us
    ppermute x13 -> x11, starting transfers between devices: 15.4 us -> 14 us  [turned(): lax.ppermute(value, axis, [(i, i ^ by if pairs else (i + by) % count) for...]
    pallas_call x5 -> x6, Pallas kernels: 14.1 us -> 14.4 us  [call(): pl.pallas_call(kernel, out_shape=outs, in_specs=[pl.BlockSpec(memory_spac...]
    ppermute x13 -> x11, waiting for transfers between devices: 4.95 us -> 5.25 us  [turned(): lax.ppermute(value, axis, [(i, i ^ by if pairs else (i + by) % count) for...]
  transfers between devices with their start and end apart: 13 -> 11, of which waited for: 5 -> 4; matrix products, arithmetic and copies ran while one was open for 2% -> 2% of each run, Pallas kernels for 25% -> 33%
where the time goes in v4:
time: 36.5 us; the launch traced here: 36.3 us
  Pallas kernels  14.4 us (39%)
  starting transfers between devices  14 us (38%)
  waiting for transfers between devices  5.25 us (14%)
  other arithmetic  1.2 us (3%)
  local copies, waits for them, and re-layouts  0.77 us (2%)
  between operations  0.7 us (2%)
    pallas_call x6, Pallas kernels, call(): pl.pallas_call(kernel, out_shape=outs, in_specs=[pl.BlockSpec(memory_spac...  14.4 us
    ppermute x11, starting transfers between devices, turned(): lax.ppermute(value, axis, [(i, i ^ by if pairs else (i + by) % count) for...  14 us
    ppermute x11, waiting for transfers between devices, turned(): lax.ppermute(value, axis, [(i, i ^ by if pairs else (i + by) % count) for...  5.25 us
    convert_element_type x1, other arithmetic, whole_sample(): early = ((part.astype(F32) + part_other.astype(F32)) * scale).astype(BF)  1.2 us
    reshape x1, local copies, waits for them, and re-layouts, whole_sample(): cot = cotangent.reshape(cx * lplane, cl)  0.77 us
  transfers between devices with their start and end apart: 11, of which 4 were waited for; matrix products, arithmetic and copies ran while one was open for 2% of the time, Pallas kernels for 33%

profile of v4, /device:TPU:0, one launch (start us, length us, event | category | flops | bytes accessed | tf_op | source)
XLA Modules:
  0.0 36.3 jit_solution(5741455515350681133)
XLA Ops:
  0.6 5.1 %collective-permute-start = (bf16[256,128]{1,0:T(8,128)(2,1)}, bf16[256,128]{1,0:T(8,128)(2,1)S(1)}, u32[]{:S(2)}, u32[]{:S(2)}) collective-permute-start(bf16[256,128]{1,0:T(8,128)(2,1)} %bitcast.6), channel_id=1, source_target_pairs={{0,12},{4,8},{8,4},{12,0},{1,13},{5,9},{9,5},{13,1},{2,14},{6,10},... | collective-permute-start | bytes 196616 | tf_op jit(solution)/shard_map/ppermute | solution.py:479
  5.7 0.0 collective-permute-start.1
  5.7 0.6 %collective-permute-start.2 = (bf16[256,128]{1,0:T(8,128)(2,1)}, bf16[256,128]{1,0:T(8,128)(2,1)S(1)}, u32[]{:S(2)}, u32[]{:S(2)}) collective-permute-start(bf16[256,128]{1,0:T(8,128)(2,1)} %bitcast.8), channel_id=1, source_target_pairs={{0,4},{4,0},{8,12},{12,8},{1,5},{5,1},{9,13},{13,9},{2,6},{6,2},{1... | collective-permute-start | bytes 196616 | tf_op jit(solution)/shard_map/ppermute | solution.py:479
  6.4 0.8 %reshape.22.refs_3_ = bf16[64,256]{1,0:T(8,128)(2,1)S(1)} reshape(bf16[1,1,16,4,256]{4,3,2,1,0:T(4,128)(2,1)} %param.7) | data formatting | bytes 65536 | tf_op jit(solution)/shard_map/reshape | solution.py:513
  7.2 3.8 %collective-permute-start.3 = (bf16[64,256]{1,0:T(8,128)(2,1)S(1)}, bf16[64,256]{1,0:T(8,128)(2,1)S(1)}, u32[]{:S(2)}, u32[]{:S(2)}) collective-permute-start(bf16[64,256]{1,0:T(8,128)(2,1)S(1)} %reshape.22.refs_3_), channel_id=1, source_target_pairs={{0,12},{4,8},{8,4},{12,0},{1,13},{5,9},{9,5},{13,1},{2,14},{6,10},... | collective-permute-start | bytes 98312 | tf_op jit(solution)/shard_map/ppermute | solution.py:479
  11.0 0.0 collective-permute-start.4
  11.0 0.0 collective-permute-done.refs_1_
  11.0 0.6 %collective-permute-start.5 = (bf16[64,256]{1,0:T(8,128)(2,1)S(1)}, bf16[64,256]{1,0:T(8,128)(2,1)S(1)}, u32[]{:S(2)}, u32[]{:S(2)}) collective-permute-start(bf16[64,256]{1,0:T(8,128)(2,1)S(1)} %reshape.22.refs_3_), channel_id=1, source_target_pairs={{0,4},{4,0},{8,12},{12,8},{1,5},{5,1},{9,13},{13,9},{2,6},{6,2},{1... | collective-permute-start | bytes 98312 | tf_op jit(solution)/shard_map/ppermute | solution.py:479
  11.6 0.9 %collective-permute-done.1.refs_2_ = bf16[256,128]{1,0:T(8,128)(2,1)S(1)} collective-permute-done((bf16[256,128]{1,0:T(8,128)(2,1)}, bf16[256,128]{1,0:T(8,128)(2,1)S(1)}, u32[]{:S(2)}, u32[]{:S(2)}) %collective-permute-start.1) | collective-permute-done | bytes 65568 | tf_op jit(solution)/shard_map/ppermute | solution.py:479
  12.5 0.0 collective-permute-done.2.refs_3_
  12.5 3.4 %early.1 = (bf16[3,3,3,128,128]{4,3,2,1,0:T(8,128)(2,1)S(1)}, bf16[3,3,3,128,256]{4,3,2,1,0:T(8,128)(2,1)S(1)}, bf16[1152,384]{1,0:T(8,128)(2,1)S(1)}, bf16[1024...) custom-call(bf16[256,128]{1,0:T(8,128)(2,1)} %bitcast.9, ...), custom_call_target="tpu_custom_call" | custom-call | tf_op jit(solution)/shard_map/early/pallas_call | solution.py:488
  15.9 0.0 collective-permute-done.3.refs_4_
  15.9 0.0 collective-permute-done.4.refs_5_
  15.9 0.0 collective-permute-done.5.refs_6_
  15.9 1.4 %collective-permute-start.6 = (bf16[320,128]{1,0:T(8,128)(2,1)S(1)}, bf16[320,128]{1,0:T(8,128)(2,1)S(1)}, u32[]{:S(2)}, u32[]{:S(2)}) collective-permute-start(bf16[320,128]{1,0:T(8,128)(2,1)S(1)} %get-tuple-element.27.refs_0_), channel_id=1, source_target_pairs={{0,2},{2,0},{1,3},{3,1},{4,6},{6,4},{5,7},{7,5},{8,10},{10,8},{9,1... | collective-permute-start | bytes 245768 | tf_op jit(solution)/shard_map/ppermute | solution.py:479
  17.3 0.7 %collective-permute-start.9 = (bf16[1024,128]{1,0:T(8,128)(2,1)S(1)}, bf16[1024,128]{1,0:T(8,128)(2,1)S(1)}, u32[]{:S(2)}, u32[]{:S(2)}) collective-permute-start(bf16[1024,128]{1,0:T(8,128)(2,1)S(1)} %get-tuple-element.38.half_ref), channel_id=1, source_target_pairs={{0,2},{2,0},{1,3},{3,1},{4,6},{6,4},{5,7},{7,5},{8,10},{10,8},{9,1... | collective-permute-start | bytes 786440 | tf_op jit(solution)/shard_map/ppermute | solution.py:479
  18.0 3.2 %collective-permute-done.6.refs_1_ = bf16[320,128]{1,0:T(8,128)(2,1)S(1)} collective-permute-done((bf16[320,128]{1,0:T(8,128)(2,1)S(1)}, bf16[320,128]{1,0:T(8,128)(2,1)S(1)}, u32[]{:S(2)}, u32[]{:S(2)}) %collective-permute-start.6) | collective-permute-done | bytes 81952 | tf_op jit(solution)/shard_map/ppermute | solution.py:479
  21.2 2.6 %late.1 = (bf16[256,384]{1,0:T(8,128)(2,1)S(1)}, bf16[256,128]{1,0:T(8,128)(2,1)S(1)}, f32[256,128]{1,0:T(8,128)S(1)}, f32[64,128]{1,0:T(8,128)S(1)}) custom-call(bf16[320,128]{1,0:T(8,128)(2,1)S(1)} %get-tuple-element.27.refs_0_, bf16[320,128]{1,0:T(8,128)(2,1)S(1)} %collective-permute-done.6.refs_1_, f32[192,128]{1,0:T(8,128)S(1)} %get-tuple-element.28.refs_2_, ...), custom_call_target="tpu_custom_call" | custom-call | tf_op jit(solution)/shard_map/late/pallas_call | solution.py:488
  23.8 0.1 collective-permute-start.7
  23.9 1.5 %collective-permute-start.8 = (bf16[256,128]{1,0:T(8,128)(2,1)S(1)}, bf16[256,128]{1,0:T(8,128)(2,1)S(1)}, u32[]{:S(2)}, u32[]{:S(2)}) collective-permute-start(bf16[256,128]{1,0:T(8,128)(2,1)S(1)} %get-tuple-element.36), channel_id=1, source_target_pairs={{0,2},{2,0},{1,3},{3,1},{4,6},{6,4},{5,7},{7,5},{8,10},{10,8},{9,1... | collective-permute-start | bytes 196616 | tf_op jit(solution)/shard_map/ppermute | solution.py:479
  25.4 0.1 collective-permute-done.9.got_ref
  25.5 2.1 %other.1 = (bf16[2048,1152]{1,0:T(8,128)(2,1)S(1)}, f32[1024,128]{1,0:T(8,128)S(1)}) custom-call(bf16[1024,128]{1,0:T(8,128)(2,1)S(1)} %get-tuple-element.38.half_ref, bf16[1024,128]{1,0:T(8,128)(2,1)S(1)} %collective-permute-done.9.got_ref, bf16[1152,384]{1,0:T(8,128)(2,1)S(1)} %get-tuple-element.41.wcat_ref), custom_call_target="tpu_custom_call" | custom-call | tf_op jit(solution)/shard_map/other/pallas_call | solution.py:488
  27.7 0.0 collective-permute-done.7.other_ref
  27.7 2.4 %late_grad.1 = bf16[3456,256]{1,0:T(8,128)(2,1)} custom-call(bf16[256,384]{1,0:T(8,128)(2,1)S(1)} %get-tuple-element.34.mine_ref, bf16[256,384]{1,0:T(8,128)(2,1)S(1)} %collective-permute-done.7.other_ref), custom_call_target="tpu_custom_call" | custom-call | tf_op jit(solution)/shard_map/late_grad/pallas_call | solution.py:488
  30.1 0.0 collective-permute-done.8.other_ref
  30.1 2.5 %early_grad.1 = (bf16[3456,128]{1,0:T(8,128)(2,1)S(1)}, f32[4,160,128]{2,1,0:T(8,128)S(1)}) custom-call(f32[256,128]{1,0:T(8,128)S(1)} %get-tuple-element.35.mine_ref, bf16[256,128]{1,0:T(8,128)(2,1)S(1)} %collective-permute-done.8.other_ref, f32[1024,128]{1,0:T(8,128)S(1)} %get-tuple-element.37.slope_ref, f32[1024,128]{1,0:T(8,128)S(1)} %get-tuple-element.42.far_ref, ...), custom_call_target="tpu_custom_call" | custom-call | tf_op jit(solution)/shard_map/early_grad/pallas_call | solution.py:488
  32.6 0.1 collective-permute-start.10
  32.7 1.4 %grad_volume.1 = bf16[256,128]{1,0:T(8,128)(2,1)} custom-call(f32[4,160,128]{2,1,0:T(8,128)S(1)} %get-tuple-element.47.win_ref, bf16[3,3,3,128,128]{4,3,2,1,0:T(8,128)(2,1)S(1)} %get-tuple-element.48.we_ref), custom_call_target="tpu_custom_call" | custom-call | tf_op jit(solution)/shard_map/grad_volume/pallas_call | solution.py:488
  34.1 1.0 %collective-permute-done.10 = bf16[3456,128]{1,0:T(8,128)(2,1)S(1)} collective-permute-done((bf16[3456,128]{1,0:T(8,128)(2,1)S(1)}, bf16[3456,128]{1,0:T(8,128)(2,1)S(1)}, u32[]{:S(2)}, u32[]{:S(2)}) %collective-permute-start.10) | collective-permute-done | bytes 884768 | tf_op jit(solution)/shard_map/ppermute | solution.py:479
  35.1 1.2 %multiply_convert_fusion = bf16[3456,128]{1,0:T(8,128)(2,1)} fusion(bf16[3456,128]{1,0:T(8,128)(2,1)S(1)} %collective-permute-done.10, bf16[3456,128]{1,0:T(8,128)(2,1)S(1)} %get-tuple-element.45), kind=kLoop, calls=%fused_computation | loop fusion | flops 2211840 | bytes 2654208 | tf_op jit(solution)/shard_map/convert_element_type | solution.py:604
Async XLA Ops:
  0.6 10.3 %collective-permute-start = (bf16[256,128]{1,0:T(8,128)(2,1)}, bf16[256,128]{1,0:T(8,128)(2,1)S(1)}, u32[]{:S(2)}, u32[]{:S(2)}) collective-permute-start(bf16[256,128]{1,0:T(8,128)(2,1)} %bitcast.6), channel_id=1, source_target_pairs={{0,12},{4,8},{8,4},{12,0},{1,13},{5,9},{9,5},{13,1},{2,14},{6,10},... | collective-permute-start | bytes 196616 | tf_op jit(solution)/shard_map/ppermute | solution.py:479
  5.7 6.8 %collective-permute-start.1 = (bf16[256,128]{1,0:T(8,128)(2,1)}, bf16[256,128]{1,0:T(8,128)(2,1)S(1)}, u32[]{:S(2)}, u32[]{:S(2)}) collective-permute-start(bf16[256,128]{1,0:T(8,128)(2,1)} %bitcast.7), channel_id=1, source_target_pairs={{0,8},{4,12},{8,0},{12,4},{1,9},{5,13},{9,1},{13,5},{2,10},{6,14},... | collective-permute-start | bytes 196616 | tf_op jit(solution)/shard_map/ppermute | solution.py:479
  5.7 6.8 %collective-permute-start.2 = (bf16[256,128]{1,0:T(8,128)(2,1)}, bf16[256,128]{1,0:T(8,128)(2,1)S(1)}, u32[]{:S(2)}, u32[]{:S(2)}) collective-permute-start(bf16[256,128]{1,0:T(8,128)(2,1)} %bitcast.8), channel_id=1, source_target_pairs={{0,4},{4,0},{8,12},{12,8},{1,5},{5,1},{9,13},{13,9},{2,6},{6,2},{1... | collective-permute-start | bytes 196616 | tf_op jit(solution)/shard_map/ppermute | solution.py:479
  7.2 8.7 %collective-permute-start.3 = (bf16[64,256]{1,0:T(8,128)(2,1)S(1)}, bf16[64,256]{1,0:T(8,128)(2,1)S(1)}, u32[]{:S(2)}, u32[]{:S(2)}) collective-permute-start(bf16[64,256]{1,0:T(8,128)(2,1)S(1)} %reshape.22.refs_3_), channel_id=1, source_target_pairs={{0,12},{4,8},{8,4},{12,0},{1,13},{5,9},{9,5},{13,1},{2,14},{6,10},... | collective-permute-start | bytes 98312 | tf_op jit(solution)/shard_map/ppermute | solution.py:479
  11.0 4.9 %collective-permute-start.4 = (bf16[64,256]{1,0:T(8,128)(2,1)S(1)}, bf16[64,256]{1,0:T(8,128)(2,1)S(1)}, u32[]{:S(2)}, u32[]{:S(2)}) collective-permute-start(bf16[64,256]{1,0:T(8,128)(2,1)S(1)} %reshape.22.refs_3_), channel_id=1, source_target_pairs={{0,8},{4,12},{8,0},{12,4},{1,9},{5,13},{9,1},{13,5},{2,10},{6,14},... | collective-permute-start | bytes 98312 | tf_op jit(solution)/shard_map/ppermute | solution.py:479
  11.0 5.0 %collective-permute-start.5 = (bf16[64,256]{1,0:T(8,128)(2,1)S(1)}, bf16[64,256]{1,0:T(8,128)(2,1)S(1)}, u32[]{:S(2)}, u32[]{:S(2)}) collective-permute-start(bf16[64,256]{1,0:T(8,128)(2,1)S(1)} %reshape.22.refs_3_), channel_id=1, source_target_pairs={{0,4},{4,0},{8,12},{12,8},{1,5},{5,1},{9,13},{13,9},{2,6},{6,2},{1... | collective-permute-start | bytes 98312 | tf_op jit(solution)/shard_map/ppermute | solution.py:479
  15.9 5.3 %collective-permute-start.6 = (bf16[320,128]{1,0:T(8,128)(2,1)S(1)}, bf16[320,128]{1,0:T(8,128)(2,1)S(1)}, u32[]{:S(2)}, u32[]{:S(2)}) collective-permute-start(bf16[320,128]{1,0:T(8,128)(2,1)S(1)} %get-tuple-element.27.refs_0_), channel_id=1, source_target_pairs={{0,2},{2,0},{1,3},{3,1},{4,6},{6,4},{5,7},{7,5},{8,10},{10,8},{9,1... | collective-permute-start | bytes 245768 | tf_op jit(solution)/shard_map/ppermute | solution.py:479
  17.3 8.2 %collective-permute-start.9 = (bf16[1024,128]{1,0:T(8,128)(2,1)S(1)}, bf16[1024,128]{1,0:T(8,128)(2,1)S(1)}, u32[]{:S(2)}, u32[]{:S(2)}) collective-permute-start(bf16[1024,128]{1,0:T(8,128)(2,1)S(1)} %get-tuple-element.38.half_ref), channel_id=1, source_target_pairs={{0,2},{2,0},{1,3},{3,1},{4,6},{6,4},{5,7},{7,5},{8,10},{10,8},{9,1... | collective-permute-start | bytes 786440 | tf_op jit(solution)/shard_map/ppermute | solution.py:479
  23.8 3.8 %collective-permute-start.7 = (bf16[256,384]{1,0:T(8,128)(2,1)S(1)}, bf16[256,384]{1,0:T(8,128)(2,1)S(1)}, u32[]{:S(2)}, u32[]{:S(2)}) collective-permute-start(bf16[256,384]{1,0:T(8,128)(2,1)S(1)} %get-tuple-element.34.mine_ref), channel_id=1, source_target_pairs={{0,1},{1,0},{2,3},{3,2},{4,5},{5,4},{6,7},{7,6},{8,9},{9,8},{10,11... | collective-permute-start | bytes 589832 | tf_op jit(solution)/shard_map/ppermute | solution.py:479
  23.9 6.2 %collective-permute-start.8 = (bf16[256,128]{1,0:T(8,128)(2,1)S(1)}, bf16[256,128]{1,0:T(8,128)(2,1)S(1)}, u32[]{:S(2)}, u32[]{:S(2)}) collective-permute-start(bf16[256,128]{1,0:T(8,128)(2,1)S(1)} %get-tuple-element.36), channel_id=1, source_target_pairs={{0,2},{2,0},{1,3},{3,1},{4,6},{6,4},{5,7},{7,5},{8,10},{10,8},{9,1... | collective-permute-start | bytes 196616 | tf_op jit(solution)/shard_map/ppermute | solution.py:479
  32.6 2.5 %collective-permute-start.10 = (bf16[3456,128]{1,0:T(8,128)(2,1)S(1)}, bf16[3456,128]{1,0:T(8,128)(2,1)S(1)}, u32[]{:S(2)}, u32[]{:S(2)}) collective-permute-start(bf16[3456,128]{1,0:T(8,128)(2,1)S(1)} %get-tuple-element.45), channel_id=1, source_target_pairs={{0,1},{1,0},{2,3},{3,2},{4,5},{5,4},{6,7},{7,6},{8,9},{9,8},{10,11... | collective-permute-start | bytes 2654216 | tf_op jit(solution)/shard_map/ppermute | solution.py:479

commit v5 on v4

--- a/solution.py
+++ b/solution.py
@@ -171,25 +171,30 @@
     )
 
 
+def begin_kernel(own_hbm, we_hbm, own_ref, we_ref, wcat_ref, sems):
+    own = pltpu.make_async_copy(own_hbm, own_ref, sems.at[3])
+    copies = [pltpu.make_async_copy(we_hbm.at[a], we_ref.at[a], sems.at[a]) for a in range(3)]
+    for copy in (*copies, own):
+        copy.start()
+    for a in range(3):
+        copies[a].wait()
+        for n in range(9):
+            b, c = divmod(n, 3)
+            wcat_ref[pl.ds(n * 128, 128), pl.ds(a * 128, 128)] = we_ref[a, b, c]
+    own.wait()
+
+
 def early_kernel(*refs, nk, dims):
     gx, gy, gz, lx, ly, lz, bx, by = dims
     blocks, refs = refs[:nk], refs[nk:]
-    we_hbm, wl_hbm, we_ref, wl_ref, wcat_ref, half_ref, slope_ref, send_ref, edge_ref = refs[:9]
-    vol_ref, own_ref, col_ref, p_ref, pre_ref, h_ref, row_ref, sems = refs[9:]
+    wcat_ref, half_ref, slope_ref, send_ref, edge_ref = refs[:5]
+    vol_ref, col_ref, p_ref, pre_ref, h_ref, row_ref = refs[5:]
     k, j = lax.axis_index("space"), lax.axis_index("chan")
     brows, hl, line = by * gz, by // 2 * lz, gx * gz
-    own_copy = pltpu.make_async_copy(blocks[0], own_ref, sems.at[0])
-    we_copy = pltpu.make_async_copy(we_hbm, we_ref, sems.at[1])
-    wl_copy = pltpu.make_async_copy(wl_hbm, wl_ref, sems.at[2])
-    we_copy.start()
-    own_copy.start()
-
     vol_ref[:, pl.ds(0, 16), :] = jnp.zeros((gx, 16, 128), F32)
     vol_ref[:, pl.ds(16 + brows, 16), :] = jnp.zeros((gx, 16, 128), F32)
-    for n, dk in [*enumerate(far_first(nk), 1), (0, 0)]:
-        if n == 0:
-            own_copy.wait()
-        src = blocks[n] if n else own_ref
+    for n, dk in enumerate([0, *far_first(nk)]):
+        src = blocks[n]
         kk = partner(k, dk, nk)
         for q in range(bx):
             got = src[pl.ds(q * brows, brows), :]
@@ -203,12 +208,6 @@
                 vol_ref, (x,), 16, brows, cell, gz, step
             ).astype(BF)
 
-    we_copy.wait()
-    wl_copy.start()
-    for n in range(9):
-        b, c = divmod(n, 3)
-        for a in range(3):
-            wcat_ref[pl.ds(n * 128, 128), pl.ds(a * 128, 128)] = we_ref[a, b, c]
     p_ref[...] = jnp.dot(col_ref[...], wcat_ref[...], preferred_element_type=F32)
 
     outer = pl.multiple_of((brows - gz) * (1 - j), gz)
@@ -247,7 +246,18 @@
         edge_ref[pl.ds(line + x * gz, gz), :] = pre_ref[x, pl.ds(outer, gz), :]
     edge_ref[pl.ds(2 * line, line), :] = given
     send_ref[pl.ds(lx * hl, 3 * line), :] = edge_ref[...].astype(BF)
-    wl_copy.wait()
+
+
+def fetch_kernel(far_ref, near_ref, back_ref, sems):
+    copies = [pltpu.make_async_copy(far_ref.at[a], near_ref.at[a], sems.at[a]) for a in range(3)]
+    cl = near_ref.shape[-1]
+    for copy in copies:
+        copy.start()
+    for a in range(3):
+        copies[a].wait()
+        for n in range(9):
+            b, c = divmod(n, 3)
+            back_ref[pl.ds(n * cl, cl), pl.ds(a * 128, 128)] = near_ref[a, b, c].astype(F32).T.astype(BF)
 
 
 def border_pool(inner, outer, tmp_ref, tile_ref, dims):
@@ -266,8 +276,8 @@
 def late_kernel(*refs, nk, dims):
     gx, gz, lx, ly, lz, cx = dims
     sent_ref, got_ref, edge_ref, cots, refs = *refs[:3], refs[3 : nk + 3], refs[nk + 3 :]
-    wl_ref, pd_ref, back_ref, mine_ref, patch_ref = refs[:5]
-    pool_ref, lcol_ref, dl_ref, cot_ref, tmp_ref, tile_ref = refs[5:]
+    wl_ref, wback_ref, pd_ref, back_ref, mine_ref, patch_ref = refs[:6]
+    pool_ref, lcol_ref, dl_ref, dcol_ref, cot_ref, tmp_ref, tile_ref = refs[6:]
     lplane, hl, line = ly * lz, ly // 2 * lz, gx * gz
     cl = wl_ref.shape[-1]
     crow = cx * lplane
@@ -320,39 +330,47 @@
     wide = delta.astype(F32)
     for x in range(lx):
         dl_ref[x, pl.ds(8, lplane), :] = wide[x * lplane : (x + 1) * lplane]
-    total = None
     for n, (b, c) in enumerate(STEPS):
-        part = jnp.concatenate(
-            [shifted(dl_ref, (x,), 8, lplane, lcell, lz, (-b, -c)) for x in range(lx)], axis=0
-        ).astype(BF)
-        w = wl_ref[:, b + 1, c + 1].reshape(3 * 128, cl)
-        term = lax.dot_general(part, w, NT, preferred_element_type=F32)
-        total = term if total is None else total + term
+        for x in range(lx):
+            dcol_ref[pl.ds(x * lplane, lplane), pl.ds(n * cl, cl)] = shifted(
+                dl_ref, (x,), 8, lplane, lcell, lz, (-b, -c)
+            ).astype(BF)
+    total = jnp.dot(dcol_ref[...], wback_ref[...], preferred_element_type=F32)
     back = fold([total[:, (2 - a) * 128 : (3 - a) * 128] for a in range(3)], lplane)
     back_ref[...] = back.astype(BF)
     mine_ref[...] = back
 
 
-def late_grad_kernel(mine_ref, other_ref, out_ref, pool_ref, lcol_ref, *, dims, scale):
+def late_grad_kernel(mine_ref, other_ref, out_ref, pool_ref, lcol_ref, wide_ref, *, dims, scale):
     lx, ly, lz = dims
     lplane = ly * lz
     rows = lx * lplane
+    cl = mine_ref.shape[1] - 128
     lcell = depth_of(lplane, lz)
-    pool_ref[...] = jnp.zeros(pool_ref.shape, F32)
+    for x in range(lx):
+        pool_ref[x, pl.ds(0, 8), :] = jnp.zeros((8, 128), F32)
+        pool_ref[x, pl.ds(8 + lplane, 8), :] = jnp.zeros((8, 128), F32)
     for s, ref in enumerate((mine_ref, other_ref)):
         for x in range(lx):
-            pool_ref[s, x + 1, pl.ds(8, lplane), :] = ref[pl.ds(x * lplane, lplane), pl.ds(0, 128)].astype(F32)
-        for x in range(lx + 2):
+            pool_ref[x, pl.ds(8, lplane), :] = ref[pl.ds(x * lplane, lplane), pl.ds(0, 128)].astype(F32)
+        for x in range(lx):
             for n, step in enumerate(STEPS):
-                lcol_ref[s, pl.ds(x * lplane, lplane), pl.ds(n * 128, 128)] = shifted(
-                    pool_ref, (s, x), 8, lplane, lcell, lz, step
+                lcol_ref[pl.ds(s * rows + x * lplane, lplane), pl.ds(n * 128, 128)] = shifted(
+                    pool_ref, (x,), 8, lplane, lcell, lz, step
                 ).astype(BF)
-    cl = mine_ref.shape[1] - 128
-    delta = jnp.concatenate([mine_ref[:, pl.ds(128, cl)], other_ref[:, pl.ds(128, cl)]], axis=0)
+        zero = jnp.zeros((lplane, cl), BF)
+        wide_ref[pl.ds(s * rows + rows - lplane, lplane), pl.ds(0, cl)] = zero
+        wide_ref[pl.ds(s * rows, rows - lplane), pl.ds(0, cl)] = ref[pl.ds(lplane, rows - lplane), pl.ds(128, cl)]
+        wide_ref[pl.ds(s * rows, rows), pl.ds(cl, cl)] = ref[:, pl.ds(128, cl)]
+        wide_ref[pl.ds(s * rows, lplane), pl.ds(2 * cl, cl)] = zero
+        wide_ref[pl.ds(s * rows + lplane, rows - lplane), pl.ds(2 * cl, cl)] = ref[
+            pl.ds(0, rows - lplane), pl.ds(128, cl)
+        ]
+    got = lax.dot_general(
+        lcol_ref[...], wide_ref[...], (((0,), (0,)), ((), ())), preferred_element_type=F32
+    )
     for a in range(3):
-        left = jnp.concatenate([lcol_ref[s, pl.ds(a * lplane, rows), :] for s in (0, 1)], axis=0)
-        got = lax.dot_general(left, delta, (((0,), (0,)), ((), ())), preferred_element_type=F32)
-        out_ref[pl.ds(a * 9 * 128, 9 * 128), :] = (got * scale).astype(BF)
+        out_ref[pl.ds(a * 9 * 128, 9 * 128), :] = (got[:, a * cl : (a + 1) * cl] * scale).astype(BF)
 
 
 def other_kernel(
@@ -511,16 +529,22 @@
     mine = volume.reshape(bx * brows, 128)
     line = [mine] + [turned(mine, "space", dk) for dk in far_first(nk)]
     cot = cotangent.reshape(cx * lplane, cl)
+    own, we, wcat = call(
+        begin_kernel,
+        [sds(mine.shape, BF), sds(early_weight.shape, BF), sds((9 * 128, 3 * 128), BF)],
+        [pltpu.SemaphoreType.DMA((4,))],
+        [mine, early_weight],
+        "begin",
+        raw=(0, 1),
+    )
+    line[0] = own
     cots = [cot] + [turned(cot, "space", dk) for dk in far_first(nk)]
 
     dims = (gx, gy, gz, lx, ly, lz, bx, by)
     hrows, edge = gx * brows, 3 * gx * gz
-    we, wl, wcat, half, slope, send, edges = call(
+    half, slope, send, edges = call(
         functools.partial(early_kernel, nk=nk, dims=dims),
         [
-            sds(early_weight.shape, BF),
-            sds(late_weight.shape, BF),
-            sds((9 * 128, 3 * 128), BF),
             sds((hrows, 128), BF),
             sds((hrows, 128), F32),
             sds((lrows // 2 + edge, 128), BF),
@@ -528,21 +552,27 @@
         ],
         [
             pltpu.VMEM((gx, brows + 32, 128), F32),
-            pltpu.VMEM((bx * brows, 128), BF),
             pltpu.VMEM((hrows, 9 * 128), BF),
             pltpu.VMEM((hrows, 3 * 128), F32),
             pltpu.VMEM((gx, brows, 128), F32),
             pltpu.VMEM((by // 2 * gz, 128), F32),
             pltpu.VMEM((gx * gz, 128), F32),
-            pltpu.SemaphoreType.DMA((3,)),
-        ],
-        line + [early_weight, late_weight],
+        ],
+        line + [wcat],
         "early",
-        raw=(0, nk, nk + 1),
     )
     ready, *cots[1:] = lax.optimization_barrier((send, *cots[1:]))
     send_other = turned(ready, "chan", 1)
     half_other = turned(half, "chan", 1)
+    held, _ = lax.optimization_barrier((late_weight, send))
+    wl, wback = call(
+        fetch_kernel,
+        [sds(late_weight.shape, BF), sds((9 * cl, 3 * 128), BF)],
+        [pltpu.SemaphoreType.DMA((3,))],
+        [held],
+        "fetch",
+        raw=(0,),
+    )
     pooled_delta, back, back_mine, patch = call(
         functools.partial(late_kernel, nk=nk, dims=(gx, gz, lx, ly, lz, cx)),
         [
@@ -555,11 +585,12 @@
             pltpu.VMEM((lx, lplane + 16, 128), F32),
             pltpu.VMEM((lrows, 9 * 128), BF),
             pltpu.VMEM((lx, lplane + 16, cl), F32),
+            pltpu.VMEM((lrows, 9 * cl), BF),
             pltpu.VMEM((lrows, cl), F32),
             pltpu.VMEM((lx * gz, 128), F32),
             pltpu.VMEM((lx * 2 * lz, 128), F32),
         ],
-        [send, send_other, edges] + cots + [wl],
+        [send, send_other, edges] + cots + [wl, wback],
         "late",
     )
     pd_other = turned(pooled_delta, "rep", 1)
@@ -567,10 +598,13 @@
     (late,) = call(
         functools.partial(late_grad_kernel, dims=(lx, ly, lz), scale=scale),
         [sds((27 * 128, cl), BF)],
-        [pltpu.VMEM((2, lx + 2, lplane + 16, 128), F32), pltpu.VMEM((2, (lx + 2) * lplane, 9 * 128), BF)],
+        [
+            pltpu.VMEM((lx, lplane + 16, 128), F32),
+            pltpu.VMEM((2 * lrows, 9 * 128), BF),
+            pltpu.VMEM((2 * lrows, 3 * cl), BF),
+        ],
         [pooled_delta, pd_other],
         "late_grad",
-        far=(0,),
     )
     half_other, wcat, _ = lax.optimization_barrier((half_other, wcat, back))
     col, far_slope = call(

time: 36.5 us -> 35.2 us (0.964)
  waiting for transfers between devices: 5.25 us -> 2.65 us
  local copies, waits for them, and re-layouts: 0.77 us -> 1.98 us
    ppermute x11, waiting for transfers between devices: 5.25 us -> 2.65 us  [turned(): lax.ppermute(value, axis, [(i, i ^ by if pairs else (i + by) % count) for...]
    unnamed x0 -> x1, local copies, waits for them, and re-layouts: none -> 1.21 us
    pallas_call x6 -> x8, Pallas kernels: 14.4 us -> 14.6 us  [call(): pl.pallas_call(kernel, out_shape=outs, in_specs=[pl.BlockSpec(memory_spac...]
  transfers between devices with their start and end apart: 11 -> 11, of which waited for: 4 -> 2; matrix products, arithmetic and copies ran while one was open for 2% -> 6% of each run, Pallas kernels for 33% -> 35%
where the time goes in v5:
time: 35.2 us; the launch traced here: 34.9 us
  Pallas kernels  14.6 us (41%)
  starting transfers between devices  13.8 us (39%)
  waiting for transfers between devices  2.65 us (8%)
  local copies, waits for them, and re-layouts  1.98 us (6%)
  other arithmetic  1.2 us (3%)
  between operations  0.72 us (2%)
    pallas_call x8, Pallas kernels, call(): pl.pallas_call(kernel, out_shape=outs, in_specs=[pl.BlockSpec(memory_spac...  14.6 us
    ppermute x11, starting transfers between devices, turned(): lax.ppermute(value, axis, [(i, i ^ by if pairs else (i + by) % count) for...  13.8 us
    ppermute x11, waiting for transfers between devices, turned(): lax.ppermute(value, axis, [(i, i ^ by if pairs else (i + by) % count) for...  2.65 us
    unnamed x1, local copies, waits for them, and re-layouts  1.21 us
    convert_element_type x1, other arithmetic, whole_sample(): early = ((part.astype(F32) + part_other.astype(F32)) * scale).astype(BF)  1.2 us
    reshape x1, local copies, waits for them, and re-layouts, whole_sample(): cot = cotangent.reshape(cx * lplane, cl)  0.77 us
  transfers between devices with their start and end apart: 11, of which 2 were waited for; matrix products, arithmetic and copies ran while one was open for 6% of the time, Pallas kernels for 35%

profile of v5, /device:TPU:0, one launch (start us, length us, event | category | flops | bytes accessed | tf_op | source)
XLA Modules:
  0.0 34.9 jit_solution(1086188088273969636)
XLA Ops:
  0.6 5.1 %collective-permute-start = (bf16[256,128]{1,0:T(8,128)(2,1)}, bf16[256,128]{1,0:T(8,128)(2,1)S(1)}, u32[]{:S(2)}, u32[]{:S(2)}) collective-permute-start(bf16[256,128]{1,0:T(8,128)(2,1)} %bitcast.7), channel_id=1, source_target_pairs={{0,12},{4,8},{8,4},{12,0},{1,13},{5,9},{9,5},{13,1},{2,14},{6,10},... | collective-permute-start | bytes 196616 | tf_op jit(solution)/shard_map/ppermute | solution.py:497
  5.7 0.0 collective-permute-start.1
  5.7 0.6 %collective-permute-start.2 = (bf16[256,128]{1,0:T(8,128)(2,1)}, bf16[256,128]{1,0:T(8,128)(2,1)S(1)}, u32[]{:S(2)}, u32[]{:S(2)}) collective-permute-start(bf16[256,128]{1,0:T(8,128)(2,1)} %bitcast.9), channel_id=1, source_target_pairs={{0,4},{4,0},{8,12},{12,8},{1,5},{5,1},{9,13},{13,9},{2,6},{6,2},{1... | collective-permute-start | bytes 196616 | tf_op jit(solution)/shard_map/ppermute | solution.py:497
  6.4 0.8 %reshape.22.refs_3_ = bf16[64,256]{1,0:T(8,128)(2,1)S(1)} reshape(bf16[1,1,16,4,256]{4,3,2,1,0:T(4,128)(2,1)} %param.7) | data formatting | bytes 65536 | tf_op jit(solution)/shard_map/reshape | solution.py:531
  7.2 3.8 %collective-permute-start.3 = (bf16[64,256]{1,0:T(8,128)(2,1)S(1)}, bf16[64,256]{1,0:T(8,128)(2,1)S(1)}, u32[]{:S(2)}, u32[]{:S(2)}) collective-permute-start(bf16[64,256]{1,0:T(8,128)(2,1)S(1)} %reshape.22.refs_3_), channel_id=1, source_target_pairs={{0,12},{4,8},{8,4},{12,0},{1,13},{5,9},{9,5},{13,1},{2,14},{6,10},... | collective-permute-start | bytes 98312 | tf_op jit(solution)/shard_map/ppermute | solution.py:497
  11.0 0.0 collective-permute-start.4
  11.0 0.0 collective-permute-done.refs_1_
  11.0 0.6 %collective-permute-start.5 = (bf16[64,256]{1,0:T(8,128)(2,1)S(1)}, bf16[64,256]{1,0:T(8,128)(2,1)S(1)}, u32[]{:S(2)}, u32[]{:S(2)}) collective-permute-start(bf16[64,256]{1,0:T(8,128)(2,1)S(1)} %reshape.22.refs_3_), channel_id=1, source_target_pairs={{0,4},{4,0},{8,12},{12,8},{1,5},{5,1},{9,13},{13,9},{2,6},{6,2},{1... | collective-permute-start | bytes 98312 | tf_op jit(solution)/shard_map/ppermute | solution.py:497
  11.6 1.2 %begin.1 = (bf16[256,128]{1,0:T(8,128)(2,1)S(1)}, bf16[3,3,3,128,128]{4,3,2,1,0:T(8,128)(2,1)S(1)}, bf16[1152,384]{1,0:T(8,128)(2,1)S(1)}) custom-call(bf16[256,128]{1,0:T(8,128)(2,1)} %bitcast.10, bf16[3,3,3,128,128]{4,3,2,1,0:T(8,128)(2,1)} %we_hbm.1), custom_call_target="tpu_custom_call" | custom-call | tf_op jit(solution)/shard_map/begin/pallas_call | solution.py:506
  12.9 0.0 collective-permute-done.1.refs_2_
  12.9 0.0 collective-permute-done.2.refs_3_
  12.9 1.8 %early.1 = (bf16[1024,128]{1,0:T(8,128)(2,1)S(1)}, f32[1024,128]{1,0:T(8,128)S(1)}, bf16[320,128]{1,0:T(8,128)(2,1)S(1)}, f32[192,128]{1,0:T(8,128)S(1)}) custom-call(bf16[256,128]{1,0:T(8,128)(2,1)S(1)} %get-tuple-element.29.refs_0_, bf16[256,128]{1,0:T(8,128)(2,1)S(1)} %collective-permute-done.refs_1_, ...), custom_call_target="tpu_custom_call" | custom-call | tf_op jit(solution)/shard_map/early/pallas_call | solution.py:506
  14.6 0.0 collective-permute-done.3.refs_4_
  14.6 1.1 %collective-permute-done.4.refs_5_ = bf16[64,256]{1,0:T(8,128)(2,1)S(1)} collective-permute-done((bf16[64,256]{1,0:T(8,128)(2,1)S(1)}, bf16[64,256]{1,0:T(8,128)(2,1)S(1)}, u32[]{:S(2)}, u32[]{:S(2)}) %collective-permute-start.4) | collective-permute-done | bytes 32800 | tf_op jit(solution)/shard_map/ppermute | solution.py:497
  15.8 0.0 collective-permute-done.5.refs_6_
  15.8 1.5 %collective-permute-start.6 = (bf16[320,128]{1,0:T(8,128)(2,1)S(1)}, bf16[320,128]{1,0:T(8,128)(2,1)S(1)}, u32[]{:S(2)}, u32[]{:S(2)}) collective-permute-start(bf16[320,128]{1,0:T(8,128)(2,1)S(1)} %get-tuple-element.32.refs_0_), channel_id=1, source_target_pairs={{0,2},{2,0},{1,3},{3,1},{4,6},{6,4},{5,7},{7,5},{8,10},{10,8},{9,1... | collective-permute-start | bytes 245768 | tf_op jit(solution)/shard_map/ppermute | solution.py:497
  17.3 0.5 %collective-permute-start.9 = (bf16[1024,128]{1,0:T(8,128)(2,1)S(1)}, bf16[1024,128]{1,0:T(8,128)(2,1)S(1)}, u32[]{:S(2)}, u32[]{:S(2)}) collective-permute-start(bf16[1024,128]{1,0:T(8,128)(2,1)S(1)} %get-tuple-element.45.half_ref), channel_id=1, source_target_pairs={{0,2},{2,0},{1,3},{3,1},{4,6},{6,4},{5,7},{7,5},{8,10},{10,8},{9,1... | collective-permute-start | bytes 786440 | tf_op jit(solution)/shard_map/ppermute | solution.py:497
  17.8 1.8 %fetch.1 = (bf16[3,3,3,128,256]{4,3,2,1,0:T(8,128)(2,1)S(1)}, bf16[2304,384]{1,0:T(8,128)(2,1)S(1)}) custom-call(bf16[3,3,3,128,256]{4,3,2,1,0:T(8,128)(2,1)} %far_ref), custom_call_target="tpu_custom_call" | custom-call | tf_op jit(solution)/shard_map/fetch/pallas_call | solution.py:506
  19.6 1.5 %collective-permute-done.6.refs_1_ = bf16[320,128]{1,0:T(8,128)(2,1)S(1)} collective-permute-done((bf16[320,128]{1,0:T(8,128)(2,1)S(1)}, bf16[320,128]{1,0:T(8,128)(2,1)S(1)}, u32[]{:S(2)}, u32[]{:S(2)}) %collective-permute-start.6) | collective-permute-done | bytes 81952 | tf_op jit(solution)/shard_map/ppermute | solution.py:497
  21.1 2.5 %late.1 = (bf16[256,384]{1,0:T(8,128)(2,1)S(1)}, bf16[256,128]{1,0:T(8,128)(2,1)S(1)}, f32[256,128]{1,0:T(8,128)S(1)}, f32[64,128]{1,0:T(8,128)S(1)}) custom-call(bf16[320,128]{1,0:T(8,128)(2,1)S(1)} %get-tuple-element.32.refs_0_, bf16[320,128]{1,0:T(8,128)(2,1)S(1)} %collective-permute-done.6.refs_1_, f32[192,128]{1,0:T(8,128)S(1)} %get-tuple-element.33.refs_2_, ...), custom_call_target="tpu_custom_call" | custom-call | tf_op jit(solution)/shard_map/late/pallas_call | solution.py:506
  23.7 0.1 collective-permute-start.7
  23.7 1.2 %collective-permute-start.8 = (bf16[256,128]{1,0:T(8,128)(2,1)S(1)}, bf16[256,128]{1,0:T(8,128)(2,1)S(1)}, u32[]{:S(2)}, u32[]{:S(2)}) collective-permute-start(bf16[256,128]{1,0:T(8,128)(2,1)S(1)} %get-tuple-element.43), channel_id=1, source_target_pairs={{0,2},{2,0},{1,3},{3,1},{4,6},{6,4},{5,7},{7,5},{8,10},{10,8},{9,1... | collective-permute-start | bytes 196616 | tf_op jit(solution)/shard_map/ppermute | solution.py:497
  25.0 0.0 collective-permute-done.9.got_ref
  25.0 2.1 %other.1 = (bf16[2048,1152]{1,0:T(8,128)(2,1)S(1)}, f32[1024,128]{1,0:T(8,128)S(1)}) custom-call(bf16[1024,128]{1,0:T(8,128)(2,1)S(1)} %get-tuple-element.45.half_ref, bf16[1024,128]{1,0:T(8,128)(2,1)S(1)} %collective-permute-done.9.got_ref, bf16[1152,384]{1,0:T(8,128)(2,1)S(1)} %get-tuple-element.47.refs_4_.wcat_ref), custom_call_target="tpu_custom_call" | custom-call | tf_op jit(solution)/shard_map/other/pallas_call | solution.py:506
  27.1 0.0 collective-permute-done.7.other_ref
  27.1 1.2 %late_grad.1 = bf16[3456,256]{1,0:T(8,128)(2,1)S(1)} custom-call(bf16[256,384]{1,0:T(8,128)(2,1)S(1)} %get-tuple-element.41.mine_ref, bf16[256,384]{1,0:T(8,128)(2,1)S(1)} %collective-permute-done.7.other_ref), custom_call_target="tpu_custom_call" | custom-call | tf_op jit(solution)/shard_map/late_grad/pallas_call | solution.py:506
  28.4 0.0 collective-permute-done.8.other_ref
  28.4 2.5 %early_grad.1 = (bf16[3456,128]{1,0:T(8,128)(2,1)S(1)}, f32[4,160,128]{2,1,0:T(8,128)S(1)}) custom-call(f32[256,128]{1,0:T(8,128)S(1)} %get-tuple-element.42.mine_ref, bf16[256,128]{1,0:T(8,128)(2,1)S(1)} %collective-permute-done.8.other_ref, f32[1024,128]{1,0:T(8,128)S(1)} %get-tuple-element.44.slope_ref, f32[1024,128]{1,0:T(8,128)S(1)} %get-tuple-element.48.far_ref, ...), custom_call_target="tpu_custom_call" | custom-call | tf_op jit(solution)/shard_map/early_grad/pallas_call | solution.py:506
  30.9 0.2 collective-permute-start.10
  31.1 1.2 %copy.7 = bf16[3,3,3,128,256]{4,3,2,1,0:T(8,128)(2,1)} copy(bf16[3,3,3,128,256]{4,3,2,1,0:T(8,128)(2,1)S(1)} %bitcast.4) | data formatting | bytes 3538944
  32.3 1.4 %grad_volume.1 = bf16[256,128]{1,0:T(8,128)(2,1)} custom-call(f32[4,160,128]{2,1,0:T(8,128)S(1)} %get-tuple-element.53.win_ref, bf16[3,3,3,128,128]{4,3,2,1,0:T(8,128)(2,1)S(1)} %get-tuple-element.54.we_ref), custom_call_target="tpu_custom_call" | custom-call | tf_op jit(solution)/shard_map/grad_volume/pallas_call | solution.py:506
  33.7 0.0 collective-permute-done.10
  33.7 1.2 %multiply_convert_fusion = bf16[3456,128]{1,0:T(8,128)(2,1)} fusion(bf16[3456,128]{1,0:T(8,128)(2,1)S(1)} %collective-permute-done.10, bf16[3456,128]{1,0:T(8,128)(2,1)S(1)} %get-tuple-element.51), kind=kLoop, calls=%fused_computation | loop fusion | flops 2211840 | bytes 2654208 | tf_op jit(solution)/shard_map/convert_element_type | solution.py:638
Async XLA Ops:
  0.6 10.3 %collective-permute-start = (bf16[256,128]{1,0:T(8,128)(2,1)}, bf16[256,128]{1,0:T(8,128)(2,1)S(1)}, u32[]{:S(2)}, u32[]{:S(2)}) collective-permute-start(bf16[256,128]{1,0:T(8,128)(2,1)} %bitcast.7), channel_id=1, source_target_pairs={{0,12},{4,8},{8,4},{12,0},{1,13},{5,9},{9,5},{13,1},{2,14},{6,10},... | collective-permute-start | bytes 196616 | tf_op jit(solution)/shard_map/ppermute | solution.py:497
  5.7 7.1 %collective-permute-start.1 = (bf16[256,128]{1,0:T(8,128)(2,1)}, bf16[256,128]{1,0:T(8,128)(2,1)S(1)}, u32[]{:S(2)}, u32[]{:S(2)}) collective-permute-start(bf16[256,128]{1,0:T(8,128)(2,1)} %bitcast.8), channel_id=1, source_target_pairs={{0,8},{4,12},{8,0},{12,4},{1,9},{5,13},{9,1},{13,5},{2,10},{6,14},... | collective-permute-start | bytes 196616 | tf_op jit(solution)/shard_map/ppermute | solution.py:497
  5.7 7.1 %collective-permute-start.2 = (bf16[256,128]{1,0:T(8,128)(2,1)}, bf16[256,128]{1,0:T(8,128)(2,1)S(1)}, u32[]{:S(2)}, u32[]{:S(2)}) collective-permute-start(bf16[256,128]{1,0:T(8,128)(2,1)} %bitcast.9), channel_id=1, source_target_pairs={{0,4},{4,0},{8,12},{12,8},{1,5},{5,1},{9,13},{13,9},{2,6},{6,2},{1... | collective-permute-start | bytes 196616 | tf_op jit(solution)/shard_map/ppermute | solution.py:497
  7.2 7.5 %collective-permute-start.3 = (bf16[64,256]{1,0:T(8,128)(2,1)S(1)}, bf16[64,256]{1,0:T(8,128)(2,1)S(1)}, u32[]{:S(2)}, u32[]{:S(2)}) collective-permute-start(bf16[64,256]{1,0:T(8,128)(2,1)S(1)} %reshape.22.refs_3_), channel_id=1, source_target_pairs={{0,12},{4,8},{8,4},{12,0},{1,13},{5,9},{9,5},{13,1},{2,14},{6,10},... | collective-permute-start | bytes 98312 | tf_op jit(solution)/shard_map/ppermute | solution.py:497
  11.0 4.8 %collective-permute-start.4 = (bf16[64,256]{1,0:T(8,128)(2,1)S(1)}, bf16[64,256]{1,0:T(8,128)(2,1)S(1)}, u32[]{:S(2)}, u32[]{:S(2)}) collective-permute-start(bf16[64,256]{1,0:T(8,128)(2,1)S(1)} %reshape.22.refs_3_), channel_id=1, source_target_pairs={{0,8},{4,12},{8,0},{12,4},{1,9},{5,13},{9,1},{13,5},{2,10},{6,14},... | collective-permute-start | bytes 98312 | tf_op jit(solution)/shard_map/ppermute | solution.py:497
  11.0 4.8 %collective-permute-start.5 = (bf16[64,256]{1,0:T(8,128)(2,1)S(1)}, bf16[64,256]{1,0:T(8,128)(2,1)S(1)}, u32[]{:S(2)}, u32[]{:S(2)}) collective-permute-start(bf16[64,256]{1,0:T(8,128)(2,1)S(1)} %reshape.22.refs_3_), channel_id=1, source_target_pairs={{0,4},{4,0},{8,12},{12,8},{1,5},{5,1},{9,13},{13,9},{2,6},{6,2},{1... | collective-permute-start | bytes 98312 | tf_op jit(solution)/shard_map/ppermute | solution.py:497
  15.8 5.3 %collective-permute-start.6 = (bf16[320,128]{1,0:T(8,128)(2,1)S(1)}, bf16[320,128]{1,0:T(8,128)(2,1)S(1)}, u32[]{:S(2)}, u32[]{:S(2)}) collective-permute-start(bf16[320,128]{1,0:T(8,128)(2,1)S(1)} %get-tuple-element.32.refs_0_), channel_id=1, source_target_pairs={{0,2},{2,0},{1,3},{3,1},{4,6},{6,4},{5,7},{7,5},{8,10},{10,8},{9,1... | collective-permute-start | bytes 245768 | tf_op jit(solution)/shard_map/ppermute | solution.py:497
  17.3 7.7 %collective-permute-start.9 = (bf16[1024,128]{1,0:T(8,128)(2,1)S(1)}, bf16[1024,128]{1,0:T(8,128)(2,1)S(1)}, u32[]{:S(2)}, u32[]{:S(2)}) collective-permute-start(bf16[1024,128]{1,0:T(8,128)(2,1)S(1)} %get-tuple-element.45.half_ref), channel_id=1, source_target_pairs={{0,2},{2,0},{1,3},{3,1},{4,6},{6,4},{5,7},{7,5},{8,10},{10,8},{9,1... | collective-permute-start | bytes 786440 | tf_op jit(solution)/shard_map/ppermute | solution.py:497
  23.7 3.5 %collective-permute-start.7 = (bf16[256,384]{1,0:T(8,128)(2,1)S(1)}, bf16[256,384]{1,0:T(8,128)(2,1)S(1)}, u32[]{:S(2)}, u32[]{:S(2)}) collective-permute-start(bf16[256,384]{1,0:T(8,128)(2,1)S(1)} %get-tuple-element.41.mine_ref), channel_id=1, source_target_pairs={{0,1},{1,0},{2,3},{3,2},{4,5},{5,4},{6,7},{7,6},{8,9},{9,8},{10,11... | collective-permute-start | bytes 589832 | tf_op jit(solution)/shard_map/ppermute | solution.py:497
  23.7 4.6 %collective-permute-start.8 = (bf16[256,128]{1,0:T(8,128)(2,1)S(1)}, bf16[256,128]{1,0:T(8,128)(2,1)S(1)}, u32[]{:S(2)}, u32[]{:S(2)}) collective-permute-start(bf16[256,128]{1,0:T(8,128)(2,1)S(1)} %get-tuple-element.43), channel_id=1, source_target_pairs={{0,2},{2,0},{1,3},{3,1},{4,6},{6,4},{5,7},{7,5},{8,10},{10,8},{9,1... | collective-permute-start | bytes 196616 | tf_op jit(solution)/shard_map/ppermute | solution.py:497
  30.9 2.9 %collective-permute-start.10 = (bf16[3456,128]{1,0:T(8,128)(2,1)S(1)}, bf16[3456,128]{1,0:T(8,128)(2,1)S(1)}, u32[]{:S(2)}, u32[]{:S(2)}) collective-permute-start(bf16[3456,128]{1,0:T(8,128)(2,1)S(1)} %get-tuple-element.51), channel_id=1, source_target_pairs={{0,1},{1,0},{2,3},{3,2},{4,5},{5,4},{6,7},{7,6},{8,9},{9,8},{10,11... | collective-permute-start | bytes 2654216 | tf_op jit(solution)/shard_map/ppermute | solution.py:497

commit v6 on v5

--- a/solution.py
+++ b/solution.py
@@ -193,7 +193,7 @@
     brows, hl, line = by * gz, by // 2 * lz, gx * gz
     vol_ref[:, pl.ds(0, 16), :] = jnp.zeros((gx, 16, 128), F32)
     vol_ref[:, pl.ds(16 + brows, 16), :] = jnp.zeros((gx, 16, 128), F32)
-    for n, dk in enumerate([0, *far_first(nk)]):
+    for n, dk in enumerate([0, *steps_of(nk)]):
         src = blocks[n]
         kk = partner(k, dk, nk)
         for q in range(bx):
@@ -248,11 +248,15 @@
     send_ref[pl.ds(lx * hl, 3 * line), :] = edge_ref[...].astype(BF)
 
 
-def fetch_kernel(far_ref, near_ref, back_ref, sems):
+def fetch_kernel(far_ref, we_ref, near_ref, back_ref, wt_ref, sems):
     copies = [pltpu.make_async_copy(far_ref.at[a], near_ref.at[a], sems.at[a]) for a in range(3)]
     cl = near_ref.shape[-1]
     for copy in copies:
         copy.start()
+    for n in range(9):
+        b, c = divmod(n, 3)
+        for a in range(3):
+            wt_ref[a, pl.ds(n * 128, 128), :] = we_ref[a, b, c].astype(F32).T.astype(BF)
     for a in range(3):
         copies[a].wait()
         for n in range(9):
@@ -276,8 +280,8 @@
 def late_kernel(*refs, nk, dims):
     gx, gz, lx, ly, lz, cx = dims
     sent_ref, got_ref, edge_ref, cots, refs = *refs[:3], refs[3 : nk + 3], refs[nk + 3 :]
-    wl_ref, wback_ref, pd_ref, back_ref, mine_ref, patch_ref = refs[:6]
-    pool_ref, lcol_ref, dl_ref, dcol_ref, cot_ref, tmp_ref, tile_ref = refs[6:]
+    wl_ref, pd_ref, patch_ref = refs[:3]
+    pool_ref, lcol_ref, cot_ref, tmp_ref, tile_ref = refs[3:]
     lplane, hl, line = ly * lz, ly // 2 * lz, gx * gz
     cl = wl_ref.shape[-1]
     crow = cx * lplane
@@ -316,20 +320,25 @@
     parts = [
         jnp.dot(lcol, wl_ref[a].reshape(9 * 128, cl), preferred_element_type=F32) for a in range(3)
     ]
-    for x in range(lx):
-        dl_ref[x, pl.ds(0, 8), :] = jnp.zeros((8, cl), F32)
-        dl_ref[x, pl.ds(8 + lplane, 8), :] = jnp.zeros((8, cl), F32)
     pre = fold(parts, lplane)
     slope = gelu_and_slope(pre)[1]
-    for n, dk in enumerate([0, *far_first(nk)]):
+    for n, dk in enumerate([0, *steps_of(nk)]):
         kk = partner(k, dk, nk)
         start = pl.multiple_of(kk * crow, 8)
         cot_ref[pl.ds(start, crow), :] = cots[n][...].astype(F32)
     delta = (cot_ref[...] * slope).astype(BF)
     pd_ref[:, pl.ds(128, cl)] = delta
-    wide = delta.astype(F32)
+
+
+def late_back_kernel(pd_ref, wback_ref, back_ref, mine_ref, dl_ref, dcol_ref, *, dims):
+    lx, ly, lz = dims
+    lplane = ly * lz
+    cl = pd_ref.shape[1] - 128
+    lcell = depth_of(lplane, lz)
     for x in range(lx):
-        dl_ref[x, pl.ds(8, lplane), :] = wide[x * lplane : (x + 1) * lplane]
+        dl_ref[x, pl.ds(0, 8), :] = jnp.zeros((8, cl), F32)
+        dl_ref[x, pl.ds(8 + lplane, 8), :] = jnp.zeros((8, cl), F32)
+        dl_ref[x, pl.ds(8, lplane), :] = pd_ref[pl.ds(x * lplane, lplane), pl.ds(128, cl)].astype(F32)
     for n, (b, c) in enumerate(STEPS):
         for x in range(lx):
             dcol_ref[pl.ds(x * lplane, lplane), pl.ds(n * cl, cl)] = shifted(
@@ -409,9 +418,11 @@
 
 
 def early_grad_kernel(
-    mine_ref, other_ref, slope_ref, far_ref, patch_ref, col_ref,
-    part_ref, win_ref, wide_ref, d_ref, dt_ref, *, dims
+    mine_ref, other_ref, slope_ref, far_ref, patch_ref, col_ref, late_ref,
+    part_ref, win_ref, out_ref, wide_ref, d_ref, dt_ref, sem, *, dims
 ):
+    leave = pltpu.make_async_copy(late_ref, out_ref, sem)
+    leave.start()
     gx, gy, gz, lx, ly, lz, bx, by = dims
     plane, lplane = gy * gz, ly * lz
     k, j = lax.axis_index("space"), lax.axis_index("chan")
@@ -461,13 +472,10 @@
     row = pl.multiple_of(j * brows, 8)
     for q in range(bx + 2):
         win_ref[q] = d_ref[k * bx + q, pl.ds(row, brows + 32), :]
-
-
-def grad_volume_kernel(win_ref, we_ref, gv_ref, vcol_ref, wt_ref, *, bx, brows, gz):
-    for n in range(9):
-        b, c = divmod(n, 3)
-        for a in range(3):
-            wt_ref[a, pl.ds(n * 128, 128), :] = we_ref[a, b, c].astype(F32).T.astype(BF)
+    leave.wait()
+
+
+def grad_volume_kernel(win_ref, wt_ref, gv_ref, vcol_ref, *, bx, brows, gz):
     cell = depth_of(brows, gz)
     for q in range(bx + 2):
         for n, (b, c) in enumerate(STEPS):
@@ -481,8 +489,8 @@
     gv_ref[...] = total.astype(BF)
 
 
-def far_first(count):
-    return range(count - 1, 0, -1)
+def steps_of(count):
+    return range(1, count)
 
 
 def partner(index, by, count):
@@ -497,19 +505,21 @@
     return lax.ppermute(value, axis, [(i, i ^ by if pairs else (i + by) % count) for i in range(count)])
 
 
-def call(kernel, outs, scratch, args, name, far=(), raw=()):
+def call(kernel, outs, scratch, args, name, far=(), raw=(), away=()):
     args = [
         pltpu.with_memory_space_constraint(arg, pltpu.HBM if n in raw else pltpu.VMEM)
         for n, arg in enumerate(args)
     ]
-    outs = [out if n in far else pltpu.VMEM(out.shape, out.dtype) for n, out in enumerate(outs)]
+    outs = [out if n in (*far, *away) else pltpu.VMEM(out.shape, out.dtype) for n, out in enumerate(outs)]
     return pl.pallas_call(
         kernel,
         out_shape=outs,
         in_specs=[
             pl.BlockSpec(memory_space=pltpu.HBM if n in raw else pltpu.VMEM) for n in range(len(args))
         ],
-        out_specs=[pl.BlockSpec(memory_space=pltpu.VMEM)] * len(outs),
+        out_specs=[
+            pl.BlockSpec(memory_space=pltpu.HBM if n in away else pltpu.VMEM) for n in range(len(outs))
+        ],
         scratch_shapes=scratch,
         compiler_params=pltpu.CompilerParams(vmem_limit_bytes=VMEM_BYTES),
         name=name,
@@ -527,7 +537,7 @@
     sds = jax.ShapeDtypeStruct
 
     mine = volume.reshape(bx * brows, 128)
-    line = [mine] + [turned(mine, "space", dk) for dk in far_first(nk)]
+    line = [mine] + [turned(mine, "space", dk) for dk in steps_of(nk)]
     cot = cotangent.reshape(cx * lplane, cl)
     own, we, wcat = call(
         begin_kernel,
@@ -538,7 +548,7 @@
         raw=(0, 1),
     )
     line[0] = own
-    cots = [cot] + [turned(cot, "space", dk) for dk in far_first(nk)]
+    cots = [cot] + [turned(cot, "space", dk) for dk in steps_of(nk)]
 
     dims = (gx, gy, gz, lx, ly, lz, bx, by)
     hrows, edge = gx * brows, 3 * gx * gz
@@ -565,33 +575,33 @@
     send_other = turned(ready, "chan", 1)
     half_other = turned(half, "chan", 1)
     held, _ = lax.optimization_barrier((late_weight, send))
-    wl, wback = call(
+    wl, wback, wt = call(
         fetch_kernel,
-        [sds(late_weight.shape, BF), sds((9 * cl, 3 * 128), BF)],
+        [sds(late_weight.shape, BF), sds((9 * cl, 3 * 128), BF), sds((3, 9 * 128, 128), BF)],
         [pltpu.SemaphoreType.DMA((3,))],
-        [held],
+        [held, we],
         "fetch",
         raw=(0,),
     )
-    pooled_delta, back, back_mine, patch = call(
+    pooled_delta, patch = call(
         functools.partial(late_kernel, nk=nk, dims=(gx, gz, lx, ly, lz, cx)),
-        [
-            sds((lrows, 128 + cl), BF),
-            sds((lrows, 128), BF),
-            sds((lrows, 128), F32),
-            sds((gx * gz, 128), F32),
-        ],
+        [sds((lrows, 128 + cl), BF), sds((gx * gz, 128), F32)],
         [
             pltpu.VMEM((lx, lplane + 16, 128), F32),
             pltpu.VMEM((lrows, 9 * 128), BF),
-            pltpu.VMEM((lx, lplane + 16, cl), F32),
-            pltpu.VMEM((lrows, 9 * cl), BF),
             pltpu.VMEM((lrows, cl), F32),
             pltpu.VMEM((lx * gz, 128), F32),
             pltpu.VMEM((lx * 2 * lz, 128), F32),
         ],
-        [send, send_other, edges] + cots + [wl, wback],
+        [send, send_other, edges] + cots + [wl],
         "late",
+    )
+    back, back_mine = call(
+        functools.partial(late_back_kernel, dims=(lx, ly, lz)),
+        [sds((lrows, 128), BF), sds((lrows, 128), F32)],
+        [pltpu.VMEM((lx, lplane + 16, cl), F32), pltpu.VMEM((lrows, 9 * cl), BF)],
+        [pooled_delta, wback],
+        "late_back",
     )
     pd_other = turned(pooled_delta, "rep", 1)
     back_other = turned(back, "chan", 1)
@@ -615,23 +625,25 @@
         "other",
     )
     back_mine, late = lax.optimization_barrier((back_mine, late))
-    part, win = call(
+    part, win, late = call(
         functools.partial(early_grad_kernel, dims=dims),
-        [sds((27 * 128, 128), BF), sds((bx + 2, brows + 32, 128), F32)],
+        [sds((27 * 128, 128), BF), sds((bx + 2, brows + 32, 128), F32), sds(late.shape, BF)],
         [
             pltpu.VMEM((lx * ly * gz, 128), F32),
             pltpu.VMEM((gx + 2, plane + 32, 128), F32),
             pltpu.VMEM((128, (gx + 2) * plane), BF),
-        ],
-        [back_mine, back_other, slope, far_slope, patch, col],
+            pltpu.SemaphoreType.DMA(()),
+        ],
+        [back_mine, back_other, slope, far_slope, patch, col, late],
         "early_grad",
+        away=(2,),
     )
     part_other = turned(part, "rep", 1)
     (gv,) = call(
         functools.partial(grad_volume_kernel, bx=bx, brows=brows, gz=gz),
         [sds((bx * brows, 128), BF)],
-        [pltpu.VMEM(((bx + 2) * brows, 9 * 128), BF), pltpu.VMEM((3, 9 * 128, 128), BF)],
-        [win, we],
+        [pltpu.VMEM(((bx + 2) * brows, 9 * 128), BF)],
+        [win, wt],
         "grad_volume",
         far=(0,),
     )

time: 35.2 us -> 33.9 us (0.963)
  local copies, waits for them, and re-layouts: 1.98 us -> 0.77 us
  Pallas kernels: 14.6 us -> 13.6 us
  waiting for transfers between devices: 2.65 us -> 3.6 us
    unnamed x1 -> x0, local copies, waits for them, and re-layouts: 1.21 us -> none
    pallas_call x8 -> x9, Pallas kernels: 14.6 us -> 13.6 us  [call(): pl.pallas_call(kernel, out_shape=outs, in_specs=[pl.BlockSpec(memory_spac...]
    ppermute x11, waiting for transfers between devices: 2.65 us -> 3.6 us  [turned(): lax.ppermute(value, axis, [(i, i ^ by if pairs else (i + by) % count) for...]
  transfers between devices with their start and end apart: 11 -> 11, of which waited for: 2 -> 3; matrix products, arithmetic and copies ran while one was open for 6% -> 2% of each run, Pallas kernels for 35% -> 33%
where the time goes in v6:
time: 33.9 us; the launch traced here: 33.7 us
  starting transfers between devices  13.8 us (41%)
  Pallas kernels  13.6 us (40%)
  waiting for transfers between devices  3.6 us (11%)
  other arithmetic  1.2 us (4%)
  local copies, waits for them, and re-layouts  0.77 us (2%)
  between operations  0.73 us (2%)
    ppermute x11, starting transfers between devices, turned(): lax.ppermute(value, axis, [(i, i ^ by if pairs else (i + by) % count) for...  13.8 us
    pallas_call x9, Pallas kernels, call(): pl.pallas_call(kernel, out_shape=outs, in_specs=[pl.BlockSpec(memory_spac...  13.6 us
    ppermute x11, waiting for transfers between devices, turned(): lax.ppermute(value, axis, [(i, i ^ by if pairs else (i + by) % count) for...  3.6 us
    convert_element_type x1, other arithmetic, whole_sample(): early = ((part.astype(F32) + part_other.astype(F32)) * scale).astype(BF)  1.2 us
    reshape x1, local copies, waits for them, and re-layouts, whole_sample(): cot = cotangent.reshape(cx * lplane, cl)  0.77 us
  transfers between devices with their start and end apart: 11, of which 3 were waited for; matrix products, arithmetic and copies ran while one was open for 2% of the time, Pallas kernels for 33%

profile of v6, /device:TPU:0, one launch (start us, length us, event | category | flops | bytes accessed | tf_op | source)
XLA Modules:
  0.0 33.7 jit_solution(8644067961423337407)
XLA Ops:
  0.6 5.1 %collective-permute-start.2 = (bf16[256,128]{1,0:T(8,128)(2,1)}, bf16[256,128]{1,0:T(8,128)(2,1)S(1)}, u32[]{:S(2)}, u32[]{:S(2)}) collective-permute-start(bf16[256,128]{1,0:T(8,128)(2,1)} %bitcast.6), channel_id=1, source_target_pairs={{0,12},{4,8},{8,4},{12,0},{1,13},{5,9},{9,5},{13,1},{2,14},{6,10},... | collective-permute-start | bytes 196616 | tf_op jit(solution)/shard_map/ppermute | solution.py:505
  5.7 0.0 collective-permute-start.1
  5.7 0.6 %collective-permute-start = (bf16[256,128]{1,0:T(8,128)(2,1)}, bf16[256,128]{1,0:T(8,128)(2,1)S(1)}, u32[]{:S(2)}, u32[]{:S(2)}) collective-permute-start(bf16[256,128]{1,0:T(8,128)(2,1)} %bitcast.8), channel_id=1, source_target_pairs={{0,4},{4,0},{8,12},{12,8},{1,5},{5,1},{9,13},{13,9},{2,6},{6,2},{1... | collective-permute-start | bytes 196616 | tf_op jit(solution)/shard_map/ppermute | solution.py:505
  6.4 0.8 %reshape.22.refs_3_ = bf16[64,256]{1,0:T(8,128)(2,1)S(1)} reshape(bf16[1,1,16,4,256]{4,3,2,1,0:T(4,128)(2,1)} %param.7) | data formatting | bytes 65536 | tf_op jit(solution)/shard_map/reshape | solution.py:541
  7.2 3.8 %collective-permute-start.5 = (bf16[64,256]{1,0:T(8,128)(2,1)S(1)}, bf16[64,256]{1,0:T(8,128)(2,1)S(1)}, u32[]{:S(2)}, u32[]{:S(2)}) collective-permute-start(bf16[64,256]{1,0:T(8,128)(2,1)S(1)} %reshape.22.refs_3_), channel_id=1, source_target_pairs={{0,12},{4,8},{8,4},{12,0},{1,13},{5,9},{9,5},{13,1},{2,14},{6,10},... | collective-permute-start | bytes 98312 | tf_op jit(solution)/shard_map/ppermute | solution.py:505
  11.0 0.0 collective-permute-start.4
  11.0 0.0 collective-permute-done.2.refs_3_
  11.0 0.6 %collective-permute-start.3 = (bf16[64,256]{1,0:T(8,128)(2,1)S(1)}, bf16[64,256]{1,0:T(8,128)(2,1)S(1)}, u32[]{:S(2)}, u32[]{:S(2)}) collective-permute-start(bf16[64,256]{1,0:T(8,128)(2,1)S(1)} %reshape.22.refs_3_), channel_id=1, source_target_pairs={{0,4},{4,0},{8,12},{12,8},{1,5},{5,1},{9,13},{13,9},{2,6},{6,2},{1... | collective-permute-start | bytes 98312 | tf_op jit(solution)/shard_map/ppermute | solution.py:505
  11.6 1.2 %begin.1 = (bf16[256,128]{1,0:T(8,128)(2,1)S(1)}, bf16[3,3,3,128,128]{4,3,2,1,0:T(8,128)(2,1)S(1)}, bf16[1152,384]{1,0:T(8,128)(2,1)S(1)}) custom-call(bf16[256,128]{1,0:T(8,128)(2,1)} %bitcast.9, bf16[3,3,3,128,128]{4,3,2,1,0:T(8,128)(2,1)} %we_hbm.1), custom_call_target="tpu_custom_call" | custom-call | tf_op jit(solution)/shard_map/begin/pallas_call | solution.py:514
  12.9 0.0 collective-permute-done.1.refs_2_
  12.9 0.0 collective-permute-done.refs_1_
  12.9 1.8 %early.1 = (bf16[1024,128]{1,0:T(8,128)(2,1)S(1)}, f32[1024,128]{1,0:T(8,128)S(1)}, bf16[320,128]{1,0:T(8,128)(2,1)S(1)}, f32[192,128]{1,0:T(8,128)S(1)}) custom-call(bf16[256,128]{1,0:T(8,128)(2,1)S(1)} %get-tuple-element.31.refs_0_, bf16[256,128]{1,0:T(8,128)(2,1)S(1)} %collective-permute-done.refs_1_, ...), custom_call_target="tpu_custom_call" | custom-call | tf_op jit(solution)/shard_map/early/pallas_call | solution.py:514
  14.6 0.0 collective-permute-done.5.refs_6_
  14.6 1.1 %collective-permute-done.4.refs_5_ = bf16[64,256]{1,0:T(8,128)(2,1)S(1)} collective-permute-done((bf16[64,256]{1,0:T(8,128)(2,1)S(1)}, bf16[64,256]{1,0:T(8,128)(2,1)S(1)}, u32[]{:S(2)}, u32[]{:S(2)}) %collective-permute-start.4) | collective-permute-done | bytes 32800 | tf_op jit(solution)/shard_map/ppermute | solution.py:505
  15.8 0.0 collective-permute-done.3.refs_4_
  15.8 1.5 %collective-permute-start.6 = (bf16[320,128]{1,0:T(8,128)(2,1)S(1)}, bf16[320,128]{1,0:T(8,128)(2,1)S(1)}, u32[]{:S(2)}, u32[]{:S(2)}) collective-permute-start(bf16[320,128]{1,0:T(8,128)(2,1)S(1)} %get-tuple-element.34.refs_0_), channel_id=1, source_target_pairs={{0,2},{2,0},{1,3},{3,1},{4,6},{6,4},{5,7},{7,5},{8,10},{10,8},{9,1... | collective-permute-start | bytes 245768 | tf_op jit(solution)/shard_map/ppermute | solution.py:505
  17.3 0.5 %collective-permute-start.9 = (bf16[1024,128]{1,0:T(8,128)(2,1)S(1)}, bf16[1024,128]{1,0:T(8,128)(2,1)S(1)}, u32[]{:S(2)}, u32[]{:S(2)}) collective-permute-start(bf16[1024,128]{1,0:T(8,128)(2,1)S(1)} %get-tuple-element.48.half_ref), channel_id=1, source_target_pairs={{0,2},{2,0},{1,3},{3,1},{4,6},{6,4},{5,7},{7,5},{8,10},{10,8},{9,1... | collective-permute-start | bytes 786440 | tf_op jit(solution)/shard_map/ppermute | solution.py:505
  17.8 1.8 %fetch.1 = (bf16[3,3,3,128,256]{4,3,2,1,0:T(8,128)(2,1)S(1)}, bf16[2304,384]{1,0:T(8,128)(2,1)S(1)}, bf16[3,1152,128]{2,1,0:T(8,128)(2,1)S(1)}) custom-call(bf16[3,3,3,128,256]{4,3,2,1,0:T(8,128)(2,1)} %far_ref, bf16[3,3,3,128,128]{4,3,2,1,0:T(8,128)(2,1)S(1)} %get-tuple-element.40.we_ref), custom_call_target="tpu_custom_call" | custom-call | tf_op jit(solution)/shard_map/fetch/pallas_call | solution.py:514
  19.6 1.5 %collective-permute-done.6.refs_1_ = bf16[320,128]{1,0:T(8,128)(2,1)S(1)} collective-permute-done((bf16[320,128]{1,0:T(8,128)(2,1)S(1)}, bf16[320,128]{1,0:T(8,128)(2,1)S(1)}, u32[]{:S(2)}, u32[]{:S(2)}) %collective-permute-start.6) | collective-permute-done | bytes 81952 | tf_op jit(solution)/shard_map/ppermute | solution.py:505
  21.1 0.9 %late.1 = (bf16[256,384]{1,0:T(8,128)(2,1)S(1)}, f32[64,128]{1,0:T(8,128)S(1)}) custom-call(bf16[320,128]{1,0:T(8,128)(2,1)S(1)} %get-tuple-element.34.refs_0_, bf16[320,128]{1,0:T(8,128)(2,1)S(1)} %collective-permute-done.6.refs_1_, f32[192,128]{1,0:T(8,128)S(1)} %get-tuple-element.35.refs_2_, bf16[64,256]{1,0:T(8,128)(2,1)S(1)} %reshape.22.refs_3_, ...), custom_call_target="tpu_custom_call" | custom-call | tf_op jit(solution)/shard_map/late/pallas_call | solution.py:514
  22.0 0.1 collective-permute-start.7
  22.1 0.8 %late_back.1 = (bf16[256,128]{1,0:T(8,128)(2,1)S(1)}, f32[256,128]{1,0:T(8,128)S(1)}) custom-call(bf16[256,384]{1,0:T(8,128)(2,1)S(1)} %get-tuple-element.42.pd_ref.mine_ref, bf16[2304,384]{1,0:T(8,128)(2,1)S(1)} %get-tuple-element.43.wback_ref), custom_call_target="tpu_custom_call" | custom-call | tf_op jit(solution)/shard_map/late_back/pallas_call | solution.py:514
  22.9 1.2 %collective-permute-start.8 = (bf16[256,128]{1,0:T(8,128)(2,1)S(1)}, bf16[256,128]{1,0:T(8,128)(2,1)S(1)}, u32[]{:S(2)}, u32[]{:S(2)}) collective-permute-start(bf16[256,128]{1,0:T(8,128)(2,1)S(1)} %get-tuple-element.46), channel_id=1, source_target_pairs={{0,2},{2,0},{1,3},{3,1},{4,6},{6,4},{5,7},{7,5},{8,10},{10,8},{9,1... | collective-permute-start | bytes 196616 | tf_op jit(solution)/shard_map/ppermute | solution.py:505
  24.1 0.0 collective-permute-done.9.got_ref
  24.1 2.1 %other.1 = (bf16[2048,1152]{1,0:T(8,128)(2,1)S(1)}, f32[1024,128]{1,0:T(8,128)S(1)}) custom-call(bf16[1024,128]{1,0:T(8,128)(2,1)S(1)} %get-tuple-element.48.half_ref, bf16[1024,128]{1,0:T(8,128)(2,1)S(1)} %collective-permute-done.9.got_ref, bf16[1152,384]{1,0:T(8,128)(2,1)S(1)} %get-tuple-element.50.refs_4_.wcat_ref), custom_call_target="tpu_custom_call" | custom-call | tf_op jit(solution)/shard_map/other/pallas_call | solution.py:514
  26.2 0.0 collective-permute-done.7.other_ref
  26.2 1.2 %late_grad.1.late_ref = bf16[3456,256]{1,0:T(8,128)(2,1)S(1)} custom-call(bf16[256,384]{1,0:T(8,128)(2,1)S(1)} %get-tuple-element.42.pd_ref.mine_ref, bf16[256,384]{1,0:T(8,128)(2,1)S(1)} %collective-permute-done.7.other_ref), custom_call_target="tpu_custom_call" | custom-call | tf_op jit(solution)/shard_map/late_grad/pallas_call | solution.py:514
  27.5 0.0 collective-permute-done.8.other_ref
  27.5 2.5 %early_grad.1 = (bf16[3456,128]{1,0:T(8,128)(2,1)S(1)}, f32[4,160,128]{2,1,0:T(8,128)S(1)}, bf16[3456,256]{1,0:T(8,128)(2,1)}) custom-call(f32[256,128]{1,0:T(8,128)S(1)} %get-tuple-element.45.mine_ref, bf16[256,128]{1,0:T(8,128)(2,1)S(1)} %collective-permute-done.8.other_ref, f32[1024,128]{1,0:T(8,128)S(1)} %get-tuple-element.47.slope_ref, ...), custom_call_target="tpu_custom_call" | custom-call | tf_op jit(solution)/shard_map/early_grad/pallas_call | solution.py:514
  30.0 0.3 collective-permute-start.10
  30.3 1.3 %grad_volume.1 = bf16[256,128]{1,0:T(8,128)(2,1)} custom-call(f32[4,160,128]{2,1,0:T(8,128)S(1)} %get-tuple-element.57.win_ref, bf16[3,1152,128]{2,1,0:T(8,128)(2,1)S(1)} %get-tuple-element.58.wt_ref), custom_call_target="tpu_custom_call" | custom-call | tf_op jit(solution)/shard_map/grad_volume/pallas_call | solution.py:514
  31.6 1.0 %collective-permute-done.10 = bf16[3456,128]{1,0:T(8,128)(2,1)S(1)} collective-permute-done((bf16[3456,128]{1,0:T(8,128)(2,1)S(1)}, bf16[3456,128]{1,0:T(8,128)(2,1)S(1)}, u32[]{:S(2)}, u32[]{:S(2)}) %collective-permute-start.10) | collective-permute-done | bytes 884768 | tf_op jit(solution)/shard_map/ppermute | solution.py:505
  32.5 1.2 %multiply_convert_fusion = bf16[3456,128]{1,0:T(8,128)(2,1)} fusion(bf16[3456,128]{1,0:T(8,128)(2,1)S(1)} %collective-permute-done.10, bf16[3456,128]{1,0:T(8,128)(2,1)S(1)} %get-tuple-element.55), kind=kLoop, calls=%fused_computation | loop fusion | flops 2211840 | bytes 2654208 | tf_op jit(solution)/shard_map/convert_element_type | solution.py:650
Async XLA Ops:
  0.6 10.3 %collective-permute-start.2 = (bf16[256,128]{1,0:T(8,128)(2,1)}, bf16[256,128]{1,0:T(8,128)(2,1)S(1)}, u32[]{:S(2)}, u32[]{:S(2)}) collective-permute-start(bf16[256,128]{1,0:T(8,128)(2,1)} %bitcast.6), channel_id=1, source_target_pairs={{0,12},{4,8},{8,4},{12,0},{1,13},{5,9},{9,5},{13,1},{2,14},{6,10},... | collective-permute-start | bytes 196616 | tf_op jit(solution)/shard_map/ppermute | solution.py:505
  5.7 7.1 %collective-permute-start.1 = (bf16[256,128]{1,0:T(8,128)(2,1)}, bf16[256,128]{1,0:T(8,128)(2,1)S(1)}, u32[]{:S(2)}, u32[]{:S(2)}) collective-permute-start(bf16[256,128]{1,0:T(8,128)(2,1)} %bitcast.7), channel_id=1, source_target_pairs={{0,8},{4,12},{8,0},{12,4},{1,9},{5,13},{9,1},{13,5},{2,10},{6,14},... | collective-permute-start | bytes 196616 | tf_op jit(solution)/shard_map/ppermute | solution.py:505
  5.7 7.1 %collective-permute-start = (bf16[256,128]{1,0:T(8,128)(2,1)}, bf16[256,128]{1,0:T(8,128)(2,1)S(1)}, u32[]{:S(2)}, u32[]{:S(2)}) collective-permute-start(bf16[256,128]{1,0:T(8,128)(2,1)} %bitcast.8), channel_id=1, source_target_pairs={{0,4},{4,0},{8,12},{12,8},{1,5},{5,1},{9,13},{13,9},{2,6},{6,2},{1... | collective-permute-start | bytes 196616 | tf_op jit(solution)/shard_map/ppermute | solution.py:505
  7.2 7.5 %collective-permute-start.5 = (bf16[64,256]{1,0:T(8,128)(2,1)S(1)}, bf16[64,256]{1,0:T(8,128)(2,1)S(1)}, u32[]{:S(2)}, u32[]{:S(2)}) collective-permute-start(bf16[64,256]{1,0:T(8,128)(2,1)S(1)} %reshape.22.refs_3_), channel_id=1, source_target_pairs={{0,12},{4,8},{8,4},{12,0},{1,13},{5,9},{9,5},{13,1},{2,14},{6,10},... | collective-permute-start | bytes 98312 | tf_op jit(solution)/shard_map/ppermute | solution.py:505
  11.0 4.8 %collective-permute-start.4 = (bf16[64,256]{1,0:T(8,128)(2,1)S(1)}, bf16[64,256]{1,0:T(8,128)(2,1)S(1)}, u32[]{:S(2)}, u32[]{:S(2)}) collective-permute-start(bf16[64,256]{1,0:T(8,128)(2,1)S(1)} %reshape.22.refs_3_), channel_id=1, source_target_pairs={{0,8},{4,12},{8,0},{12,4},{1,9},{5,13},{9,1},{13,5},{2,10},{6,14},... | collective-permute-start | bytes 98312 | tf_op jit(solution)/shard_map/ppermute | solution.py:505
  11.0 4.8 %collective-permute-start.3 = (bf16[64,256]{1,0:T(8,128)(2,1)S(1)}, bf16[64,256]{1,0:T(8,128)(2,1)S(1)}, u32[]{:S(2)}, u32[]{:S(2)}) collective-permute-start(bf16[64,256]{1,0:T(8,128)(2,1)S(1)} %reshape.22.refs_3_), channel_id=1, source_target_pairs={{0,4},{4,0},{8,12},{12,8},{1,5},{5,1},{9,13},{13,9},{2,6},{6,2},{1... | collective-permute-start | bytes 98312 | tf_op jit(solution)/shard_map/ppermute | solution.py:505
  15.8 5.3 %collective-permute-start.6 = (bf16[320,128]{1,0:T(8,128)(2,1)S(1)}, bf16[320,128]{1,0:T(8,128)(2,1)S(1)}, u32[]{:S(2)}, u32[]{:S(2)}) collective-permute-start(bf16[320,128]{1,0:T(8,128)(2,1)S(1)} %get-tuple-element.34.refs_0_), channel_id=1, source_target_pairs={{0,2},{2,0},{1,3},{3,1},{4,6},{6,4},{5,7},{7,5},{8,10},{10,8},{9,1... | collective-permute-start | bytes 245768 | tf_op jit(solution)/shard_map/ppermute | solution.py:505
  17.3 6.8 %collective-permute-start.9 = (bf16[1024,128]{1,0:T(8,128)(2,1)S(1)}, bf16[1024,128]{1,0:T(8,128)(2,1)S(1)}, u32[]{:S(2)}, u32[]{:S(2)}) collective-permute-start(bf16[1024,128]{1,0:T(8,128)(2,1)S(1)} %get-tuple-element.48.half_ref), channel_id=1, source_target_pairs={{0,2},{2,0},{1,3},{3,1},{4,6},{6,4},{5,7},{7,5},{8,10},{10,8},{9,1... | collective-permute-start | bytes 786440 | tf_op jit(solution)/shard_map/ppermute | solution.py:505
  22.0 4.2 %collective-permute-start.7 = (bf16[256,384]{1,0:T(8,128)(2,1)S(1)}, bf16[256,384]{1,0:T(8,128)(2,1)S(1)}, u32[]{:S(2)}, u32[]{:S(2)}) collective-permute-start(bf16[256,384]{1,0:T(8,128)(2,1)S(1)} %get-tuple-element.42.pd_ref.mine_ref), channel_id=1, source_target_pairs={{0,1},{1,0},{2,3},{3,2},{4,5},{5,4},{6,7},{7,6},{8,9},{9,8},{10,11... | collective-permute-start | bytes 589832 | tf_op jit(solution)/shard_map/ppermute | solution.py:505
  22.9 4.6 %collective-permute-start.8 = (bf16[256,128]{1,0:T(8,128)(2,1)S(1)}, bf16[256,128]{1,0:T(8,128)(2,1)S(1)}, u32[]{:S(2)}, u32[]{:S(2)}) collective-permute-start(bf16[256,128]{1,0:T(8,128)(2,1)S(1)} %get-tuple-element.46), channel_id=1, source_target_pairs={{0,2},{2,0},{1,3},{3,1},{4,6},{6,4},{5,7},{7,5},{8,10},{10,8},{9,1... | collective-permute-start | bytes 196616 | tf_op jit(solution)/shard_map/ppermute | solution.py:505
  30.0 2.5 %collective-permute-start.10 = (bf16[3456,128]{1,0:T(8,128)(2,1)S(1)}, bf16[3456,128]{1,0:T(8,128)(2,1)S(1)}, u32[]{:S(2)}, u32[]{:S(2)}) collective-permute-start(bf16[3456,128]{1,0:T(8,128)(2,1)S(1)} %get-tuple-element.55), channel_id=1, source_target_pairs={{0,1},{1,0},{2,3},{3,2},{4,5},{5,4},{6,7},{7,6},{8,9},{9,8},{10,11... | collective-permute-start | bytes 2654216 | tf_op jit(solution)/shard_map/ppermute | solution.py:505

commit v7 on v6

--- a/solution.py
+++ b/solution.py
@@ -12,6 +12,7 @@
 F32 = jnp.float32
 VMEM_BYTES = 14 * 2**20
 GATHER_BLOCKS = 8
+EARLY_TAPS = 5
 
 
 def padded_2(block, sides, width):
@@ -325,7 +326,7 @@
     for n, dk in enumerate([0, *steps_of(nk)]):
         kk = partner(k, dk, nk)
         start = pl.multiple_of(kk * crow, 8)
-        cot_ref[pl.ds(start, crow), :] = cots[n][...].astype(F32)
+        cot_ref[pl.ds(start, crow), :] = cots[n][...].astype(F32).reshape(crow, cl)
     delta = (cot_ref[...] * slope).astype(BF)
     pd_ref[:, pl.ds(128, cl)] = delta
 
@@ -417,9 +418,40 @@
         slope_ref[pl.ds(x * brows, brows), :] = gelu_and_slope(pre)[1]
 
 
+def tap_terms(left_ref, col_ref, part_ref, first, count):
+    got = jnp.dot(left_ref[...], col_ref[:, pl.ds(first * 128, count * 128)], preferred_element_type=F32)
+    for a in range(3):
+        for n in range(count):
+            part_ref[pl.ds((a * count + n) * 128, 128), :] = got[
+                a * 128 : (a + 1) * 128, n * 128 : (n + 1) * 128
+            ].T.astype(part_ref.dtype)
+
+
+def more_kernel(left_ref, col_ref, part_ref):
+    tap_terms(left_ref, col_ref, part_ref, EARLY_TAPS, 9 - EARLY_TAPS)
+
+
+def finish_kernel(one_ref, one_got_ref, two_ref, two_got_ref, out_ref, sum_ref, sems, *, scale):
+    copies = []
+    for a in range(3):
+        at = a * 9 * 128
+        for mine_ref, got_ref, count in (
+            (one_ref, one_got_ref, EARLY_TAPS), (two_ref, two_got_ref, 9 - EARLY_TAPS)
+        ):
+            rows = pl.ds(a * count * 128, count * 128)
+            total = mine_ref[rows, :].astype(F32) + got_ref[rows, :].astype(F32)
+            sum_ref[pl.ds(at, count * 128), :] = (total * scale).astype(BF)
+            at += count * 128
+        rows = pl.ds(a * 9 * 128, 9 * 128)
+        copies.append(pltpu.make_async_copy(sum_ref.at[rows], out_ref.at[rows], sems.at[a]))
+        copies[-1].start()
+    for copy in copies:
+        copy.wait()
+
+
 def early_grad_kernel(
     mine_ref, other_ref, slope_ref, far_ref, patch_ref, col_ref, late_ref,
-    part_ref, win_ref, out_ref, wide_ref, d_ref, dt_ref, sem, *, dims
+    part_ref, win_ref, out_ref, left_ref, wide_ref, d_ref, sem, *, dims
 ):
     leave = pltpu.make_async_copy(late_ref, out_ref, sem)
     leave.start()
@@ -427,14 +459,14 @@
     plane, lplane = gy * gz, ly * lz
     k, j = lax.axis_index("space"), lax.axis_index("chan")
     brows = by * gz
-    span = (gx + 2) * brows
+    half = gx * brows
     for q in (0, gx + 1):
         d_ref[q] = jnp.zeros(d_ref.shape[1:], F32)
     d_ref[:, pl.ds(0, 16), :] = jnp.zeros((gx + 2, 16, 128), F32)
     d_ref[:, pl.ds(16 + plane, 16), :] = jnp.zeros((gx + 2, 16, 128), F32)
     for h in (0, 1):
-        dt_ref[:, pl.ds(h * span, brows)] = jnp.zeros((128, brows), BF)
-        dt_ref[:, pl.ds((h + 1) * span - brows, brows)] = jnp.zeros((128, brows), BF)
+        left_ref[pl.ds(0, 128), pl.ds((h + 1) * half - brows, brows)] = jnp.zeros((128, brows), BF)
+        left_ref[pl.ds(2 * 128, 128), pl.ds(h * half, brows)] = jnp.zeros((128, brows), BF)
     back = (mine_ref[...] + other_ref[...].astype(F32)) * 0.125
     wide_ref[pl.ds(0, lx * lplane, stride=2), :] = back
     wide_ref[pl.ds(1, lx * lplane, stride=2), :] = back
@@ -453,22 +485,11 @@
                     slope = jnp.where(border, tiles, slope)
                 delta = (rows * slope).astype(BF).astype(F32)
                 d_ref[x + 1, pl.ds(pl.multiple_of(16 + side * brows, 8), brows), :] = delta
-                dt_ref[:, pl.ds(h * span + (x + 1) * brows, brows)] = delta.T.astype(BF)
-    left = jnp.concatenate(
-        [
-            jnp.concatenate(
-                [dt_ref[:, pl.ds(h * span + (2 - a) * brows, gx * brows)] for h in (0, 1)], axis=1
-            )
-            for a in range(3)
-        ],
-        axis=0,
-    )
-    got = jnp.dot(left, col_ref[...], preferred_element_type=F32)
-    for a in range(3):
-        for n in range(9):
-            part_ref[pl.ds((a * 9 + n) * 128, 128), :] = got[
-                a * 128 : (a + 1) * 128, n * 128 : (n + 1) * 128
-            ].T.astype(part_ref.dtype)
+                tile = delta.T.astype(BF)
+                for a in range(3):
+                    if 0 <= x + a - 1 < gx:
+                        left_ref[pl.ds(a * 128, 128), pl.ds(h * half + (x + a - 1) * brows, brows)] = tile
+    tap_terms(left_ref, col_ref, part_ref, 0, EARLY_TAPS)
     row = pl.multiple_of(j * brows, 8)
     for q in range(bx + 2):
         win_ref[q] = d_ref[k * bx + q, pl.ds(row, brows + 32), :]
@@ -538,7 +559,7 @@
 
     mine = volume.reshape(bx * brows, 128)
     line = [mine] + [turned(mine, "space", dk) for dk in steps_of(nk)]
-    cot = cotangent.reshape(cx * lplane, cl)
+    cot = cotangent.reshape(cx * ly, lz, cl)
     own, we, wcat = call(
         begin_kernel,
         [sds(mine.shape, BF), sds(early_weight.shape, BF), sds((9 * 128, 3 * 128), BF)],
@@ -616,7 +637,7 @@
         [pooled_delta, pd_other],
         "late_grad",
     )
-    half_other, wcat, _ = lax.optimization_barrier((half_other, wcat, back))
+    half_other, wcat, _, late = lax.optimization_barrier((half_other, wcat, back, late))
     col, far_slope = call(
         functools.partial(other_kernel, dims=dims),
         [sds((rows, 9 * 128), BF), sds((hrows, 128), F32)],
@@ -625,13 +646,17 @@
         "other",
     )
     back_mine, late = lax.optimization_barrier((back_mine, late))
-    part, win, late = call(
+    part, win, late, left = call(
         functools.partial(early_grad_kernel, dims=dims),
-        [sds((27 * 128, 128), BF), sds((bx + 2, brows + 32, 128), F32), sds(late.shape, BF)],
+        [
+            sds((3 * EARLY_TAPS * 128, 128), BF),
+            sds((bx + 2, brows + 32, 128), F32),
+            sds(late.shape, BF),
+            sds((3 * 128, rows), BF),
+        ],
         [
             pltpu.VMEM((lx * ly * gz, 128), F32),
             pltpu.VMEM((gx + 2, plane + 32, 128), F32),
-            pltpu.VMEM((128, (gx + 2) * plane), BF),
             pltpu.SemaphoreType.DMA(()),
         ],
         [back_mine, back_other, slope, far_slope, patch, col, late],
@@ -639,6 +664,9 @@
         away=(2,),
     )
     part_other = turned(part, "rep", 1)
+    (more,) = call(more_kernel, [sds((3 * (9 - EARLY_TAPS) * 128, 128), BF)], [], [left, col], "more")
+    more_other = turned(more, "rep", 1)
+    win, _ = lax.optimization_barrier((win, more))
     (gv,) = call(
         functools.partial(grad_volume_kernel, bx=bx, brows=brows, gz=gz),
         [sds((bx * brows, 128), BF)],
@@ -647,7 +675,14 @@
         "grad_volume",
         far=(0,),
     )
-    early = ((part.astype(F32) + part_other.astype(F32)) * scale).astype(BF)
+    (early,) = call(
+        functools.partial(finish_kernel, scale=scale),
+        [sds((27 * 128, 128), BF)],
+        [pltpu.VMEM((27 * 128, 128), BF), pltpu.SemaphoreType.DMA((3,))],
+        [part, part_other, more, more_other],
+        "finish",
+        away=(0,),
+    )
     return (
         early.reshape(3, 3, 3, 128, 128),
         late.reshape(3, 3, 3, 128, cl),

time: 33.9 us -> 33.4 us (0.985)
  Pallas kernels: 13.6 us -> 15 us
  other arithmetic: 1.2 us -> 0 us
  starting transfers between devices: 13.8 us -> 14.9 us
  waiting for transfers between devices: 3.6 us -> 2.65 us
  local copies, waits for them, and re-layouts: 0.77 us -> 0.01 us
    pallas_call x9 -> x11, Pallas kernels: 13.6 us -> 15 us  [call(): pl.pallas_call(kernel, out_shape=outs, in_specs=[pl.BlockSpec(memory_spac...]
    convert_element_type x1 -> x0, other arithmetic: 1.2 us -> none  [whole_sample(): early = ((part.astype(F32) + part_other.astype(F32)) * scale).astype(BF)]
    ppermute x11 -> x12, starting transfers between devices: 13.8 us -> 14.9 us  [turned(): lax.ppermute(value, axis, [(i, i ^ by if pairs else (i + by) % count) for...]
    ppermute x11 -> x12, waiting for transfers between devices: 3.6 us -> 2.65 us  [turned(): lax.ppermute(value, axis, [(i, i ^ by if pairs else (i + by) % count) for...]
    reshape x1 -> x0, local copies, waits for them, and re-layouts: 0.77 us -> none  [whole_sample(): cot = cotangent.reshape(cx * lplane, cl)]
  transfers between devices with their start and end apart: 11 -> 12, of which waited for: 3 -> 4; matrix products, arithmetic and copies ran while one was open for 2% -> 0% of each run, Pallas kernels for 33% -> 37%
where the time goes in v7:
time: 33.4 us; the launch traced here: 33.2 us
  Pallas kernels  15 us (45%)
  starting transfers between devices  14.9 us (45%)
  waiting for transfers between devices  2.65 us (8%)
  between operations  0.73 us (2%)
    pallas_call x11, Pallas kernels, call(): pl.pallas_call(kernel, out_shape=outs, in_specs=[pl.BlockSpec(memory_spac...  15 us
    ppermute x12, starting transfers between devices, turned(): lax.ppermute(value, axis, [(i, i ^ by if pairs else (i + by) % count) for...  14.9 us
    ppermute x12, waiting for transfers between devices, turned(): lax.ppermute(value, axis, [(i, i ^ by if pairs else (i + by) % count) for...  2.65 us
  transfers between devices with their start and end apart: 12, of which 4 were waited for; matrix products, arithmetic and copies ran while one was open for 0% of the time, Pallas kernels for 37%

profile of v7, /device:TPU:0, one launch (start us, length us, event | category | flops | bytes accessed | tf_op | source)
XLA Modules:
  0.0 33.2 jit_solution(15844326202992400025)
XLA Ops:
  0.6 5.1 %collective-permute-start.2 = (bf16[256,128]{1,0:T(8,128)(2,1)}, bf16[256,128]{1,0:T(8,128)(2,1)S(1)}, u32[]{:S(2)}, u32[]{:S(2)}) collective-permute-start(bf16[256,128]{1,0:T(8,128)(2,1)} %bitcast.11), channel_id=1, source_target_pairs={{0,12},{4,8},{8,4},{12,0},{1,13},{5,9},{9,5},{13,1},{2,14},{6,10},... | collective-permute-start | bytes 196616 | tf_op jit(solution)/shard_map/ppermute | solution.py:526
  5.7 0.0 collective-permute-start.1
  5.7 0.6 %collective-permute-start = (bf16[256,128]{1,0:T(8,128)(2,1)}, bf16[256,128]{1,0:T(8,128)(2,1)S(1)}, u32[]{:S(2)}, u32[]{:S(2)}) collective-permute-start(bf16[256,128]{1,0:T(8,128)(2,1)} %bitcast.13), channel_id=1, source_target_pairs={{0,4},{4,0},{8,12},{12,8},{1,5},{5,1},{9,13},{13,9},{2,6},{6,2},{1... | collective-permute-start | bytes 196616 | tf_op jit(solution)/shard_map/ppermute | solution.py:526
  6.4 3.7 %collective-permute-start.5 = (bf16[16,4,256]{2,1,0:T(4,128)(2,1)}, bf16[16,4,256]{2,1,0:T(4,128)(2,1)S(1)}, u32[]{:S(2)}, u32[]{:S(2)}) collective-permute-start(bf16[16,4,256]{2,1,0:T(4,128)(2,1)} %bitcast.5), channel_id=1, source_target_pairs={{0,12},{4,8},{8,4},{12,0},{1,13},{5,9},{9,5},{13,1},{2,14},{6,10},... | collective-permute-start | bytes 98312 | tf_op jit(solution)/shard_map/ppermute | solution.py:526
  10.1 0.0 collective-permute-start.4
  10.1 0.0 collective-permute-done.2.refs_3_
  10.1 1.0 %collective-permute-start.3 = (bf16[16,4,256]{2,1,0:T(4,128)(2,1)}, bf16[16,4,256]{2,1,0:T(4,128)(2,1)S(1)}, u32[]{:S(2)}, u32[]{:S(2)}) collective-permute-start(bf16[16,4,256]{2,1,0:T(4,128)(2,1)} %bitcast.7), channel_id=1, source_target_pairs={{0,4},{4,0},{8,12},{12,8},{1,5},{5,1},{9,13},{13,9},{2,6},{6,2},{1... | collective-permute-start | bytes 98312 | tf_op jit(solution)/shard_map/ppermute | solution.py:526
  11.2 1.2 %begin.1 = (bf16[256,128]{1,0:T(8,128)(2,1)S(1)}, bf16[3,3,3,128,128]{4,3,2,1,0:T(8,128)(2,1)S(1)}, bf16[1152,384]{1,0:T(8,128)(2,1)S(1)}) custom-call(bf16[256,128]{1,0:T(8,128)(2,1)} %bitcast.14, bf16[3,3,3,128,128]{4,3,2,1,0:T(8,128)(2,1)} %we_hbm.1), custom_call_target="tpu_custom_call" | custom-call | tf_op jit(solution)/shard_map/begin/pallas_call | solution.py:535
  12.4 0.2 collective-permute-done.1.refs_2_
  12.6 0.0 collective-permute-done.refs_1_
  12.6 0.0 copy-start
  12.6 1.8 %early.1 = (bf16[1024,128]{1,0:T(8,128)(2,1)S(1)}, f32[1024,128]{1,0:T(8,128)S(1)}, bf16[320,128]{1,0:T(8,128)(2,1)S(1)}, f32[192,128]{1,0:T(8,128)S(1)}) custom-call(bf16[256,128]{1,0:T(8,128)(2,1)S(1)} %get-tuple-element.34.refs_0_, bf16[256,128]{1,0:T(8,128)(2,1)S(1)} %collective-permute-done.refs_1_, ...), custom_call_target="tpu_custom_call" | custom-call | tf_op jit(solution)/shard_map/early/pallas_call | solution.py:535
  14.4 0.0 collective-permute-done.5.refs_6_
  14.4 0.8 %collective-permute-done.4.refs_5_ = bf16[16,4,256]{2,1,0:T(4,128)(2,1)S(1)} collective-permute-done((bf16[16,4,256]{2,1,0:T(4,128)(2,1)}, bf16[16,4,256]{2,1,0:T(4,128)(2,1)S(1)}, u32[]{:S(2)}, u32[]{:S(2)}) %collective-permute-start.4) | collective-permute-done | bytes 32800 | tf_op jit(solution)/shard_map/ppermute | solution.py:526
  15.2 0.0 collective-permute-done.3.refs_4_
  15.2 1.5 %collective-permute-start.6 = (bf16[320,128]{1,0:T(8,128)(2,1)S(1)}, bf16[320,128]{1,0:T(8,128)(2,1)S(1)}, u32[]{:S(2)}, u32[]{:S(2)}) collective-permute-start(bf16[320,128]{1,0:T(8,128)(2,1)S(1)} %get-tuple-element.37.refs_0_), channel_id=1, source_target_pairs={{0,2},{2,0},{1,3},{3,1},{4,6},{6,4},{5,7},{7,5},{8,10},{10,8},{9,1... | collective-permute-start | bytes 245768 | tf_op jit(solution)/shard_map/ppermute | solution.py:526
  16.7 0.5 %collective-permute-start.7 = (bf16[1024,128]{1,0:T(8,128)(2,1)S(1)}, bf16[1024,128]{1,0:T(8,128)(2,1)S(1)}, u32[]{:S(2)}, u32[]{:S(2)}) collective-permute-start(bf16[1024,128]{1,0:T(8,128)(2,1)S(1)} %get-tuple-element.48.half_ref), channel_id=1, source_target_pairs={{0,2},{2,0},{1,3},{3,1},{4,6},{6,4},{5,7},{7,5},{8,10},{10,8},{9,1... | collective-permute-start | bytes 786440 | tf_op jit(solution)/shard_map/ppermute | solution.py:526
  17.2 1.8 %fetch.1 = (bf16[3,3,3,128,256]{4,3,2,1,0:T(8,128)(2,1)S(1)}, bf16[2304,384]{1,0:T(8,128)(2,1)S(1)}, bf16[3,1152,128]{2,1,0:T(8,128)(2,1)S(1)}) custom-call(bf16[3,3,3,128,256]{4,3,2,1,0:T(8,128)(2,1)} %far_ref, bf16[3,3,3,128,128]{4,3,2,1,0:T(8,128)(2,1)S(1)} %get-tuple-element.43.we_ref), custom_call_target="tpu_custom_call" | custom-call | tf_op jit(solution)/shard_map/fetch/pallas_call | solution.py:535
  19.0 1.5 %collective-permute-done.6.refs_1_ = bf16[320,128]{1,0:T(8,128)(2,1)S(1)} collective-permute-done((bf16[320,128]{1,0:T(8,128)(2,1)S(1)}, bf16[320,128]{1,0:T(8,128)(2,1)S(1)}, u32[]{:S(2)}, u32[]{:S(2)}) %collective-permute-start.6) | collective-permute-done | bytes 81952 | tf_op jit(solution)/shard_map/ppermute | solution.py:526
  20.5 0.0 copy-done
  20.5 0.9 %late.1 = (bf16[256,384]{1,0:T(8,128)(2,1)S(1)}, f32[64,128]{1,0:T(8,128)S(1)}) custom-call(bf16[320,128]{1,0:T(8,128)(2,1)S(1)} %get-tuple-element.37.refs_0_, bf16[320,128]{1,0:T(8,128)(2,1)S(1)} %collective-permute-done.6.refs_1_, f32[192,128]{1,0:T(8,128)S(1)} %get-tuple-element.38.refs_2_, bf16[16,4,256]{2,1,0:T(4,128)(2,1)S(1)} %bitcast.8, ...), custom_call_target="tpu_custom_call" | custom-call | tf_op jit(solution)/shard_map/late/pallas_call | solution.py:535
  21.4 0.1 collective-permute-start.8
  21.5 0.8 %late_back.1 = (bf16[256,128]{1,0:T(8,128)(2,1)S(1)}, f32[256,128]{1,0:T(8,128)S(1)}) custom-call(bf16[256,384]{1,0:T(8,128)(2,1)S(1)} %get-tuple-element.45.pd_ref.mine_ref, bf16[2304,384]{1,0:T(8,128)(2,1)S(1)} %get-tuple-element.46.wback_ref), custom_call_target="tpu_custom_call" | custom-call | tf_op jit(solution)/shard_map/late_back/pallas_call | solution.py:535
  22.2 1.6 %collective-permute-start.9 = (bf16[256,128]{1,0:T(8,128)(2,1)S(1)}, bf16[256,128]{1,0:T(8,128)(2,1)S(1)}, u32[]{:S(2)}, u32[]{:S(2)}) collective-permute-start(bf16[256,128]{1,0:T(8,128)(2,1)S(1)} %get-tuple-element.49), channel_id=1, source_target_pairs={{0,2},{2,0},{1,3},{3,1},{4,6},{6,4},{5,7},{7,5},{8,10},{10,8},{9,1... | collective-permute-start | bytes 196616 | tf_op jit(solution)/shard_map/ppermute | solution.py:526
  23.9 0.0 collective-permute-done.8.other_ref
  23.9 1.2 %late_grad.1.late_ref = bf16[3456,256]{1,0:T(8,128)(2,1)S(1)} custom-call(bf16[256,384]{1,0:T(8,128)(2,1)S(1)} %get-tuple-element.45.pd_ref.mine_ref, bf16[256,384]{1,0:T(8,128)(2,1)S(1)} %collective-permute-done.8.other_ref), custom_call_target="tpu_custom_call" | custom-call | tf_op jit(solution)/shard_map/late_grad/pallas_call | solution.py:535
  25.1 0.0 collective-permute-done.7.got_ref
  25.1 2.1 %other.1 = (bf16[2048,1152]{1,0:T(8,128)(2,1)S(1)}, f32[1024,128]{1,0:T(8,128)S(1)}) custom-call(bf16[1024,128]{1,0:T(8,128)(2,1)S(1)} %get-tuple-element.48.half_ref, bf16[1024,128]{1,0:T(8,128)(2,1)S(1)} %collective-permute-done.7.got_ref, bf16[1152,384]{1,0:T(8,128)(2,1)S(1)} %get-tuple-element.54.refs_4_.wcat_ref), custom_call_target="tpu_custom_call" | custom-call | tf_op jit(solution)/shard_map/other/pallas_call | solution.py:535
  27.3 0.0 collective-permute-done.9.other_ref
  27.3 1.8 %early_grad.1 = (bf16[1920,128]{1,0:T(8,128)(2,1)S(1)}, f32[4,160,128]{2,1,0:T(8,128)S(1)}, bf16[3456,256]{1,0:T(8,128)(2,1)}, bf16[384,2048]{1,0:T(8,128)(2,1)S(1)}) custom-call(f32[256,128]{1,0:T(8,128)S(1)} %get-tuple-element.51.mine_ref, bf16[256,128]{1,0:T(8,128)(2,1)S(1)} %collective-permute-done.9.other_ref, ...), custom_call_target="tpu_custom_call" | custom-call | tf_op jit(solution)/shard_map/early_grad/pallas_call | solution.py:535
  29.1 0.3 collective-permute-start.10
  29.4 1.0 %more.1.two_ref = bf16[1536,128]{1,0:T(8,128)(2,1)S(1)} custom-call(bf16[384,2048]{1,0:T(8,128)(2,1)S(1)} %get-tuple-element.60.left_ref, bf16[2048,1152]{1,0:T(8,128)(2,1)S(1)} %get-tuple-element.57.col_ref), custom_call_target="tpu_custom_call" | custom-call | tf_op jit(solution)/shard_map/more/pallas_call | solution.py:535
  30.4 0.4 %collective-permute-start.11 = (bf16[1536,128]{1,0:T(8,128)(2,1)S(1)}, bf16[1536,128]{1,0:T(8,128)(2,1)S(1)}, u32[]{:S(2)}, u32[]{:S(2)}) collective-permute-start(bf16[1536,128]{1,0:T(8,128)(2,1)S(1)} %more.1.two_ref), channel_id=1, source_target_pairs={{0,1},{1,0},{2,3},{3,2},{4,5},{5,4},{6,7},{7,6},{8,9},{9,8},{10,11... | collective-permute-start | bytes 1179656 | tf_op jit(solution)/shard_map/ppermute | solution.py:526
  30.8 1.3 %grad_volume.1 = bf16[256,128]{1,0:T(8,128)(2,1)} custom-call(f32[4,160,128]{2,1,0:T(8,128)S(1)} %get-tuple-element.63.win_ref, bf16[3,1152,128]{2,1,0:T(8,128)(2,1)S(1)} %get-tuple-element.64.wt_ref), custom_call_target="tpu_custom_call" | custom-call | tf_op jit(solution)/shard_map/grad_volume/pallas_call | solution.py:535
  32.0 0.2 collective-permute-done.11.two_got_ref
  32.2 0.0 collective-permute-done.10.one_got_ref
  32.2 1.0 %finish.1 = bf16[3456,128]{1,0:T(8,128)(2,1)} custom-call(bf16[1920,128]{1,0:T(8,128)(2,1)S(1)} %get-tuple-element.59.one_ref, bf16[1920,128]{1,0:T(8,128)(2,1)S(1)} %collective-permute-done.10.one_got_ref, bf16[1536,128]{1,0:T(8,128)(2,1)S(1)} %more.1.two_ref, bf16[1536,128]{1,0:T(8,128)(2,1)S(1)} %collective-permute-done.11.two_got_ref), custom_call_target="tpu_custom_call" | custom-call | tf_op jit(solution)/shard_map/finish/pallas_call | solution.py:535
Async XLA Ops:
  0.6 9.5 %collective-permute-start.2 = (bf16[256,128]{1,0:T(8,128)(2,1)}, bf16[256,128]{1,0:T(8,128)(2,1)S(1)}, u32[]{:S(2)}, u32[]{:S(2)}) collective-permute-start(bf16[256,128]{1,0:T(8,128)(2,1)} %bitcast.11), channel_id=1, source_target_pairs={{0,12},{4,8},{8,4},{12,0},{1,13},{5,9},{9,5},{13,1},{2,14},{6,10},... | collective-permute-start | bytes 196616 | tf_op jit(solution)/shard_map/ppermute | solution.py:526
  5.7 6.9 %collective-permute-start.1 = (bf16[256,128]{1,0:T(8,128)(2,1)}, bf16[256,128]{1,0:T(8,128)(2,1)S(1)}, u32[]{:S(2)}, u32[]{:S(2)}) collective-permute-start(bf16[256,128]{1,0:T(8,128)(2,1)} %bitcast.12), channel_id=1, source_target_pairs={{0,8},{4,12},{8,0},{12,4},{1,9},{5,13},{9,1},{13,5},{2,10},{6,14},... | collective-permute-start | bytes 196616 | tf_op jit(solution)/shard_map/ppermute | solution.py:526
  5.7 6.9 %collective-permute-start = (bf16[256,128]{1,0:T(8,128)(2,1)}, bf16[256,128]{1,0:T(8,128)(2,1)S(1)}, u32[]{:S(2)}, u32[]{:S(2)}) collective-permute-start(bf16[256,128]{1,0:T(8,128)(2,1)} %bitcast.13), channel_id=1, source_target_pairs={{0,4},{4,0},{8,12},{12,8},{1,5},{5,1},{9,13},{13,9},{2,6},{6,2},{1... | collective-permute-start | bytes 196616 | tf_op jit(solution)/shard_map/ppermute | solution.py:526
  6.4 8.0 %collective-permute-start.5 = (bf16[16,4,256]{2,1,0:T(4,128)(2,1)}, bf16[16,4,256]{2,1,0:T(4,128)(2,1)S(1)}, u32[]{:S(2)}, u32[]{:S(2)}) collective-permute-start(bf16[16,4,256]{2,1,0:T(4,128)(2,1)} %bitcast.5), channel_id=1, source_target_pairs={{0,12},{4,8},{8,4},{12,0},{1,13},{5,9},{9,5},{13,1},{2,14},{6,10},... | collective-permute-start | bytes 98312 | tf_op jit(solution)/shard_map/ppermute | solution.py:526
  10.1 5.0 %collective-permute-start.4 = (bf16[16,4,256]{2,1,0:T(4,128)(2,1)}, bf16[16,4,256]{2,1,0:T(4,128)(2,1)S(1)}, u32[]{:S(2)}, u32[]{:S(2)}) collective-permute-start(bf16[16,4,256]{2,1,0:T(4,128)(2,1)} %bitcast.6), channel_id=1, source_target_pairs={{0,8},{4,12},{8,0},{12,4},{1,9},{5,13},{9,1},{13,5},{2,10},{6,14},... | collective-permute-start | bytes 98312 | tf_op jit(solution)/shard_map/ppermute | solution.py:526
  10.1 5.0 %collective-permute-start.3 = (bf16[16,4,256]{2,1,0:T(4,128)(2,1)}, bf16[16,4,256]{2,1,0:T(4,128)(2,1)S(1)}, u32[]{:S(2)}, u32[]{:S(2)}) collective-permute-start(bf16[16,4,256]{2,1,0:T(4,128)(2,1)} %bitcast.7), channel_id=1, source_target_pairs={{0,4},{4,0},{8,12},{12,8},{1,5},{5,1},{9,13},{13,9},{2,6},{6,2},{1... | collective-permute-start | bytes 98312 | tf_op jit(solution)/shard_map/ppermute | solution.py:526
  12.6 7.8 %copy-start = (bf16[1,1,16,4,256]{4,3,2,1,0:T(4,128)(2,1)S(1)}, bf16[1,1,16,4,256]{4,3,2,1,0:T(4,128)(2,1)}, u32[]{:S(2)}) copy-start(bf16[1,1,16,4,256]{4,3,2,1,0:T(4,128)(2,1)} %param.7) | copy-start | bytes 98308
  15.2 5.3 %collective-permute-start.6 = (bf16[320,128]{1,0:T(8,128)(2,1)S(1)}, bf16[320,128]{1,0:T(8,128)(2,1)S(1)}, u32[]{:S(2)}, u32[]{:S(2)}) collective-permute-start(bf16[320,128]{1,0:T(8,128)(2,1)S(1)} %get-tuple-element.37.refs_0_), channel_id=1, source_target_pairs={{0,2},{2,0},{1,3},{3,1},{4,6},{6,4},{5,7},{7,5},{8,10},{10,8},{9,1... | collective-permute-start | bytes 245768 | tf_op jit(solution)/shard_map/ppermute | solution.py:526
  16.7 8.5 %collective-permute-start.7 = (bf16[1024,128]{1,0:T(8,128)(2,1)S(1)}, bf16[1024,128]{1,0:T(8,128)(2,1)S(1)}, u32[]{:S(2)}, u32[]{:S(2)}) collective-permute-start(bf16[1024,128]{1,0:T(8,128)(2,1)S(1)} %get-tuple-element.48.half_ref), channel_id=1, source_target_pairs={{0,2},{2,0},{1,3},{3,1},{4,6},{6,4},{5,7},{7,5},{8,10},{10,8},{9,1... | collective-permute-start | bytes 786440 | tf_op jit(solution)/shard_map/ppermute | solution.py:526
  21.4 2.5 %collective-permute-start.8 = (bf16[256,384]{1,0:T(8,128)(2,1)S(1)}, bf16[256,384]{1,0:T(8,128)(2,1)S(1)}, u32[]{:S(2)}, u32[]{:S(2)}) collective-permute-start(bf16[256,384]{1,0:T(8,128)(2,1)S(1)} %get-tuple-element.45.pd_ref.mine_ref), channel_id=1, source_target_pairs={{0,1},{1,0},{2,3},{3,2},{4,5},{5,4},{6,7},{7,6},{8,9},{9,8},{10,11... | collective-permute-start | bytes 589832 | tf_op jit(solution)/shard_map/ppermute | solution.py:526
  22.2 5.0 %collective-permute-start.9 = (bf16[256,128]{1,0:T(8,128)(2,1)S(1)}, bf16[256,128]{1,0:T(8,128)(2,1)S(1)}, u32[]{:S(2)}, u32[]{:S(2)}) collective-permute-start(bf16[256,128]{1,0:T(8,128)(2,1)S(1)} %get-tuple-element.49), channel_id=1, source_target_pairs={{0,2},{2,0},{1,3},{3,1},{4,6},{6,4},{5,7},{7,5},{8,10},{10,8},{9,1... | collective-permute-start | bytes 196616 | tf_op jit(solution)/shard_map/ppermute | solution.py:526
  29.1 3.1 %collective-permute-start.10 = (bf16[1920,128]{1,0:T(8,128)(2,1)S(1)}, bf16[1920,128]{1,0:T(8,128)(2,1)S(1)}, u32[]{:S(2)}, u32[]{:S(2)}) collective-permute-start(bf16[1920,128]{1,0:T(8,128)(2,1)S(1)} %get-tuple-element.59.one_ref), channel_id=1, source_target_pairs={{0,1},{1,0},{2,3},{3,2},{4,5},{5,4},{6,7},{7,6},{8,9},{9,8},{10,11... | collective-permute-start | bytes 1474568 | tf_op jit(solution)/shard_map/ppermute | solution.py:526
  30.4 1.8 %collective-permute-start.11 = (bf16[1536,128]{1,0:T(8,128)(2,1)S(1)}, bf16[1536,128]{1,0:T(8,128)(2,1)S(1)}, u32[]{:S(2)}, u32[]{:S(2)}) collective-permute-start(bf16[1536,128]{1,0:T(8,128)(2,1)S(1)} %more.1.two_ref), channel_id=1, source_target_pairs={{0,1},{1,0},{2,3},{3,2},{4,5},{5,4},{6,7},{7,6},{8,9},{9,8},{10,11... | collective-permute-start | bytes 1179656 | tf_op jit(solution)/shard_map/ppermute | solution.py:526

commit v8 on v7

--- a/solution.py
+++ b/solution.py
@@ -569,7 +569,8 @@
         raw=(0, 1),
     )
     line[0] = own
-    cots = [cot] + [turned(cot, "space", dk) for dk in steps_of(nk)]
+    late_steps = [dk for dk in range(1, nk) if nk & (nk - 1) == 0 and dk & (dk - 1)]
+    cots = {dk: turned(cot, "space", dk) for dk in steps_of(nk) if dk not in late_steps}
 
     dims = (gx, gy, gz, lx, ly, lz, bx, by)
     hrows, edge = gx * brows, 3 * gx * gz
@@ -592,9 +593,13 @@
         line + [wcat],
         "early",
     )
-    ready, *cots[1:] = lax.optimization_barrier((send, *cots[1:]))
+    ready, cots = lax.optimization_barrier((send, cots))
     send_other = turned(ready, "chan", 1)
     half_other = turned(half, "chan", 1)
+    for dk in late_steps:
+        low = dk & -dk
+        cots[dk] = turned(cots[dk ^ low], "space", low)
+    cots = [cot] + [cots[dk] for dk in steps_of(nk)]
     held, _ = lax.optimization_barrier((late_weight, send))
     wl, wback, wt = call(
         fetch_kernel,

time: 33.4 us -> 32.8 us (0.982)
  waiting for transfers between devices: 2.65 us -> 1.53 us
  starting transfers between devices: 14.9 us -> 15.4 us
    ppermute x12, waiting for transfers between devices: 2.65 us -> 1.53 us  [turned(): lax.ppermute(value, axis, [(i, i ^ by if pairs else (i + by) % count) for...]
    ppermute x12, starting transfers between devices: 14.9 us -> 15.4 us  [turned(): lax.ppermute(value, axis, [(i, i ^ by if pairs else (i + by) % count) for...]
  transfers between devices with their start and end apart: 12 -> 12, of which waited for: 4 -> 3; matrix products, arithmetic and copies ran while one was open for 0% -> 0% of each run, Pallas kernels for 37% -> 37%
where the time goes in v8:
time: 32.8 us; the launch traced here: 32.7 us
  starting transfers between devices  15.4 us (47%)
  Pallas kernels  15 us (46%)
  waiting for transfers between devices  1.53 us (5%)
  between operations  0.74 us (2%)
    ppermute x12, starting transfers between devices, turned(): lax.ppermute(value, axis, [(i, i ^ by if pairs else (i + by) % count) for...  15.4 us
    pallas_call x11, Pallas kernels, call(): pl.pallas_call(kernel, out_shape=outs, in_specs=[pl.BlockSpec(memory_spac...  15 us
    ppermute x12, waiting for transfers between devices, turned(): lax.ppermute(value, axis, [(i, i ^ by if pairs else (i + by) % count) for...  1.53 us
  transfers between devices with their start and end apart: 12, of which 3 were waited for; matrix products, arithmetic and copies ran while one was open for 0% of the time, Pallas kernels for 37%

profile of v8, /device:TPU:0, one launch (start us, length us, event | category | flops | bytes accessed | tf_op | source)
XLA Modules:
  0.0 32.7 jit_solution(4428241743488478324)
XLA Ops:
  0.6 5.1 %collective-permute-start.2 = (bf16[256,128]{1,0:T(8,128)(2,1)}, bf16[256,128]{1,0:T(8,128)(2,1)S(1)}, u32[]{:S(2)}, u32[]{:S(2)}) collective-permute-start(bf16[256,128]{1,0:T(8,128)(2,1)} %bitcast.10), channel_id=1, source_target_pairs={{0,12},{4,8},{8,4},{12,0},{1,13},{5,9},{9,5},{13,1},{2,14},{6,10},... | collective-permute-start | bytes 196616 | tf_op jit(solution)/shard_map/ppermute | solution.py:526
  5.7 0.0 collective-permute-start.1
  5.7 0.6 %collective-permute-start = (bf16[256,128]{1,0:T(8,128)(2,1)}, bf16[256,128]{1,0:T(8,128)(2,1)S(1)}, u32[]{:S(2)}, u32[]{:S(2)}) collective-permute-start(bf16[256,128]{1,0:T(8,128)(2,1)} %bitcast.12), channel_id=1, source_target_pairs={{0,4},{4,0},{8,12},{12,8},{1,5},{5,1},{9,13},{13,9},{2,6},{6,2},{1... | collective-permute-start | bytes 196616 | tf_op jit(solution)/shard_map/ppermute | solution.py:526
  6.4 2.3 %collective-permute-start.4 = (bf16[16,4,256]{2,1,0:T(4,128)(2,1)}, bf16[16,4,256]{2,1,0:T(4,128)(2,1)S(1)}, u32[]{:S(2)}, u32[]{:S(2)}) collective-permute-start(bf16[16,4,256]{2,1,0:T(4,128)(2,1)} %bitcast.5), channel_id=1, source_target_pairs={{0,8},{4,12},{8,0},{12,4},{1,9},{5,13},{9,1},{13,5},{2,10},{6,14},... | collective-permute-start | bytes 98312 | tf_op jit(solution)/shard_map/ppermute | solution.py:526
  8.7 2.0 %collective-permute-start.3 = (bf16[16,4,256]{2,1,0:T(4,128)(2,1)}, bf16[16,4,256]{2,1,0:T(4,128)(2,1)S(1)}, u32[]{:S(2)}, u32[]{:S(2)}) collective-permute-start(bf16[16,4,256]{2,1,0:T(4,128)(2,1)} %bitcast.6), channel_id=1, source_target_pairs={{0,4},{4,0},{8,12},{12,8},{1,5},{5,1},{9,13},{13,9},{2,6},{6,2},{1... | collective-permute-start | bytes 98312 | tf_op jit(solution)/shard_map/ppermute | solution.py:526
  10.7 1.2 %begin.1 = (bf16[256,128]{1,0:T(8,128)(2,1)S(1)}, bf16[3,3,3,128,128]{4,3,2,1,0:T(8,128)(2,1)S(1)}, bf16[1152,384]{1,0:T(8,128)(2,1)S(1)}) custom-call(bf16[256,128]{1,0:T(8,128)(2,1)} %bitcast.13, bf16[3,3,3,128,128]{4,3,2,1,0:T(8,128)(2,1)} %we_hbm.1), custom_call_target="tpu_custom_call" | custom-call | tf_op jit(solution)/shard_map/begin/pallas_call | solution.py:535
  11.9 0.0 collective-permute-done.2.refs_3_
  11.9 0.3 collective-permute-done.1.refs_2_
  12.3 0.0 collective-permute-done.refs_1_
  12.3 0.0 copy-start
  12.3 1.8 %early.1 = (bf16[1024,128]{1,0:T(8,128)(2,1)S(1)}, f32[1024,128]{1,0:T(8,128)S(1)}, bf16[320,128]{1,0:T(8,128)(2,1)S(1)}, f32[192,128]{1,0:T(8,128)S(1)}) custom-call(bf16[256,128]{1,0:T(8,128)(2,1)S(1)} %get-tuple-element.33.refs_0_, bf16[256,128]{1,0:T(8,128)(2,1)S(1)} %collective-permute-done.refs_1_, ...), custom_call_target="tpu_custom_call" | custom-call | tf_op jit(solution)/shard_map/early/pallas_call | solution.py:535
  14.0 0.0 collective-permute-done.4.refs_5_
  14.0 0.0 collective-permute-done.3.refs_4_
  14.0 1.5 %collective-permute-start.5 = (bf16[320,128]{1,0:T(8,128)(2,1)S(1)}, bf16[320,128]{1,0:T(8,128)(2,1)S(1)}, u32[]{:S(2)}, u32[]{:S(2)}) collective-permute-start(bf16[320,128]{1,0:T(8,128)(2,1)S(1)} %get-tuple-element.36.refs_0_), channel_id=1, source_target_pairs={{0,2},{2,0},{1,3},{3,1},{4,6},{6,4},{5,7},{7,5},{8,10},{10,8},{9,1... | collective-permute-start | bytes 245768 | tf_op jit(solution)/shard_map/ppermute | solution.py:526
  15.5 0.6 %collective-permute-start.7 = (bf16[1024,128]{1,0:T(8,128)(2,1)S(1)}, bf16[1024,128]{1,0:T(8,128)(2,1)S(1)}, u32[]{:S(2)}, u32[]{:S(2)}) collective-permute-start(bf16[1024,128]{1,0:T(8,128)(2,1)S(1)} %get-tuple-element.46.half_ref), channel_id=1, source_target_pairs={{0,2},{2,0},{1,3},{3,1},{4,6},{6,4},{5,7},{7,5},{8,10},{10,8},{9,1... | collective-permute-start | bytes 786440 | tf_op jit(solution)/shard_map/ppermute | solution.py:526
  16.1 1.1 %collective-permute-start.6 = (bf16[16,4,256]{2,1,0:T(4,128)(2,1)S(1)}, bf16[16,4,256]{2,1,0:T(4,128)(2,1)S(1)}, u32[]{:S(2)}, u32[]{:S(2)}) collective-permute-start(bf16[16,4,256]{2,1,0:T(4,128)(2,1)S(1)} %collective-permute-done.4.refs_5_), channel_id=1, source_target_pairs={{0,4},{4,0},{8,12},{12,8},{1,5},{5,1},{9,13},{13,9},{2,6},{6,2},{1... | collective-permute-start | bytes 98312 | tf_op jit(solution)/shard_map/ppermute | solution.py:526
  17.2 1.8 %fetch.1 = (bf16[3,3,3,128,256]{4,3,2,1,0:T(8,128)(2,1)S(1)}, bf16[2304,384]{1,0:T(8,128)(2,1)S(1)}, bf16[3,1152,128]{2,1,0:T(8,128)(2,1)S(1)}) custom-call(bf16[3,3,3,128,256]{4,3,2,1,0:T(8,128)(2,1)} %far_ref, bf16[3,3,3,128,128]{4,3,2,1,0:T(8,128)(2,1)S(1)} %get-tuple-element.41.we_ref), custom_call_target="tpu_custom_call" | custom-call | tf_op jit(solution)/shard_map/fetch/pallas_call | solution.py:535
  19.0 1.0 %collective-permute-done.6.refs_6_ = bf16[16,4,256]{2,1,0:T(4,128)(2,1)S(1)} collective-permute-done((bf16[16,4,256]{2,1,0:T(4,128)(2,1)S(1)}, bf16[16,4,256]{2,1,0:T(4,128)(2,1)S(1)}, u32[]{:S(2)}, u32[]{:S(2)}) %collective-permute-start.6) | collective-permute-done | bytes 32800 | tf_op jit(solution)/shard_map/ppermute | solution.py:526
  20.1 0.0 collective-permute-done.5.refs_1_
  20.1 0.0 copy-done
  20.1 0.9 %late.1 = (bf16[256,384]{1,0:T(8,128)(2,1)S(1)}, f32[64,128]{1,0:T(8,128)S(1)}) custom-call(bf16[320,128]{1,0:T(8,128)(2,1)S(1)} %get-tuple-element.36.refs_0_, bf16[320,128]{1,0:T(8,128)(2,1)S(1)} %collective-permute-done.5.refs_1_, f32[192,128]{1,0:T(8,128)S(1)} %get-tuple-element.37.refs_2_, bf16[16,4,256]{2,1,0:T(4,128)(2,1)S(1)} %bitcast.7, ...), custom_call_target="tpu_custom_call" | custom-call | tf_op jit(solution)/shard_map/late/pallas_call | solution.py:535
  21.0 0.1 collective-permute-start.8
  21.0 0.8 %late_back.1 = (bf16[256,128]{1,0:T(8,128)(2,1)S(1)}, f32[256,128]{1,0:T(8,128)S(1)}) custom-call(bf16[256,384]{1,0:T(8,128)(2,1)S(1)} %get-tuple-element.43.pd_ref.mine_ref, bf16[2304,384]{1,0:T(8,128)(2,1)S(1)} %get-tuple-element.44.wback_ref), custom_call_target="tpu_custom_call" | custom-call | tf_op jit(solution)/shard_map/late_back/pallas_call | solution.py:535
  21.8 1.5 %collective-permute-start.9 = (bf16[256,128]{1,0:T(8,128)(2,1)S(1)}, bf16[256,128]{1,0:T(8,128)(2,1)S(1)}, u32[]{:S(2)}, u32[]{:S(2)}) collective-permute-start(bf16[256,128]{1,0:T(8,128)(2,1)S(1)} %get-tuple-element.47), channel_id=1, source_target_pairs={{0,2},{2,0},{1,3},{3,1},{4,6},{6,4},{5,7},{7,5},{8,10},{10,8},{9,1... | collective-permute-start | bytes 196616 | tf_op jit(solution)/shard_map/ppermute | solution.py:526
  23.3 0.0 collective-permute-done.8.other_ref
  23.3 1.2 %late_grad.1.late_ref = bf16[3456,256]{1,0:T(8,128)(2,1)S(1)} custom-call(bf16[256,384]{1,0:T(8,128)(2,1)S(1)} %get-tuple-element.43.pd_ref.mine_ref, bf16[256,384]{1,0:T(8,128)(2,1)S(1)} %collective-permute-done.8.other_ref), custom_call_target="tpu_custom_call" | custom-call | tf_op jit(solution)/shard_map/late_grad/pallas_call | solution.py:535
  24.5 0.0 collective-permute-done.7.got_ref
  24.6 2.1 %other.1 = (bf16[2048,1152]{1,0:T(8,128)(2,1)S(1)}, f32[1024,128]{1,0:T(8,128)S(1)}) custom-call(bf16[1024,128]{1,0:T(8,128)(2,1)S(1)} %get-tuple-element.46.half_ref, bf16[1024,128]{1,0:T(8,128)(2,1)S(1)} %collective-permute-done.7.got_ref, bf16[1152,384]{1,0:T(8,128)(2,1)S(1)} %get-tuple-element.52.refs_4_.wcat_ref), custom_call_target="tpu_custom_call" | custom-call | tf_op jit(solution)/shard_map/other/pallas_call | solution.py:535
  26.7 0.0 collective-permute-done.9.other_ref
  26.7 1.8 %early_grad.1 = (bf16[1920,128]{1,0:T(8,128)(2,1)S(1)}, f32[4,160,128]{2,1,0:T(8,128)S(1)}, bf16[3456,256]{1,0:T(8,128)(2,1)}, bf16[384,2048]{1,0:T(8,128)(2,1)S(1)}) custom-call(f32[256,128]{1,0:T(8,128)S(1)} %get-tuple-element.49.mine_ref, bf16[256,128]{1,0:T(8,128)(2,1)S(1)} %collective-permute-done.9.other_ref, ...), custom_call_target="tpu_custom_call" | custom-call | tf_op jit(solution)/shard_map/early_grad/pallas_call | solution.py:535
  28.5 0.3 collective-permute-start.10
  28.8 1.0 %more.1.two_ref = bf16[1536,128]{1,0:T(8,128)(2,1)S(1)} custom-call(bf16[384,2048]{1,0:T(8,128)(2,1)S(1)} %get-tuple-element.58.left_ref, bf16[2048,1152]{1,0:T(8,128)(2,1)S(1)} %get-tuple-element.55.col_ref), custom_call_target="tpu_custom_call" | custom-call | tf_op jit(solution)/shard_map/more/pallas_call | solution.py:535
  29.8 0.4 %collective-permute-start.11 = (bf16[1536,128]{1,0:T(8,128)(2,1)S(1)}, bf16[1536,128]{1,0:T(8,128)(2,1)S(1)}, u32[]{:S(2)}, u32[]{:S(2)}) collective-permute-start(bf16[1536,128]{1,0:T(8,128)(2,1)S(1)} %more.1.two_ref), channel_id=1, source_target_pairs={{0,1},{1,0},{2,3},{3,2},{4,5},{5,4},{6,7},{7,6},{8,9},{9,8},{10,11... | collective-permute-start | bytes 1179656 | tf_op jit(solution)/shard_map/ppermute | solution.py:526
  30.2 1.3 %grad_volume.1 = bf16[256,128]{1,0:T(8,128)(2,1)} custom-call(f32[4,160,128]{2,1,0:T(8,128)S(1)} %get-tuple-element.61.win_ref, bf16[3,1152,128]{2,1,0:T(8,128)(2,1)S(1)} %get-tuple-element.62.wt_ref), custom_call_target="tpu_custom_call" | custom-call | tf_op jit(solution)/shard_map/grad_volume/pallas_call | solution.py:535
  31.5 0.2 collective-permute-done.11.two_got_ref
  31.6 0.0 collective-permute-done.10.one_got_ref
  31.6 1.0 %finish.1 = bf16[3456,128]{1,0:T(8,128)(2,1)} custom-call(bf16[1920,128]{1,0:T(8,128)(2,1)S(1)} %get-tuple-element.57.one_ref, bf16[1920,128]{1,0:T(8,128)(2,1)S(1)} %collective-permute-done.10.one_got_ref, bf16[1536,128]{1,0:T(8,128)(2,1)S(1)} %more.1.two_ref, bf16[1536,128]{1,0:T(8,128)(2,1)S(1)} %collective-permute-done.11.two_got_ref), custom_call_target="tpu_custom_call" | custom-call | tf_op jit(solution)/shard_map/finish/pallas_call | solution.py:535
Async XLA Ops:
  0.6 11.3 %collective-permute-start.2 = (bf16[256,128]{1,0:T(8,128)(2,1)}, bf16[256,128]{1,0:T(8,128)(2,1)S(1)}, u32[]{:S(2)}, u32[]{:S(2)}) collective-permute-start(bf16[256,128]{1,0:T(8,128)(2,1)} %bitcast.10), channel_id=1, source_target_pairs={{0,12},{4,8},{8,4},{12,0},{1,13},{5,9},{9,5},{13,1},{2,14},{6,10},... | collective-permute-start | bytes 196616 | tf_op jit(solution)/shard_map/ppermute | solution.py:526
  5.7 6.5 %collective-permute-start.1 = (bf16[256,128]{1,0:T(8,128)(2,1)}, bf16[256,128]{1,0:T(8,128)(2,1)S(1)}, u32[]{:S(2)}, u32[]{:S(2)}) collective-permute-start(bf16[256,128]{1,0:T(8,128)(2,1)} %bitcast.11), channel_id=1, source_target_pairs={{0,8},{4,12},{8,0},{12,4},{1,9},{5,13},{9,1},{13,5},{2,10},{6,14},... | collective-permute-start | bytes 196616 | tf_op jit(solution)/shard_map/ppermute | solution.py:526
  5.7 6.5 %collective-permute-start = (bf16[256,128]{1,0:T(8,128)(2,1)}, bf16[256,128]{1,0:T(8,128)(2,1)S(1)}, u32[]{:S(2)}, u32[]{:S(2)}) collective-permute-start(bf16[256,128]{1,0:T(8,128)(2,1)} %bitcast.12), channel_id=1, source_target_pairs={{0,4},{4,0},{8,12},{12,8},{1,5},{5,1},{9,13},{13,9},{2,6},{6,2},{1... | collective-permute-start | bytes 196616 | tf_op jit(solution)/shard_map/ppermute | solution.py:526
  6.4 7.6 %collective-permute-start.4 = (bf16[16,4,256]{2,1,0:T(4,128)(2,1)}, bf16[16,4,256]{2,1,0:T(4,128)(2,1)S(1)}, u32[]{:S(2)}, u32[]{:S(2)}) collective-permute-start(bf16[16,4,256]{2,1,0:T(4,128)(2,1)} %bitcast.5), channel_id=1, source_target_pairs={{0,8},{4,12},{8,0},{12,4},{1,9},{5,13},{9,1},{13,5},{2,10},{6,14},... | collective-permute-start | bytes 98312 | tf_op jit(solution)/shard_map/ppermute | solution.py:526
  8.7 5.4 %collective-permute-start.3 = (bf16[16,4,256]{2,1,0:T(4,128)(2,1)}, bf16[16,4,256]{2,1,0:T(4,128)(2,1)S(1)}, u32[]{:S(2)}, u32[]{:S(2)}) collective-permute-start(bf16[16,4,256]{2,1,0:T(4,128)(2,1)} %bitcast.6), channel_id=1, source_target_pairs={{0,4},{4,0},{8,12},{12,8},{1,5},{5,1},{9,13},{13,9},{2,6},{6,2},{1... | collective-permute-start | bytes 98312 | tf_op jit(solution)/shard_map/ppermute | solution.py:526
  12.3 7.8 %copy-start = (bf16[1,1,16,4,256]{4,3,2,1,0:T(4,128)(2,1)S(1)}, bf16[1,1,16,4,256]{4,3,2,1,0:T(4,128)(2,1)}, u32[]{:S(2)}) copy-start(bf16[1,1,16,4,256]{4,3,2,1,0:T(4,128)(2,1)} %param.7) | copy-start | bytes 98308
  14.0 6.0 %collective-permute-start.5 = (bf16[320,128]{1,0:T(8,128)(2,1)S(1)}, bf16[320,128]{1,0:T(8,128)(2,1)S(1)}, u32[]{:S(2)}, u32[]{:S(2)}) collective-permute-start(bf16[320,128]{1,0:T(8,128)(2,1)S(1)} %get-tuple-element.36.refs_0_), channel_id=1, source_target_pairs={{0,2},{2,0},{1,3},{3,1},{4,6},{6,4},{5,7},{7,5},{8,10},{10,8},{9,1... | collective-permute-start | bytes 245768 | tf_op jit(solution)/shard_map/ppermute | solution.py:526
  15.5 9.0 %collective-permute-start.7 = (bf16[1024,128]{1,0:T(8,128)(2,1)S(1)}, bf16[1024,128]{1,0:T(8,128)(2,1)S(1)}, u32[]{:S(2)}, u32[]{:S(2)}) collective-permute-start(bf16[1024,128]{1,0:T(8,128)(2,1)S(1)} %get-tuple-element.46.half_ref), channel_id=1, source_target_pairs={{0,2},{2,0},{1,3},{3,1},{4,6},{6,4},{5,7},{7,5},{8,10},{10,8},{9,1... | collective-permute-start | bytes 786440 | tf_op jit(solution)/shard_map/ppermute | solution.py:526
  16.1 3.9 %collective-permute-start.6 = (bf16[16,4,256]{2,1,0:T(4,128)(2,1)S(1)}, bf16[16,4,256]{2,1,0:T(4,128)(2,1)S(1)}, u32[]{:S(2)}, u32[]{:S(2)}) collective-permute-start(bf16[16,4,256]{2,1,0:T(4,128)(2,1)S(1)} %collective-permute-done.4.refs_5_), channel_id=1, source_target_pairs={{0,4},{4,0},{8,12},{12,8},{1,5},{5,1},{9,13},{13,9},{2,6},{6,2},{1... | collective-permute-start | bytes 98312 | tf_op jit(solution)/shard_map/ppermute | solution.py:526
  21.0 2.3 %collective-permute-start.8 = (bf16[256,384]{1,0:T(8,128)(2,1)S(1)}, bf16[256,384]{1,0:T(8,128)(2,1)S(1)}, u32[]{:S(2)}, u32[]{:S(2)}) collective-permute-start(bf16[256,384]{1,0:T(8,128)(2,1)S(1)} %get-tuple-element.43.pd_ref.mine_ref), channel_id=1, source_target_pairs={{0,1},{1,0},{2,3},{3,2},{4,5},{5,4},{6,7},{7,6},{8,9},{9,8},{10,11... | collective-permute-start | bytes 589832 | tf_op jit(solution)/shard_map/ppermute | solution.py:526
  21.8 4.9 %collective-permute-start.9 = (bf16[256,128]{1,0:T(8,128)(2,1)S(1)}, bf16[256,128]{1,0:T(8,128)(2,1)S(1)}, u32[]{:S(2)}, u32[]{:S(2)}) collective-permute-start(bf16[256,128]{1,0:T(8,128)(2,1)S(1)} %get-tuple-element.47), channel_id=1, source_target_pairs={{0,2},{2,0},{1,3},{3,1},{4,6},{6,4},{5,7},{7,5},{8,10},{10,8},{9,1... | collective-permute-start | bytes 196616 | tf_op jit(solution)/shard_map/ppermute | solution.py:526
  28.5 3.1 %collective-permute-start.10 = (bf16[1920,128]{1,0:T(8,128)(2,1)S(1)}, bf16[1920,128]{1,0:T(8,128)(2,1)S(1)}, u32[]{:S(2)}, u32[]{:S(2)}) collective-permute-start(bf16[1920,128]{1,0:T(8,128)(2,1)S(1)} %get-tuple-element.57.one_ref), channel_id=1, source_target_pairs={{0,1},{1,0},{2,3},{3,2},{4,5},{5,4},{6,7},{7,6},{8,9},{9,8},{10,11... | collective-permute-start | bytes 1474568 | tf_op jit(solution)/shard_map/ppermute | solution.py:526
  29.8 1.8 %collective-permute-start.11 = (bf16[1536,128]{1,0:T(8,128)(2,1)S(1)}, bf16[1536,128]{1,0:T(8,128)(2,1)S(1)}, u32[]{:S(2)}, u32[]{:S(2)}) collective-permute-start(bf16[1536,128]{1,0:T(8,128)(2,1)S(1)} %more.1.two_ref), channel_id=1, source_target_pairs={{0,1},{1,0},{2,3},{3,2},{4,5},{5,4},{6,7},{7,6},{8,9},{9,8},{10,11... | collective-permute-start | bytes 1179656 | tf_op jit(solution)/shard_map/ppermute | solution.py:526

commit v9 on v8

--- a/solution.py
+++ b/solution.py
@@ -278,15 +278,14 @@
     return slope
 
 
-def late_kernel(*refs, nk, dims):
-    gx, gz, lx, ly, lz, cx = dims
-    sent_ref, got_ref, edge_ref, cots, refs = *refs[:3], refs[3 : nk + 3], refs[nk + 3 :]
-    wl_ref, pd_ref, patch_ref = refs[:3]
-    pool_ref, lcol_ref, cot_ref, tmp_ref, tile_ref = refs[3:]
+def late_kernel(
+    sent_ref, got_ref, edge_ref, wl_ref, pooled_ref, slope_ref, patch_ref,
+    pool_ref, lcol_ref, tmp_ref, tile_ref, *, dims
+):
+    gx, gz, lx, ly, lz = dims
     lplane, hl, line = ly * lz, ly // 2 * lz, gx * gz
     cl = wl_ref.shape[-1]
-    crow = cx * lplane
-    k, j = lax.axis_index("space"), lax.axis_index("chan")
+    j = lax.axis_index("chan")
     edges = got_ref[pl.ds(lx * hl, 3 * line), :].astype(F32)
     lrow = lax.broadcasted_iota(jnp.int32, (hl, 128), 0)
     for x in range(lx):
@@ -309,7 +308,7 @@
                 border, tiles, ref[pl.ds(x * hl, hl), :].astype(F32)
             )
     for x in range(lx):
-        pd_ref[pl.ds(x * lplane, lplane), pl.ds(0, 128)] = pool_ref[x, pl.ds(8, lplane), :].astype(BF)
+        pooled_ref[pl.ds(x * lplane, lplane), :] = pool_ref[x, pl.ds(8, lplane), :].astype(BF)
 
     lcell = depth_of(lplane, lz)
     for x in range(lx):
@@ -322,19 +321,22 @@
         jnp.dot(lcol, wl_ref[a].reshape(9 * 128, cl), preferred_element_type=F32) for a in range(3)
     ]
     pre = fold(parts, lplane)
-    slope = gelu_and_slope(pre)[1]
+    slope_ref[...] = gelu_and_slope(pre)[1]
+
+
+def late_back_kernel(*refs, nk, dims):
+    lx, ly, lz, cx = dims
+    cots, refs = refs[:nk], refs[nk:]
+    pooled_ref, slope_ref, wback_ref, pd_ref, back_ref, mine_ref, dl_ref, dcol_ref, cot_ref = refs
+    lplane = ly * lz
+    cl = slope_ref.shape[1]
+    crow = cx * lplane
+    k = lax.axis_index("space")
     for n, dk in enumerate([0, *steps_of(nk)]):
-        kk = partner(k, dk, nk)
-        start = pl.multiple_of(kk * crow, 8)
+        start = pl.multiple_of(partner(k, dk, nk) * crow, 8)
         cot_ref[pl.ds(start, crow), :] = cots[n][...].astype(F32).reshape(crow, cl)
-    delta = (cot_ref[...] * slope).astype(BF)
-    pd_ref[:, pl.ds(128, cl)] = delta
-
-
-def late_back_kernel(pd_ref, wback_ref, back_ref, mine_ref, dl_ref, dcol_ref, *, dims):
-    lx, ly, lz = dims
-    lplane = ly * lz
-    cl = pd_ref.shape[1] - 128
+    pd_ref[:, pl.ds(0, 128)] = pooled_ref[...]
+    pd_ref[:, pl.ds(128, cl)] = (cot_ref[...] * slope_ref[...]).astype(BF)
     lcell = depth_of(lplane, lz)
     for x in range(lx):
         dl_ref[x, pl.ds(0, 8), :] = jnp.zeros((8, cl), F32)
@@ -609,24 +611,27 @@
         "fetch",
         raw=(0,),
     )
-    pooled_delta, patch = call(
-        functools.partial(late_kernel, nk=nk, dims=(gx, gz, lx, ly, lz, cx)),
-        [sds((lrows, 128 + cl), BF), sds((gx * gz, 128), F32)],
+    pooled, late_slope, patch = call(
+        functools.partial(late_kernel, dims=(gx, gz, lx, ly, lz)),
+        [sds((lrows, 128), BF), sds((lrows, cl), F32), sds((gx * gz, 128), F32)],
         [
             pltpu.VMEM((lx, lplane + 16, 128), F32),
             pltpu.VMEM((lrows, 9 * 128), BF),
-            pltpu.VMEM((lrows, cl), F32),
             pltpu.VMEM((lx * gz, 128), F32),
             pltpu.VMEM((lx * 2 * lz, 128), F32),
         ],
-        [send, send_other, edges] + cots + [wl],
+        [send, send_other, edges, wl],
         "late",
     )
-    back, back_mine = call(
-        functools.partial(late_back_kernel, dims=(lx, ly, lz)),
-        [sds((lrows, 128), BF), sds((lrows, 128), F32)],
-        [pltpu.VMEM((lx, lplane + 16, cl), F32), pltpu.VMEM((lrows, 9 * cl), BF)],
-        [pooled_delta, wback],
+    pooled_delta, back, back_mine = call(
+        functools.partial(late_back_kernel, nk=nk, dims=(lx, ly, lz, cx)),
+        [sds((lrows, 128 + cl), BF), sds((lrows, 128), BF), sds((lrows, 128), F32)],
+        [
+            pltpu.VMEM((lx, lplane + 16, cl), F32),
+            pltpu.VMEM((lrows, 9 * cl), BF),
+            pltpu.VMEM((lrows, cl), F32),
+        ],
+        cots + [pooled, late_slope, wback],
         "late_back",
     )
     pd_other = turned(pooled_delta, "rep", 1)

time: 32.8 us -> 32.2 us (0.982)
  waiting for transfers between devices: 1.53 us -> 0.84 us
    ppermute x12, waiting for transfers between devices: 1.53 us -> 0.84 us  [turned(): lax.ppermute(value, axis, [(i, i ^ by if pairs else (i + by) % count) for...]
  transfers between devices with their start and end apart: 12 -> 12, of which waited for: 3 -> 3; matrix products, arithmetic and copies ran while one was open for 0% -> 0% of each run, Pallas kernels for 37% -> 38%
where the time goes in v9:
time: 32.2 us; the launch traced here: 32.1 us
  starting transfers between devices  15.5 us (48%)
  Pallas kernels  15 us (47%)
  waiting for transfers between devices  0.84 us (3%)
  between operations  0.76 us (2%)
    ppermute x12, starting transfers between devices, turned(): lax.ppermute(value, axis, [(i, i ^ by if pairs else (i + by) % count) for...  15.5 us
    pallas_call x11, Pallas kernels, call(): pl.pallas_call(kernel, out_shape=outs, in_specs=[pl.BlockSpec(memory_spac...  15 us
    ppermute x12, waiting for transfers between devices, turned(): lax.ppermute(value, axis, [(i, i ^ by if pairs else (i + by) % count) for...  0.84 us
  transfers between devices with their start and end apart: 12, of which 3 were waited for; matrix products, arithmetic and copies ran while one was open for 0% of the time, Pallas kernels for 38%

profile of v9, /device:TPU:0, one launch (start us, length us, event | category | flops | bytes accessed | tf_op | source)
XLA Modules:
  0.0 32.1 jit_solution(4903103079245457862)
XLA Ops:
  0.6 5.1 %collective-permute-start.2 = (bf16[256,128]{1,0:T(8,128)(2,1)}, bf16[256,128]{1,0:T(8,128)(2,1)S(1)}, u32[]{:S(2)}, u32[]{:S(2)}) collective-permute-start(bf16[256,128]{1,0:T(8,128)(2,1)} %bitcast.10), channel_id=1, source_target_pairs={{0,12},{4,8},{8,4},{12,0},{1,13},{5,9},{9,5},{13,1},{2,14},{6,10},... | collective-permute-start | bytes 196616 | tf_op jit(solution)/shard_map/ppermute | solution.py:528
  5.7 0.0 collective-permute-start.1
  5.7 0.6 %collective-permute-start = (bf16[256,128]{1,0:T(8,128)(2,1)}, bf16[256,128]{1,0:T(8,128)(2,1)S(1)}, u32[]{:S(2)}, u32[]{:S(2)}) collective-permute-start(bf16[256,128]{1,0:T(8,128)(2,1)} %bitcast.12), channel_id=1, source_target_pairs={{0,4},{4,0},{8,12},{12,8},{1,5},{5,1},{9,13},{13,9},{2,6},{6,2},{1... | collective-permute-start | bytes 196616 | tf_op jit(solution)/shard_map/ppermute | solution.py:528
  6.4 2.3 %collective-permute-start.4 = (bf16[16,4,256]{2,1,0:T(4,128)(2,1)}, bf16[16,4,256]{2,1,0:T(4,128)(2,1)S(1)}, u32[]{:S(2)}, u32[]{:S(2)}) collective-permute-start(bf16[16,4,256]{2,1,0:T(4,128)(2,1)} %bitcast.5), channel_id=1, source_target_pairs={{0,8},{4,12},{8,0},{12,4},{1,9},{5,13},{9,1},{13,5},{2,10},{6,14},... | collective-permute-start | bytes 98312 | tf_op jit(solution)/shard_map/ppermute | solution.py:528
  8.7 2.0 %collective-permute-start.3 = (bf16[16,4,256]{2,1,0:T(4,128)(2,1)}, bf16[16,4,256]{2,1,0:T(4,128)(2,1)S(1)}, u32[]{:S(2)}, u32[]{:S(2)}) collective-permute-start(bf16[16,4,256]{2,1,0:T(4,128)(2,1)} %bitcast.6), channel_id=1, source_target_pairs={{0,4},{4,0},{8,12},{12,8},{1,5},{5,1},{9,13},{13,9},{2,6},{6,2},{1... | collective-permute-start | bytes 98312 | tf_op jit(solution)/shard_map/ppermute | solution.py:528
  10.7 1.2 %begin.1 = (bf16[256,128]{1,0:T(8,128)(2,1)S(1)}, bf16[3,3,3,128,128]{4,3,2,1,0:T(8,128)(2,1)S(1)}, bf16[1152,384]{1,0:T(8,128)(2,1)S(1)}) custom-call(bf16[256,128]{1,0:T(8,128)(2,1)} %bitcast.13, bf16[3,3,3,128,128]{4,3,2,1,0:T(8,128)(2,1)} %we_hbm.1), custom_call_target="tpu_custom_call" | custom-call | tf_op jit(solution)/shard_map/begin/pallas_call | solution.py:537
  11.9 0.0 collective-permute-done.2.refs_3_
  11.9 0.3 collective-permute-done.1.refs_2_
  12.3 0.0 collective-permute-done.refs_1_
  12.3 1.8 %early.1 = (bf16[1024,128]{1,0:T(8,128)(2,1)S(1)}, f32[1024,128]{1,0:T(8,128)S(1)}, bf16[320,128]{1,0:T(8,128)(2,1)S(1)}, f32[192,128]{1,0:T(8,128)S(1)}) custom-call(bf16[256,128]{1,0:T(8,128)(2,1)S(1)} %get-tuple-element.35.refs_0_, bf16[256,128]{1,0:T(8,128)(2,1)S(1)} %collective-permute-done.refs_1_, ...), custom_call_target="tpu_custom_call" | custom-call | tf_op jit(solution)/shard_map/early/pallas_call | solution.py:537
  14.0 0.0 collective-permute-done.4.refs_2_
  14.0 0.0 collective-permute-done.3.refs_1_
  14.0 1.5 %collective-permute-start.6 = (bf16[320,128]{1,0:T(8,128)(2,1)S(1)}, bf16[320,128]{1,0:T(8,128)(2,1)S(1)}, u32[]{:S(2)}, u32[]{:S(2)}) collective-permute-start(bf16[320,128]{1,0:T(8,128)(2,1)S(1)} %get-tuple-element.40.sent_ref), channel_id=1, source_target_pairs={{0,2},{2,0},{1,3},{3,1},{4,6},{6,4},{5,7},{7,5},{8,10},{10,8},{9,1... | collective-permute-start | bytes 245768 | tf_op jit(solution)/shard_map/ppermute | solution.py:528
  15.5 0.6 %collective-permute-start.7 = (bf16[1024,128]{1,0:T(8,128)(2,1)S(1)}, bf16[1024,128]{1,0:T(8,128)(2,1)S(1)}, u32[]{:S(2)}, u32[]{:S(2)}) collective-permute-start(bf16[1024,128]{1,0:T(8,128)(2,1)S(1)} %get-tuple-element.49.half_ref), channel_id=1, source_target_pairs={{0,2},{2,0},{1,3},{3,1},{4,6},{6,4},{5,7},{7,5},{8,10},{10,8},{9,1... | collective-permute-start | bytes 786440 | tf_op jit(solution)/shard_map/ppermute | solution.py:528
  16.1 1.1 %collective-permute-start.5 = (bf16[16,4,256]{2,1,0:T(4,128)(2,1)S(1)}, bf16[16,4,256]{2,1,0:T(4,128)(2,1)S(1)}, u32[]{:S(2)}, u32[]{:S(2)}) collective-permute-start(bf16[16,4,256]{2,1,0:T(4,128)(2,1)S(1)} %collective-permute-done.4.refs_2_), channel_id=1, source_target_pairs={{0,4},{4,0},{8,12},{12,8},{1,5},{5,1},{9,13},{13,9},{2,6},{6,2},{1... | collective-permute-start | bytes 98312 | tf_op jit(solution)/shard_map/ppermute | solution.py:528
  17.2 0.0 copy-start
  17.2 1.8 %fetch.1 = (bf16[3,3,3,128,256]{4,3,2,1,0:T(8,128)(2,1)S(1)}, bf16[2304,384]{1,0:T(8,128)(2,1)S(1)}, bf16[3,1152,128]{2,1,0:T(8,128)(2,1)S(1)}) custom-call(bf16[3,3,3,128,256]{4,3,2,1,0:T(8,128)(2,1)} %far_ref, bf16[3,3,3,128,128]{4,3,2,1,0:T(8,128)(2,1)S(1)} %get-tuple-element.43.we_ref), custom_call_target="tpu_custom_call" | custom-call | tf_op jit(solution)/shard_map/fetch/pallas_call | solution.py:537
  19.0 0.4 %collective-permute-done.6.got_ref = bf16[320,128]{1,0:T(8,128)(2,1)S(1)} collective-permute-done((bf16[320,128]{1,0:T(8,128)(2,1)S(1)}, bf16[320,128]{1,0:T(8,128)(2,1)S(1)}, u32[]{:S(2)}, u32[]{:S(2)}) %collective-permute-start.6) | collective-permute-done | bytes 81952 | tf_op jit(solution)/shard_map/ppermute | solution.py:528
  19.4 0.9 %late.1 = (bf16[256,128]{1,0:T(8,128)(2,1)S(1)}, f32[256,256]{1,0:T(8,128)S(1)}, f32[64,128]{1,0:T(8,128)S(1)}) custom-call(bf16[320,128]{1,0:T(8,128)(2,1)S(1)} %get-tuple-element.40.sent_ref, bf16[320,128]{1,0:T(8,128)(2,1)S(1)} %collective-permute-done.6.got_ref, f32[192,128]{1,0:T(8,128)S(1)} %get-tuple-element.41.edge_ref, ...), custom_call_target="tpu_custom_call" | custom-call | tf_op jit(solution)/shard_map/late/pallas_call | solution.py:537
  20.3 0.0 collective-permute-done.5.refs_3_
  20.3 0.0 copy-done
  20.3 0.8 %late_back.1 = (bf16[256,384]{1,0:T(8,128)(2,1)S(1)}, bf16[256,128]{1,0:T(8,128)(2,1)S(1)}, f32[256,128]{1,0:T(8,128)S(1)}) custom-call(bf16[16,4,256]{2,1,0:T(4,128)(2,1)S(1)} %bitcast.7, bf16[16,4,256]{2,1,0:T(4,128)(2,1)S(1)} %collective-permute-done.3.refs_1_, bf16[16,4,256]{2,1,0:T(4,128)(2,1)S(1)} %collective-permute-done.4.refs_2_, ...), custom_call_target="tpu_custom_call" | custom-call | tf_op jit(solution)/shard_map/late_back/pallas_call | solution.py:537
  21.2 0.1 collective-permute-start.8
  21.2 1.5 %collective-permute-start.9 = (bf16[256,128]{1,0:T(8,128)(2,1)S(1)}, bf16[256,128]{1,0:T(8,128)(2,1)S(1)}, u32[]{:S(2)}, u32[]{:S(2)}) collective-permute-start(bf16[256,128]{1,0:T(8,128)(2,1)S(1)} %get-tuple-element.50), channel_id=1, source_target_pairs={{0,2},{2,0},{1,3},{3,1},{4,6},{6,4},{5,7},{7,5},{8,10},{10,8},{9,1... | collective-permute-start | bytes 196616 | tf_op jit(solution)/shard_map/ppermute | solution.py:528
  22.8 0.0 collective-permute-done.8.other_ref
  22.8 1.2 %late_grad.1.late_ref = bf16[3456,256]{1,0:T(8,128)(2,1)S(1)} custom-call(bf16[256,384]{1,0:T(8,128)(2,1)S(1)} %get-tuple-element.51.mine_ref, bf16[256,384]{1,0:T(8,128)(2,1)S(1)} %collective-permute-done.8.other_ref), custom_call_target="tpu_custom_call" | custom-call | tf_op jit(solution)/shard_map/late_grad/pallas_call | solution.py:537
  24.0 0.0 collective-permute-done.7.got_ref
  24.0 2.1 %other.1 = (bf16[2048,1152]{1,0:T(8,128)(2,1)S(1)}, f32[1024,128]{1,0:T(8,128)S(1)}) custom-call(bf16[1024,128]{1,0:T(8,128)(2,1)S(1)} %get-tuple-element.49.half_ref, bf16[1024,128]{1,0:T(8,128)(2,1)S(1)} %collective-permute-done.7.got_ref, bf16[1152,384]{1,0:T(8,128)(2,1)S(1)} %get-tuple-element.56.refs_4_.wcat_ref), custom_call_target="tpu_custom_call" | custom-call | tf_op jit(solution)/shard_map/other/pallas_call | solution.py:537
  26.2 0.0 collective-permute-done.9.other_ref
  26.2 1.8 %early_grad.1 = (bf16[1920,128]{1,0:T(8,128)(2,1)S(1)}, f32[4,160,128]{2,1,0:T(8,128)S(1)}, bf16[3456,256]{1,0:T(8,128)(2,1)}, bf16[384,2048]{1,0:T(8,128)(2,1)S(1)}) custom-call(f32[256,128]{1,0:T(8,128)S(1)} %get-tuple-element.53.mine_ref, bf16[256,128]{1,0:T(8,128)(2,1)S(1)} %collective-permute-done.9.other_ref, ...), custom_call_target="tpu_custom_call" | custom-call | tf_op jit(solution)/shard_map/early_grad/pallas_call | solution.py:537
  28.0 0.2 collective-permute-start.10
  28.2 1.0 %more.1.two_ref = bf16[1536,128]{1,0:T(8,128)(2,1)S(1)} custom-call(bf16[384,2048]{1,0:T(8,128)(2,1)S(1)} %get-tuple-element.62.left_ref, bf16[2048,1152]{1,0:T(8,128)(2,1)S(1)} %get-tuple-element.59.col_ref), custom_call_target="tpu_custom_call" | custom-call | tf_op jit(solution)/shard_map/more/pallas_call | solution.py:537
  29.3 0.4 %collective-permute-start.11 = (bf16[1536,128]{1,0:T(8,128)(2,1)S(1)}, bf16[1536,128]{1,0:T(8,128)(2,1)S(1)}, u32[]{:S(2)}, u32[]{:S(2)}) collective-permute-start(bf16[1536,128]{1,0:T(8,128)(2,1)S(1)} %more.1.two_ref), channel_id=1, source_target_pairs={{0,1},{1,0},{2,3},{3,2},{4,5},{5,4},{6,7},{7,6},{8,9},{9,8},{10,11... | collective-permute-start | bytes 1179656 | tf_op jit(solution)/shard_map/ppermute | solution.py:528
  29.7 1.3 %grad_volume.1 = bf16[256,128]{1,0:T(8,128)(2,1)} custom-call(f32[4,160,128]{2,1,0:T(8,128)S(1)} %get-tuple-element.65.win_ref, bf16[3,1152,128]{2,1,0:T(8,128)(2,1)S(1)} %get-tuple-element.66.wt_ref), custom_call_target="tpu_custom_call" | custom-call | tf_op jit(solution)/shard_map/grad_volume/pallas_call | solution.py:537
  30.9 0.1 collective-permute-done.11.two_got_ref
  31.1 0.0 collective-permute-done.10.one_got_ref
  31.1 1.0 %finish.1 = bf16[3456,128]{1,0:T(8,128)(2,1)} custom-call(bf16[1920,128]{1,0:T(8,128)(2,1)S(1)} %get-tuple-element.61.one_ref, bf16[1920,128]{1,0:T(8,128)(2,1)S(1)} %collective-permute-done.10.one_got_ref, bf16[1536,128]{1,0:T(8,128)(2,1)S(1)} %more.1.two_ref, bf16[1536,128]{1,0:T(8,128)(2,1)S(1)} %collective-permute-done.11.two_got_ref), custom_call_target="tpu_custom_call" | custom-call | tf_op jit(solution)/shard_map/finish/pallas_call | solution.py:537
Async XLA Ops:
  0.6 11.3 %collective-permute-start.2 = (bf16[256,128]{1,0:T(8,128)(2,1)}, bf16[256,128]{1,0:T(8,128)(2,1)S(1)}, u32[]{:S(2)}, u32[]{:S(2)}) collective-permute-start(bf16[256,128]{1,0:T(8,128)(2,1)} %bitcast.10), channel_id=1, source_target_pairs={{0,12},{4,8},{8,4},{12,0},{1,13},{5,9},{9,5},{13,1},{2,14},{6,10},... | collective-permute-start | bytes 196616 | tf_op jit(solution)/shard_map/ppermute | solution.py:528
  5.7 6.5 %collective-permute-start.1 = (bf16[256,128]{1,0:T(8,128)(2,1)}, bf16[256,128]{1,0:T(8,128)(2,1)S(1)}, u32[]{:S(2)}, u32[]{:S(2)}) collective-permute-start(bf16[256,128]{1,0:T(8,128)(2,1)} %bitcast.11), channel_id=1, source_target_pairs={{0,8},{4,12},{8,0},{12,4},{1,9},{5,13},{9,1},{13,5},{2,10},{6,14},... | collective-permute-start | bytes 196616 | tf_op jit(solution)/shard_map/ppermute | solution.py:528
  5.7 6.5 %collective-permute-start = (bf16[256,128]{1,0:T(8,128)(2,1)}, bf16[256,128]{1,0:T(8,128)(2,1)S(1)}, u32[]{:S(2)}, u32[]{:S(2)}) collective-permute-start(bf16[256,128]{1,0:T(8,128)(2,1)} %bitcast.12), channel_id=1, source_target_pairs={{0,4},{4,0},{8,12},{12,8},{1,5},{5,1},{9,13},{13,9},{2,6},{6,2},{1... | collective-permute-start | bytes 196616 | tf_op jit(solution)/shard_map/ppermute | solution.py:528
  6.4 7.6 %collective-permute-start.4 = (bf16[16,4,256]{2,1,0:T(4,128)(2,1)}, bf16[16,4,256]{2,1,0:T(4,128)(2,1)S(1)}, u32[]{:S(2)}, u32[]{:S(2)}) collective-permute-start(bf16[16,4,256]{2,1,0:T(4,128)(2,1)} %bitcast.5), channel_id=1, source_target_pairs={{0,8},{4,12},{8,0},{12,4},{1,9},{5,13},{9,1},{13,5},{2,10},{6,14},... | collective-permute-start | bytes 98312 | tf_op jit(solution)/shard_map/ppermute | solution.py:528
  8.7 5.4 %collective-permute-start.3 = (bf16[16,4,256]{2,1,0:T(4,128)(2,1)}, bf16[16,4,256]{2,1,0:T(4,128)(2,1)S(1)}, u32[]{:S(2)}, u32[]{:S(2)}) collective-permute-start(bf16[16,4,256]{2,1,0:T(4,128)(2,1)} %bitcast.6), channel_id=1, source_target_pairs={{0,4},{4,0},{8,12},{12,8},{1,5},{5,1},{9,13},{13,9},{2,6},{6,2},{1... | collective-permute-start | bytes 98312 | tf_op jit(solution)/shard_map/ppermute | solution.py:528
  14.0 5.4 %collective-permute-start.6 = (bf16[320,128]{1,0:T(8,128)(2,1)S(1)}, bf16[320,128]{1,0:T(8,128)(2,1)S(1)}, u32[]{:S(2)}, u32[]{:S(2)}) collective-permute-start(bf16[320,128]{1,0:T(8,128)(2,1)S(1)} %get-tuple-element.40.sent_ref), channel_id=1, source_target_pairs={{0,2},{2,0},{1,3},{3,1},{4,6},{6,4},{5,7},{7,5},{8,10},{10,8},{9,1... | collective-permute-start | bytes 245768 | tf_op jit(solution)/shard_map/ppermute | solution.py:528
  15.5 8.5 %collective-permute-start.7 = (bf16[1024,128]{1,0:T(8,128)(2,1)S(1)}, bf16[1024,128]{1,0:T(8,128)(2,1)S(1)}, u32[]{:S(2)}, u32[]{:S(2)}) collective-permute-start(bf16[1024,128]{1,0:T(8,128)(2,1)S(1)} %get-tuple-element.49.half_ref), channel_id=1, source_target_pairs={{0,2},{2,0},{1,3},{3,1},{4,6},{6,4},{5,7},{7,5},{8,10},{10,8},{9,1... | collective-permute-start | bytes 786440 | tf_op jit(solution)/shard_map/ppermute | solution.py:528
  16.1 4.2 %collective-permute-start.5 = (bf16[16,4,256]{2,1,0:T(4,128)(2,1)S(1)}, bf16[16,4,256]{2,1,0:T(4,128)(2,1)S(1)}, u32[]{:S(2)}, u32[]{:S(2)}) collective-permute-start(bf16[16,4,256]{2,1,0:T(4,128)(2,1)S(1)} %collective-permute-done.4.refs_2_), channel_id=1, source_target_pairs={{0,4},{4,0},{8,12},{12,8},{1,5},{5,1},{9,13},{13,9},{2,6},{6,2},{1... | collective-permute-start | bytes 98312 | tf_op jit(solution)/shard_map/ppermute | solution.py:528
  17.2 3.1 %copy-start = (bf16[1,1,16,4,256]{4,3,2,1,0:T(4,128)(2,1)S(1)}, bf16[1,1,16,4,256]{4,3,2,1,0:T(4,128)(2,1)}, u32[]{:S(2)}) copy-start(bf16[1,1,16,4,256]{4,3,2,1,0:T(4,128)(2,1)} %param.7) | copy-start | bytes 98308
  21.2 1.6 %collective-permute-start.8 = (bf16[256,384]{1,0:T(8,128)(2,1)S(1)}, bf16[256,384]{1,0:T(8,128)(2,1)S(1)}, u32[]{:S(2)}, u32[]{:S(2)}) collective-permute-start(bf16[256,384]{1,0:T(8,128)(2,1)S(1)} %get-tuple-element.51.mine_ref), channel_id=1, source_target_pairs={{0,1},{1,0},{2,3},{3,2},{4,5},{5,4},{6,7},{7,6},{8,9},{9,8},{10,11... | collective-permute-start | bytes 589832 | tf_op jit(solution)/shard_map/ppermute | solution.py:528
  21.2 4.9 %collective-permute-start.9 = (bf16[256,128]{1,0:T(8,128)(2,1)S(1)}, bf16[256,128]{1,0:T(8,128)(2,1)S(1)}, u32[]{:S(2)}, u32[]{:S(2)}) collective-permute-start(bf16[256,128]{1,0:T(8,128)(2,1)S(1)} %get-tuple-element.50), channel_id=1, source_target_pairs={{0,2},{2,0},{1,3},{3,1},{4,6},{6,4},{5,7},{7,5},{8,10},{10,8},{9,1... | collective-permute-start | bytes 196616 | tf_op jit(solution)/shard_map/ppermute | solution.py:528
  28.0 3.1 %collective-permute-start.10 = (bf16[1920,128]{1,0:T(8,128)(2,1)S(1)}, bf16[1920,128]{1,0:T(8,128)(2,1)S(1)}, u32[]{:S(2)}, u32[]{:S(2)}) collective-permute-start(bf16[1920,128]{1,0:T(8,128)(2,1)S(1)} %get-tuple-element.61.one_ref), channel_id=1, source_target_pairs={{0,1},{1,0},{2,3},{3,2},{4,5},{5,4},{6,7},{7,6},{8,9},{9,8},{10,11... | collective-permute-start | bytes 1474568 | tf_op jit(solution)/shard_map/ppermute | solution.py:528
  29.3 1.8 %collective-permute-start.11 = (bf16[1536,128]{1,0:T(8,128)(2,1)S(1)}, bf16[1536,128]{1,0:T(8,128)(2,1)S(1)}, u32[]{:S(2)}, u32[]{:S(2)}) collective-permute-start(bf16[1536,128]{1,0:T(8,128)(2,1)S(1)} %more.1.two_ref), channel_id=1, source_target_pairs={{0,1},{1,0},{2,3},{3,2},{4,5},{5,4},{6,7},{7,6},{8,9},{9,8},{10,11... | collective-permute-start | bytes 1179656 | tf_op jit(solution)/shard_map/ppermute | solution.py:528

commit v10 on v9

--- a/solution.py
+++ b/solution.py
@@ -12,7 +12,7 @@
 F32 = jnp.float32
 VMEM_BYTES = 14 * 2**20
 GATHER_BLOCKS = 8
-EARLY_TAPS = 5
+EARLY_TAPS = 6
 
 
 def padded_2(block, sides, width):

time: 32.2 us -> 32.1 us (level)
  transfers between devices with their start and end apart: 12 -> 12, of which waited for: 3 -> 2; matrix products, arithmetic and copies ran while one was open for 0% -> 0% of each run, Pallas kernels for 38% -> 38%
where the time goes in v10:
time: 32.1 us; the launch traced here: 32 us
  starting transfers between devices  15.5 us (48%)
  Pallas kernels  15 us (47%)
  between operations  0.76 us (2%)
  waiting for transfers between devices  0.73 us (2%)
    ppermute x12, starting transfers between devices, turned(): lax.ppermute(value, axis, [(i, i ^ by if pairs else (i + by) % count) for...  15.5 us
    pallas_call x11, Pallas kernels, call(): pl.pallas_call(kernel, out_shape=outs, in_specs=[pl.BlockSpec(memory_spac...  15 us
    ppermute x12, waiting for transfers between devices, turned(): lax.ppermute(value, axis, [(i, i ^ by if pairs else (i + by) % count) for...  0.73 us
  transfers between devices with their start and end apart: 12, of which 2 were waited for; matrix products, arithmetic and copies ran while one was open for 0% of the time, Pallas kernels for 38%

profile of v10, /device:TPU:0, one launch (start us, length us, event | category | flops | bytes accessed | tf_op | source)
XLA Modules:
  0.0 32.0 jit_solution(15416416062079762946)
XLA Ops:
  0.6 5.1 %collective-permute-start.2 = (bf16[256,128]{1,0:T(8,128)(2,1)}, bf16[256,128]{1,0:T(8,128)(2,1)S(1)}, u32[]{:S(2)}, u32[]{:S(2)}) collective-permute-start(bf16[256,128]{1,0:T(8,128)(2,1)} %bitcast.10), channel_id=1, source_target_pairs={{0,12},{4,8},{8,4},{12,0},{1,13},{5,9},{9,5},{13,1},{2,14},{6,10},... | collective-permute-start | bytes 196616 | tf_op jit(solution)/shard_map/ppermute | solution.py:528
  5.7 0.0 collective-permute-start.1
  5.7 0.6 %collective-permute-start = (bf16[256,128]{1,0:T(8,128)(2,1)}, bf16[256,128]{1,0:T(8,128)(2,1)S(1)}, u32[]{:S(2)}, u32[]{:S(2)}) collective-permute-start(bf16[256,128]{1,0:T(8,128)(2,1)} %bitcast.12), channel_id=1, source_target_pairs={{0,4},{4,0},{8,12},{12,8},{1,5},{5,1},{9,13},{13,9},{2,6},{6,2},{1... | collective-permute-start | bytes 196616 | tf_op jit(solution)/shard_map/ppermute | solution.py:528
  6.4 2.3 %collective-permute-start.4 = (bf16[16,4,256]{2,1,0:T(4,128)(2,1)}, bf16[16,4,256]{2,1,0:T(4,128)(2,1)S(1)}, u32[]{:S(2)}, u32[]{:S(2)}) collective-permute-start(bf16[16,4,256]{2,1,0:T(4,128)(2,1)} %bitcast.5), channel_id=1, source_target_pairs={{0,8},{4,12},{8,0},{12,4},{1,9},{5,13},{9,1},{13,5},{2,10},{6,14},... | collective-permute-start | bytes 98312 | tf_op jit(solution)/shard_map/ppermute | solution.py:528
  8.7 2.0 %collective-permute-start.3 = (bf16[16,4,256]{2,1,0:T(4,128)(2,1)}, bf16[16,4,256]{2,1,0:T(4,128)(2,1)S(1)}, u32[]{:S(2)}, u32[]{:S(2)}) collective-permute-start(bf16[16,4,256]{2,1,0:T(4,128)(2,1)} %bitcast.6), channel_id=1, source_target_pairs={{0,4},{4,0},{8,12},{12,8},{1,5},{5,1},{9,13},{13,9},{2,6},{6,2},{1... | collective-permute-start | bytes 98312 | tf_op jit(solution)/shard_map/ppermute | solution.py:528
  10.7 1.2 %begin.1 = (bf16[256,128]{1,0:T(8,128)(2,1)S(1)}, bf16[3,3,3,128,128]{4,3,2,1,0:T(8,128)(2,1)S(1)}, bf16[1152,384]{1,0:T(8,128)(2,1)S(1)}) custom-call(bf16[256,128]{1,0:T(8,128)(2,1)} %bitcast.13, bf16[3,3,3,128,128]{4,3,2,1,0:T(8,128)(2,1)} %we_hbm.1), custom_call_target="tpu_custom_call" | custom-call | tf_op jit(solution)/shard_map/begin/pallas_call | solution.py:537
  11.9 0.0 collective-permute-done.2.refs_3_
  11.9 0.3 collective-permute-done.1.refs_2_
  12.3 0.0 collective-permute-done.refs_1_
  12.3 1.8 %early.1 = (bf16[1024,128]{1,0:T(8,128)(2,1)S(1)}, f32[1024,128]{1,0:T(8,128)S(1)}, bf16[320,128]{1,0:T(8,128)(2,1)S(1)}, f32[192,128]{1,0:T(8,128)S(1)}) custom-call(bf16[256,128]{1,0:T(8,128)(2,1)S(1)} %get-tuple-element.35.refs_0_, bf16[256,128]{1,0:T(8,128)(2,1)S(1)} %collective-permute-done.refs_1_, ...), custom_call_target="tpu_custom_call" | custom-call | tf_op jit(solution)/shard_map/early/pallas_call | solution.py:537
  14.0 0.0 collective-permute-done.4.refs_2_
  14.0 0.0 collective-permute-done.3.refs_1_
  14.0 1.5 %collective-permute-start.6 = (bf16[320,128]{1,0:T(8,128)(2,1)S(1)}, bf16[320,128]{1,0:T(8,128)(2,1)S(1)}, u32[]{:S(2)}, u32[]{:S(2)}) collective-permute-start(bf16[320,128]{1,0:T(8,128)(2,1)S(1)} %get-tuple-element.40.sent_ref), channel_id=1, source_target_pairs={{0,2},{2,0},{1,3},{3,1},{4,6},{6,4},{5,7},{7,5},{8,10},{10,8},{9,1... | collective-permute-start | bytes 245768 | tf_op jit(solution)/shard_map/ppermute | solution.py:528
  15.5 0.6 %collective-permute-start.7 = (bf16[1024,128]{1,0:T(8,128)(2,1)S(1)}, bf16[1024,128]{1,0:T(8,128)(2,1)S(1)}, u32[]{:S(2)}, u32[]{:S(2)}) collective-permute-start(bf16[1024,128]{1,0:T(8,128)(2,1)S(1)} %get-tuple-element.49.half_ref), channel_id=1, source_target_pairs={{0,2},{2,0},{1,3},{3,1},{4,6},{6,4},{5,7},{7,5},{8,10},{10,8},{9,1... | collective-permute-start | bytes 786440 | tf_op jit(solution)/shard_map/ppermute | solution.py:528
  16.1 1.1 %collective-permute-start.5 = (bf16[16,4,256]{2,1,0:T(4,128)(2,1)S(1)}, bf16[16,4,256]{2,1,0:T(4,128)(2,1)S(1)}, u32[]{:S(2)}, u32[]{:S(2)}) collective-permute-start(bf16[16,4,256]{2,1,0:T(4,128)(2,1)S(1)} %collective-permute-done.4.refs_2_), channel_id=1, source_target_pairs={{0,4},{4,0},{8,12},{12,8},{1,5},{5,1},{9,13},{13,9},{2,6},{6,2},{1... | collective-permute-start | bytes 98312 | tf_op jit(solution)/shard_map/ppermute | solution.py:528
  17.2 0.0 copy-start
  17.2 1.8 %fetch.1 = (bf16[3,3,3,128,256]{4,3,2,1,0:T(8,128)(2,1)S(1)}, bf16[2304,384]{1,0:T(8,128)(2,1)S(1)}, bf16[3,1152,128]{2,1,0:T(8,128)(2,1)S(1)}) custom-call(bf16[3,3,3,128,256]{4,3,2,1,0:T(8,128)(2,1)} %far_ref, bf16[3,3,3,128,128]{4,3,2,1,0:T(8,128)(2,1)S(1)} %get-tuple-element.43.we_ref), custom_call_target="tpu_custom_call" | custom-call | tf_op jit(solution)/shard_map/fetch/pallas_call | solution.py:537
  19.0 0.4 %collective-permute-done.6.got_ref = bf16[320,128]{1,0:T(8,128)(2,1)S(1)} collective-permute-done((bf16[320,128]{1,0:T(8,128)(2,1)S(1)}, bf16[320,128]{1,0:T(8,128)(2,1)S(1)}, u32[]{:S(2)}, u32[]{:S(2)}) %collective-permute-start.6) | collective-permute-done | bytes 81952 | tf_op jit(solution)/shard_map/ppermute | solution.py:528
  19.4 0.9 %late.1 = (bf16[256,128]{1,0:T(8,128)(2,1)S(1)}, f32[256,256]{1,0:T(8,128)S(1)}, f32[64,128]{1,0:T(8,128)S(1)}) custom-call(bf16[320,128]{1,0:T(8,128)(2,1)S(1)} %get-tuple-element.40.sent_ref, bf16[320,128]{1,0:T(8,128)(2,1)S(1)} %collective-permute-done.6.got_ref, f32[192,128]{1,0:T(8,128)S(1)} %get-tuple-element.41.edge_ref, ...), custom_call_target="tpu_custom_call" | custom-call | tf_op jit(solution)/shard_map/late/pallas_call | solution.py:537
  20.3 0.0 collective-permute-done.5.refs_3_
  20.3 0.0 copy-done
  20.3 0.8 %late_back.1 = (bf16[256,384]{1,0:T(8,128)(2,1)S(1)}, bf16[256,128]{1,0:T(8,128)(2,1)S(1)}, f32[256,128]{1,0:T(8,128)S(1)}) custom-call(bf16[16,4,256]{2,1,0:T(4,128)(2,1)S(1)} %bitcast.7, bf16[16,4,256]{2,1,0:T(4,128)(2,1)S(1)} %collective-permute-done.3.refs_1_, bf16[16,4,256]{2,1,0:T(4,128)(2,1)S(1)} %collective-permute-done.4.refs_2_, ...), custom_call_target="tpu_custom_call" | custom-call | tf_op jit(solution)/shard_map/late_back/pallas_call | solution.py:537
  21.2 0.1 collective-permute-start.8
  21.2 1.5 %collective-permute-start.9 = (bf16[256,128]{1,0:T(8,128)(2,1)S(1)}, bf16[256,128]{1,0:T(8,128)(2,1)S(1)}, u32[]{:S(2)}, u32[]{:S(2)}) collective-permute-start(bf16[256,128]{1,0:T(8,128)(2,1)S(1)} %get-tuple-element.50), channel_id=1, source_target_pairs={{0,2},{2,0},{1,3},{3,1},{4,6},{6,4},{5,7},{7,5},{8,10},{10,8},{9,1... | collective-permute-start | bytes 196616 | tf_op jit(solution)/shard_map/ppermute | solution.py:528
  22.8 0.0 collective-permute-done.8.other_ref
  22.8 1.2 %late_grad.1.late_ref = bf16[3456,256]{1,0:T(8,128)(2,1)S(1)} custom-call(bf16[256,384]{1,0:T(8,128)(2,1)S(1)} %get-tuple-element.51.mine_ref, bf16[256,384]{1,0:T(8,128)(2,1)S(1)} %collective-permute-done.8.other_ref), custom_call_target="tpu_custom_call" | custom-call | tf_op jit(solution)/shard_map/late_grad/pallas_call | solution.py:537
  24.0 0.0 collective-permute-done.7.got_ref
  24.0 2.1 %other.1 = (bf16[2048,1152]{1,0:T(8,128)(2,1)S(1)}, f32[1024,128]{1,0:T(8,128)S(1)}) custom-call(bf16[1024,128]{1,0:T(8,128)(2,1)S(1)} %get-tuple-element.49.half_ref, bf16[1024,128]{1,0:T(8,128)(2,1)S(1)} %collective-permute-done.7.got_ref, bf16[1152,384]{1,0:T(8,128)(2,1)S(1)} %get-tuple-element.56.refs_4_.wcat_ref), custom_call_target="tpu_custom_call" | custom-call | tf_op jit(solution)/shard_map/other/pallas_call | solution.py:537
  26.2 0.0 collective-permute-done.9.other_ref
  26.2 1.8 %early_grad.1 = (bf16[2304,128]{1,0:T(8,128)(2,1)S(1)}, f32[4,160,128]{2,1,0:T(8,128)S(1)}, bf16[3456,256]{1,0:T(8,128)(2,1)}, bf16[384,2048]{1,0:T(8,128)(2,1)S(1)}) custom-call(f32[256,128]{1,0:T(8,128)S(1)} %get-tuple-element.53.mine_ref, bf16[256,128]{1,0:T(8,128)(2,1)S(1)} %collective-permute-done.9.other_ref, ...), custom_call_target="tpu_custom_call" | custom-call | tf_op jit(solution)/shard_map/early_grad/pallas_call | solution.py:537
  28.0 0.2 collective-permute-start.10
  28.2 1.0 %more.1.two_ref = bf16[1152,128]{1,0:T(8,128)(2,1)S(1)} custom-call(bf16[384,2048]{1,0:T(8,128)(2,1)S(1)} %get-tuple-element.62.left_ref, bf16[2048,1152]{1,0:T(8,128)(2,1)S(1)} %get-tuple-element.59.col_ref), custom_call_target="tpu_custom_call" | custom-call | tf_op jit(solution)/shard_map/more/pallas_call | solution.py:537
  29.3 0.4 %collective-permute-start.11 = (bf16[1152,128]{1,0:T(8,128)(2,1)S(1)}, bf16[1152,128]{1,0:T(8,128)(2,1)S(1)}, u32[]{:S(2)}, u32[]{:S(2)}) collective-permute-start(bf16[1152,128]{1,0:T(8,128)(2,1)S(1)} %more.1.two_ref), channel_id=1, source_target_pairs={{0,1},{1,0},{2,3},{3,2},{4,5},{5,4},{6,7},{7,6},{8,9},{9,8},{10,11... | collective-permute-start | bytes 884744 | tf_op jit(solution)/shard_map/ppermute | solution.py:528
  29.7 1.3 %grad_volume.1 = bf16[256,128]{1,0:T(8,128)(2,1)} custom-call(f32[4,160,128]{2,1,0:T(8,128)S(1)} %get-tuple-element.65.win_ref, bf16[3,1152,128]{2,1,0:T(8,128)(2,1)S(1)} %get-tuple-element.66.wt_ref), custom_call_target="tpu_custom_call" | custom-call | tf_op jit(solution)/shard_map/grad_volume/pallas_call | solution.py:537
  30.9 0.0 collective-permute-done.11.two_got_ref
  30.9 0.0 collective-permute-done.10.one_got_ref
  30.9 1.0 %finish.1 = bf16[3456,128]{1,0:T(8,128)(2,1)} custom-call(bf16[2304,128]{1,0:T(8,128)(2,1)S(1)} %get-tuple-element.61.one_ref, bf16[2304,128]{1,0:T(8,128)(2,1)S(1)} %collective-permute-done.10.one_got_ref, bf16[1152,128]{1,0:T(8,128)(2,1)S(1)} %more.1.two_ref, bf16[1152,128]{1,0:T(8,128)(2,1)S(1)} %collective-permute-done.11.two_got_ref), custom_call_target="tpu_custom_call" | custom-call | tf_op jit(solution)/shard_map/finish/pallas_call | solution.py:537
Async XLA Ops:
  0.6 11.3 %collective-permute-start.2 = (bf16[256,128]{1,0:T(8,128)(2,1)}, bf16[256,128]{1,0:T(8,128)(2,1)S(1)}, u32[]{:S(2)}, u32[]{:S(2)}) collective-permute-start(bf16[256,128]{1,0:T(8,128)(2,1)} %bitcast.10), channel_id=1, source_target_pairs={{0,12},{4,8},{8,4},{12,0},{1,13},{5,9},{9,5},{13,1},{2,14},{6,10},... | collective-permute-start | bytes 196616 | tf_op jit(solution)/shard_map/ppermute | solution.py:528
  5.7 6.5 %collective-permute-start.1 = (bf16[256,128]{1,0:T(8,128)(2,1)}, bf16[256,128]{1,0:T(8,128)(2,1)S(1)}, u32[]{:S(2)}, u32[]{:S(2)}) collective-permute-start(bf16[256,128]{1,0:T(8,128)(2,1)} %bitcast.11), channel_id=1, source_target_pairs={{0,8},{4,12},{8,0},{12,4},{1,9},{5,13},{9,1},{13,5},{2,10},{6,14},... | collective-permute-start | bytes 196616 | tf_op jit(solution)/shard_map/ppermute | solution.py:528
  5.7 6.5 %collective-permute-start = (bf16[256,128]{1,0:T(8,128)(2,1)}, bf16[256,128]{1,0:T(8,128)(2,1)S(1)}, u32[]{:S(2)}, u32[]{:S(2)}) collective-permute-start(bf16[256,128]{1,0:T(8,128)(2,1)} %bitcast.12), channel_id=1, source_target_pairs={{0,4},{4,0},{8,12},{12,8},{1,5},{5,1},{9,13},{13,9},{2,6},{6,2},{1... | collective-permute-start | bytes 196616 | tf_op jit(solution)/shard_map/ppermute | solution.py:528
  6.4 7.6 %collective-permute-start.4 = (bf16[16,4,256]{2,1,0:T(4,128)(2,1)}, bf16[16,4,256]{2,1,0:T(4,128)(2,1)S(1)}, u32[]{:S(2)}, u32[]{:S(2)}) collective-permute-start(bf16[16,4,256]{2,1,0:T(4,128)(2,1)} %bitcast.5), channel_id=1, source_target_pairs={{0,8},{4,12},{8,0},{12,4},{1,9},{5,13},{9,1},{13,5},{2,10},{6,14},... | collective-permute-start | bytes 98312 | tf_op jit(solution)/shard_map/ppermute | solution.py:528
  8.7 5.4 %collective-permute-start.3 = (bf16[16,4,256]{2,1,0:T(4,128)(2,1)}, bf16[16,4,256]{2,1,0:T(4,128)(2,1)S(1)}, u32[]{:S(2)}, u32[]{:S(2)}) collective-permute-start(bf16[16,4,256]{2,1,0:T(4,128)(2,1)} %bitcast.6), channel_id=1, source_target_pairs={{0,4},{4,0},{8,12},{12,8},{1,5},{5,1},{9,13},{13,9},{2,6},{6,2},{1... | collective-permute-start | bytes 98312 | tf_op jit(solution)/shard_map/ppermute | solution.py:528
  14.0 5.4 %collective-permute-start.6 = (bf16[320,128]{1,0:T(8,128)(2,1)S(1)}, bf16[320,128]{1,0:T(8,128)(2,1)S(1)}, u32[]{:S(2)}, u32[]{:S(2)}) collective-permute-start(bf16[320,128]{1,0:T(8,128)(2,1)S(1)} %get-tuple-element.40.sent_ref), channel_id=1, source_target_pairs={{0,2},{2,0},{1,3},{3,1},{4,6},{6,4},{5,7},{7,5},{8,10},{10,8},{9,1... | collective-permute-start | bytes 245768 | tf_op jit(solution)/shard_map/ppermute | solution.py:528
  15.5 8.5 %collective-permute-start.7 = (bf16[1024,128]{1,0:T(8,128)(2,1)S(1)}, bf16[1024,128]{1,0:T(8,128)(2,1)S(1)}, u32[]{:S(2)}, u32[]{:S(2)}) collective-permute-start(bf16[1024,128]{1,0:T(8,128)(2,1)S(1)} %get-tuple-element.49.half_ref), channel_id=1, source_target_pairs={{0,2},{2,0},{1,3},{3,1},{4,6},{6,4},{5,7},{7,5},{8,10},{10,8},{9,1... | collective-permute-start | bytes 786440 | tf_op jit(solution)/shard_map/ppermute | solution.py:528
  16.1 4.2 %collective-permute-start.5 = (bf16[16,4,256]{2,1,0:T(4,128)(2,1)S(1)}, bf16[16,4,256]{2,1,0:T(4,128)(2,1)S(1)}, u32[]{:S(2)}, u32[]{:S(2)}) collective-permute-start(bf16[16,4,256]{2,1,0:T(4,128)(2,1)S(1)} %collective-permute-done.4.refs_2_), channel_id=1, source_target_pairs={{0,4},{4,0},{8,12},{12,8},{1,5},{5,1},{9,13},{13,9},{2,6},{6,2},{1... | collective-permute-start | bytes 98312 | tf_op jit(solution)/shard_map/ppermute | solution.py:528
  17.2 3.1 %copy-start = (bf16[1,1,16,4,256]{4,3,2,1,0:T(4,128)(2,1)S(1)}, bf16[1,1,16,4,256]{4,3,2,1,0:T(4,128)(2,1)}, u32[]{:S(2)}) copy-start(bf16[1,1,16,4,256]{4,3,2,1,0:T(4,128)(2,1)} %param.7) | copy-start | bytes 98308
  21.2 1.6 %collective-permute-start.8 = (bf16[256,384]{1,0:T(8,128)(2,1)S(1)}, bf16[256,384]{1,0:T(8,128)(2,1)S(1)}, u32[]{:S(2)}, u32[]{:S(2)}) collective-permute-start(bf16[256,384]{1,0:T(8,128)(2,1)S(1)} %get-tuple-element.51.mine_ref), channel_id=1, source_target_pairs={{0,1},{1,0},{2,3},{3,2},{4,5},{5,4},{6,7},{7,6},{8,9},{9,8},{10,11... | collective-permute-start | bytes 589832 | tf_op jit(solution)/shard_map/ppermute | solution.py:528
  21.2 4.9 %collective-permute-start.9 = (bf16[256,128]{1,0:T(8,128)(2,1)S(1)}, bf16[256,128]{1,0:T(8,128)(2,1)S(1)}, u32[]{:S(2)}, u32[]{:S(2)}) collective-permute-start(bf16[256,128]{1,0:T(8,128)(2,1)S(1)} %get-tuple-element.50), channel_id=1, source_target_pairs={{0,2},{2,0},{1,3},{3,1},{4,6},{6,4},{5,7},{7,5},{8,10},{10,8},{9,1... | collective-permute-start | bytes 196616 | tf_op jit(solution)/shard_map/ppermute | solution.py:528
  28.0 3.0 %collective-permute-start.10 = (bf16[2304,128]{1,0:T(8,128)(2,1)S(1)}, bf16[2304,128]{1,0:T(8,128)(2,1)S(1)}, u32[]{:S(2)}, u32[]{:S(2)}) collective-permute-start(bf16[2304,128]{1,0:T(8,128)(2,1)S(1)} %get-tuple-element.61.one_ref), channel_id=1, source_target_pairs={{0,1},{1,0},{2,3},{3,2},{4,5},{5,4},{6,7},{7,6},{8,9},{9,8},{10,11... | collective-permute-start | bytes 1769480 | tf_op jit(solution)/shard_map/ppermute | solution.py:528
  29.3 1.7 %collective-permute-start.11 = (bf16[1152,128]{1,0:T(8,128)(2,1)S(1)}, bf16[1152,128]{1,0:T(8,128)(2,1)S(1)}, u32[]{:S(2)}, u32[]{:S(2)}) collective-permute-start(bf16[1152,128]{1,0:T(8,128)(2,1)S(1)} %more.1.two_ref), channel_id=1, source_target_pairs={{0,1},{1,0},{2,3},{3,2},{4,5},{5,4},{6,7},{7,6},{8,9},{9,8},{10,11... | collective-permute-start | bytes 884744 | tf_op jit(solution)/shard_map/ppermute | solution.py:528

commit v11 on v10

--- a/solution.py
+++ b/solution.py
@@ -12,7 +12,7 @@
 F32 = jnp.float32
 VMEM_BYTES = 14 * 2**20
 GATHER_BLOCKS = 8
-EARLY_TAPS = 6
+EARLY_TAPS = 7
 
 
 def padded_2(block, sides, width):

time: 32.1 us -> 32 us (level)
  transfers between devices with their start and end apart: 12 -> 12, of which waited for: 2 -> 2; matrix products, arithmetic and copies ran while one was open for 0% -> 0% of each run, Pallas kernels for 38% -> 37%
where the time goes in v11:
time: 32 us; the launch traced here: 31.9 us
  starting transfers between devices  15.5 us (48%)
  Pallas kernels  14.9 us (47%)
  between operations  0.75 us (2%)
  waiting for transfers between devices  0.73 us (2%)
    ppermute x12, starting transfers between devices, turned(): lax.ppermute(value, axis, [(i, i ^ by if pairs else (i + by) % count) for...  15.5 us
    pallas_call x11, Pallas kernels, call(): pl.pallas_call(kernel, out_shape=outs, in_specs=[pl.BlockSpec(memory_spac...  14.9 us
    ppermute x12, waiting for transfers between devices, turned(): lax.ppermute(value, axis, [(i, i ^ by if pairs else (i + by) % count) for...  0.73 us
  transfers between devices with their start and end apart: 12, of which 2 were waited for; matrix products, arithmetic and copies ran while one was open for 0% of the time, Pallas kernels for 37%

profile of v11, /device:TPU:0, one launch (start us, length us, event | category | flops | bytes accessed | tf_op | source)
XLA Modules:
  0.0 31.9 jit_solution(7547091618951803935)
XLA Ops:
  0.6 5.1 %collective-permute-start.2 = (bf16[256,128]{1,0:T(8,128)(2,1)}, bf16[256,128]{1,0:T(8,128)(2,1)S(1)}, u32[]{:S(2)}, u32[]{:S(2)}) collective-permute-start(bf16[256,128]{1,0:T(8,128)(2,1)} %bitcast.10), channel_id=1, source_target_pairs={{0,12},{4,8},{8,4},{12,0},{1,13},{5,9},{9,5},{13,1},{2,14},{6,10},... | collective-permute-start | bytes 196616 | tf_op jit(solution)/shard_map/ppermute | solution.py:528
  5.7 0.0 collective-permute-start.1
  5.7 0.6 %collective-permute-start = (bf16[256,128]{1,0:T(8,128)(2,1)}, bf16[256,128]{1,0:T(8,128)(2,1)S(1)}, u32[]{:S(2)}, u32[]{:S(2)}) collective-permute-start(bf16[256,128]{1,0:T(8,128)(2,1)} %bitcast.12), channel_id=1, source_target_pairs={{0,4},{4,0},{8,12},{12,8},{1,5},{5,1},{9,13},{13,9},{2,6},{6,2},{1... | collective-permute-start | bytes 196616 | tf_op jit(solution)/shard_map/ppermute | solution.py:528
  6.4 2.3 %collective-permute-start.4 = (bf16[16,4,256]{2,1,0:T(4,128)(2,1)}, bf16[16,4,256]{2,1,0:T(4,128)(2,1)S(1)}, u32[]{:S(2)}, u32[]{:S(2)}) collective-permute-start(bf16[16,4,256]{2,1,0:T(4,128)(2,1)} %bitcast.5), channel_id=1, source_target_pairs={{0,8},{4,12},{8,0},{12,4},{1,9},{5,13},{9,1},{13,5},{2,10},{6,14},... | collective-permute-start | bytes 98312 | tf_op jit(solution)/shard_map/ppermute | solution.py:528
  8.7 2.0 %collective-permute-start.3 = (bf16[16,4,256]{2,1,0:T(4,128)(2,1)}, bf16[16,4,256]{2,1,0:T(4,128)(2,1)S(1)}, u32[]{:S(2)}, u32[]{:S(2)}) collective-permute-start(bf16[16,4,256]{2,1,0:T(4,128)(2,1)} %bitcast.6), channel_id=1, source_target_pairs={{0,4},{4,0},{8,12},{12,8},{1,5},{5,1},{9,13},{13,9},{2,6},{6,2},{1... | collective-permute-start | bytes 98312 | tf_op jit(solution)/shard_map/ppermute | solution.py:528
  10.7 1.2 %begin.1 = (bf16[256,128]{1,0:T(8,128)(2,1)S(1)}, bf16[3,3,3,128,128]{4,3,2,1,0:T(8,128)(2,1)S(1)}, bf16[1152,384]{1,0:T(8,128)(2,1)S(1)}) custom-call(bf16[256,128]{1,0:T(8,128)(2,1)} %bitcast.13, bf16[3,3,3,128,128]{4,3,2,1,0:T(8,128)(2,1)} %we_hbm.1), custom_call_target="tpu_custom_call" | custom-call | tf_op jit(solution)/shard_map/begin/pallas_call | solution.py:537
  11.9 0.0 collective-permute-done.2.refs_3_
  11.9 0.3 %collective-permute-done.1.refs_2_ = bf16[256,128]{1,0:T(8,128)(2,1)S(1)} collective-permute-done((bf16[256,128]{1,0:T(8,128)(2,1)}, bf16[256,128]{1,0:T(8,128)(2,1)S(1)}, u32[]{:S(2)}, u32[]{:S(2)}) %collective-permute-start.1) | collective-permute-done | bytes 65568 | tf_op jit(solution)/shard_map/ppermute | solution.py:528
  12.3 0.0 collective-permute-done.refs_1_
  12.3 1.8 %early.1 = (bf16[1024,128]{1,0:T(8,128)(2,1)S(1)}, f32[1024,128]{1,0:T(8,128)S(1)}, bf16[320,128]{1,0:T(8,128)(2,1)S(1)}, f32[192,128]{1,0:T(8,128)S(1)}) custom-call(bf16[256,128]{1,0:T(8,128)(2,1)S(1)} %get-tuple-element.35.refs_0_, bf16[256,128]{1,0:T(8,128)(2,1)S(1)} %collective-permute-done.refs_1_, ...), custom_call_target="tpu_custom_call" | custom-call | tf_op jit(solution)/shard_map/early/pallas_call | solution.py:537
  14.0 0.0 collective-permute-done.4.refs_2_
  14.0 0.0 collective-permute-done.3.refs_1_
  14.0 1.5 %collective-permute-start.6 = (bf16[320,128]{1,0:T(8,128)(2,1)S(1)}, bf16[320,128]{1,0:T(8,128)(2,1)S(1)}, u32[]{:S(2)}, u32[]{:S(2)}) collective-permute-start(bf16[320,128]{1,0:T(8,128)(2,1)S(1)} %get-tuple-element.40.sent_ref), channel_id=1, source_target_pairs={{0,2},{2,0},{1,3},{3,1},{4,6},{6,4},{5,7},{7,5},{8,10},{10,8},{9,1... | collective-permute-start | bytes 245768 | tf_op jit(solution)/shard_map/ppermute | solution.py:528
  15.5 0.6 %collective-permute-start.7 = (bf16[1024,128]{1,0:T(8,128)(2,1)S(1)}, bf16[1024,128]{1,0:T(8,128)(2,1)S(1)}, u32[]{:S(2)}, u32[]{:S(2)}) collective-permute-start(bf16[1024,128]{1,0:T(8,128)(2,1)S(1)} %get-tuple-element.49.half_ref), channel_id=1, source_target_pairs={{0,2},{2,0},{1,3},{3,1},{4,6},{6,4},{5,7},{7,5},{8,10},{10,8},{9,1... | collective-permute-start | bytes 786440 | tf_op jit(solution)/shard_map/ppermute | solution.py:528
  16.1 1.1 %collective-permute-start.5 = (bf16[16,4,256]{2,1,0:T(4,128)(2,1)S(1)}, bf16[16,4,256]{2,1,0:T(4,128)(2,1)S(1)}, u32[]{:S(2)}, u32[]{:S(2)}) collective-permute-start(bf16[16,4,256]{2,1,0:T(4,128)(2,1)S(1)} %collective-permute-done.4.refs_2_), channel_id=1, source_target_pairs={{0,4},{4,0},{8,12},{12,8},{1,5},{5,1},{9,13},{13,9},{2,6},{6,2},{1... | collective-permute-start | bytes 98312 | tf_op jit(solution)/shard_map/ppermute | solution.py:528
  17.2 0.0 copy-start
  17.2 1.8 %fetch.1 = (bf16[3,3,3,128,256]{4,3,2,1,0:T(8,128)(2,1)S(1)}, bf16[2304,384]{1,0:T(8,128)(2,1)S(1)}, bf16[3,1152,128]{2,1,0:T(8,128)(2,1)S(1)}) custom-call(bf16[3,3,3,128,256]{4,3,2,1,0:T(8,128)(2,1)} %far_ref, bf16[3,3,3,128,128]{4,3,2,1,0:T(8,128)(2,1)S(1)} %get-tuple-element.43.we_ref), custom_call_target="tpu_custom_call" | custom-call | tf_op jit(solution)/shard_map/fetch/pallas_call | solution.py:537
  19.0 0.4 %collective-permute-done.6.got_ref = bf16[320,128]{1,0:T(8,128)(2,1)S(1)} collective-permute-done((bf16[320,128]{1,0:T(8,128)(2,1)S(1)}, bf16[320,128]{1,0:T(8,128)(2,1)S(1)}, u32[]{:S(2)}, u32[]{:S(2)}) %collective-permute-start.6) | collective-permute-done | bytes 81952 | tf_op jit(solution)/shard_map/ppermute | solution.py:528
  19.4 0.9 %late.1 = (bf16[256,128]{1,0:T(8,128)(2,1)S(1)}, f32[256,256]{1,0:T(8,128)S(1)}, f32[64,128]{1,0:T(8,128)S(1)}) custom-call(bf16[320,128]{1,0:T(8,128)(2,1)S(1)} %get-tuple-element.40.sent_ref, bf16[320,128]{1,0:T(8,128)(2,1)S(1)} %collective-permute-done.6.got_ref, f32[192,128]{1,0:T(8,128)S(1)} %get-tuple-element.41.edge_ref, ...), custom_call_target="tpu_custom_call" | custom-call | tf_op jit(solution)/shard_map/late/pallas_call | solution.py:537
  20.3 0.0 collective-permute-done.5.refs_3_
  20.3 0.0 copy-done
  20.3 0.8 %late_back.1 = (bf16[256,384]{1,0:T(8,128)(2,1)S(1)}, bf16[256,128]{1,0:T(8,128)(2,1)S(1)}, f32[256,128]{1,0:T(8,128)S(1)}) custom-call(bf16[16,4,256]{2,1,0:T(4,128)(2,1)S(1)} %bitcast.7, bf16[16,4,256]{2,1,0:T(4,128)(2,1)S(1)} %collective-permute-done.3.refs_1_, bf16[16,4,256]{2,1,0:T(4,128)(2,1)S(1)} %collective-permute-done.4.refs_2_, ...), custom_call_target="tpu_custom_call" | custom-call | tf_op jit(solution)/shard_map/late_back/pallas_call | solution.py:537
  21.2 0.1 collective-permute-start.8
  21.2 1.5 %collective-permute-start.9 = (bf16[256,128]{1,0:T(8,128)(2,1)S(1)}, bf16[256,128]{1,0:T(8,128)(2,1)S(1)}, u32[]{:S(2)}, u32[]{:S(2)}) collective-permute-start(bf16[256,128]{1,0:T(8,128)(2,1)S(1)} %get-tuple-element.50), channel_id=1, source_target_pairs={{0,2},{2,0},{1,3},{3,1},{4,6},{6,4},{5,7},{7,5},{8,10},{10,8},{9,1... | collective-permute-start | bytes 196616 | tf_op jit(solution)/shard_map/ppermute | solution.py:528
  22.8 0.0 collective-permute-done.8.other_ref
  22.8 1.2 %late_grad.1.late_ref = bf16[3456,256]{1,0:T(8,128)(2,1)S(1)} custom-call(bf16[256,384]{1,0:T(8,128)(2,1)S(1)} %get-tuple-element.51.mine_ref, bf16[256,384]{1,0:T(8,128)(2,1)S(1)} %collective-permute-done.8.other_ref), custom_call_target="tpu_custom_call" | custom-call | tf_op jit(solution)/shard_map/late_grad/pallas_call | solution.py:537
  24.0 0.0 collective-permute-done.7.got_ref
  24.0 2.1 %other.1 = (bf16[2048,1152]{1,0:T(8,128)(2,1)S(1)}, f32[1024,128]{1,0:T(8,128)S(1)}) custom-call(bf16[1024,128]{1,0:T(8,128)(2,1)S(1)} %get-tuple-element.49.half_ref, bf16[1024,128]{1,0:T(8,128)(2,1)S(1)} %collective-permute-done.7.got_ref, bf16[1152,384]{1,0:T(8,128)(2,1)S(1)} %get-tuple-element.56.refs_4_.wcat_ref), custom_call_target="tpu_custom_call" | custom-call | tf_op jit(solution)/shard_map/other/pallas_call | solution.py:537
  26.2 0.0 collective-permute-done.9.other_ref
  26.2 2.1 %early_grad.1 = (bf16[2688,128]{1,0:T(8,128)(2,1)S(1)}, f32[4,160,128]{2,1,0:T(8,128)S(1)}, bf16[3456,256]{1,0:T(8,128)(2,1)}, bf16[384,2048]{1,0:T(8,128)(2,1)S(1)}) custom-call(f32[256,128]{1,0:T(8,128)S(1)} %get-tuple-element.53.mine_ref, bf16[256,128]{1,0:T(8,128)(2,1)S(1)} %collective-permute-done.9.other_ref, ...), custom_call_target="tpu_custom_call" | custom-call | tf_op jit(solution)/shard_map/early_grad/pallas_call | solution.py:537
  28.3 0.2 collective-permute-start.10
  28.5 0.6 %more.1.two_ref = bf16[768,128]{1,0:T(8,128)(2,1)S(1)} custom-call(bf16[384,2048]{1,0:T(8,128)(2,1)S(1)} %get-tuple-element.62.left_ref, bf16[2048,1152]{1,0:T(8,128)(2,1)S(1)} %get-tuple-element.59.col_ref), custom_call_target="tpu_custom_call" | custom-call | tf_op jit(solution)/shard_map/more/pallas_call | solution.py:537
  29.2 0.4 %collective-permute-start.11 = (bf16[768,128]{1,0:T(8,128)(2,1)S(1)}, bf16[768,128]{1,0:T(8,128)(2,1)S(1)}, u32[]{:S(2)}, u32[]{:S(2)}) collective-permute-start(bf16[768,128]{1,0:T(8,128)(2,1)S(1)} %more.1.two_ref), channel_id=1, source_target_pairs={{0,1},{1,0},{2,3},{3,2},{4,5},{5,4},{6,7},{7,6},{8,9},{9,8},{10,11... | collective-permute-start | bytes 589832 | tf_op jit(solution)/shard_map/ppermute | solution.py:528
  29.6 1.3 %grad_volume.1 = bf16[256,128]{1,0:T(8,128)(2,1)} custom-call(f32[4,160,128]{2,1,0:T(8,128)S(1)} %get-tuple-element.65.win_ref, bf16[3,1152,128]{2,1,0:T(8,128)(2,1)S(1)} %get-tuple-element.66.wt_ref), custom_call_target="tpu_custom_call" | custom-call | tf_op jit(solution)/shard_map/grad_volume/pallas_call | solution.py:537
  30.8 0.0 collective-permute-done.11.two_got_ref
  30.8 0.0 collective-permute-done.10.one_got_ref
  30.8 1.0 %finish.1 = bf16[3456,128]{1,0:T(8,128)(2,1)} custom-call(bf16[2688,128]{1,0:T(8,128)(2,1)S(1)} %get-tuple-element.61.one_ref, bf16[2688,128]{1,0:T(8,128)(2,1)S(1)} %collective-permute-done.10.one_got_ref, bf16[768,128]{1,0:T(8,128)(2,1)S(1)} %more.1.two_ref, bf16[768,128]{1,0:T(8,128)(2,1)S(1)} %collective-permute-done.11.two_got_ref), custom_call_target="tpu_custom_call" | custom-call | tf_op jit(solution)/shard_map/finish/pallas_call | solution.py:537
Async XLA Ops:
  0.6 11.3 %collective-permute-start.2 = (bf16[256,128]{1,0:T(8,128)(2,1)}, bf16[256,128]{1,0:T(8,128)(2,1)S(1)}, u32[]{:S(2)}, u32[]{:S(2)}) collective-permute-start(bf16[256,128]{1,0:T(8,128)(2,1)} %bitcast.10), channel_id=1, source_target_pairs={{0,12},{4,8},{8,4},{12,0},{1,13},{5,9},{9,5},{13,1},{2,14},{6,10},... | collective-permute-start | bytes 196616 | tf_op jit(solution)/shard_map/ppermute | solution.py:528
  5.7 6.5 %collective-permute-start.1 = (bf16[256,128]{1,0:T(8,128)(2,1)}, bf16[256,128]{1,0:T(8,128)(2,1)S(1)}, u32[]{:S(2)}, u32[]{:S(2)}) collective-permute-start(bf16[256,128]{1,0:T(8,128)(2,1)} %bitcast.11), channel_id=1, source_target_pairs={{0,8},{4,12},{8,0},{12,4},{1,9},{5,13},{9,1},{13,5},{2,10},{6,14},... | collective-permute-start | bytes 196616 | tf_op jit(solution)/shard_map/ppermute | solution.py:528
  5.7 6.5 %collective-permute-start = (bf16[256,128]{1,0:T(8,128)(2,1)}, bf16[256,128]{1,0:T(8,128)(2,1)S(1)}, u32[]{:S(2)}, u32[]{:S(2)}) collective-permute-start(bf16[256,128]{1,0:T(8,128)(2,1)} %bitcast.12), channel_id=1, source_target_pairs={{0,4},{4,0},{8,12},{12,8},{1,5},{5,1},{9,13},{13,9},{2,6},{6,2},{1... | collective-permute-start | bytes 196616 | tf_op jit(solution)/shard_map/ppermute | solution.py:528
  6.4 7.6 %collective-permute-start.4 = (bf16[16,4,256]{2,1,0:T(4,128)(2,1)}, bf16[16,4,256]{2,1,0:T(4,128)(2,1)S(1)}, u32[]{:S(2)}, u32[]{:S(2)}) collective-permute-start(bf16[16,4,256]{2,1,0:T(4,128)(2,1)} %bitcast.5), channel_id=1, source_target_pairs={{0,8},{4,12},{8,0},{12,4},{1,9},{5,13},{9,1},{13,5},{2,10},{6,14},... | collective-permute-start | bytes 98312 | tf_op jit(solution)/shard_map/ppermute | solution.py:528
  8.7 5.4 %collective-permute-start.3 = (bf16[16,4,256]{2,1,0:T(4,128)(2,1)}, bf16[16,4,256]{2,1,0:T(4,128)(2,1)S(1)}, u32[]{:S(2)}, u32[]{:S(2)}) collective-permute-start(bf16[16,4,256]{2,1,0:T(4,128)(2,1)} %bitcast.6), channel_id=1, source_target_pairs={{0,4},{4,0},{8,12},{12,8},{1,5},{5,1},{9,13},{13,9},{2,6},{6,2},{1... | collective-permute-start | bytes 98312 | tf_op jit(solution)/shard_map/ppermute | solution.py:528
  14.0 5.4 %collective-permute-start.6 = (bf16[320,128]{1,0:T(8,128)(2,1)S(1)}, bf16[320,128]{1,0:T(8,128)(2,1)S(1)}, u32[]{:S(2)}, u32[]{:S(2)}) collective-permute-start(bf16[320,128]{1,0:T(8,128)(2,1)S(1)} %get-tuple-element.40.sent_ref), channel_id=1, source_target_pairs={{0,2},{2,0},{1,3},{3,1},{4,6},{6,4},{5,7},{7,5},{8,10},{10,8},{9,1... | collective-permute-start | bytes 245768 | tf_op jit(solution)/shard_map/ppermute | solution.py:528
  15.5 8.5 %collective-permute-start.7 = (bf16[1024,128]{1,0:T(8,128)(2,1)S(1)}, bf16[1024,128]{1,0:T(8,128)(2,1)S(1)}, u32[]{:S(2)}, u32[]{:S(2)}) collective-permute-start(bf16[1024,128]{1,0:T(8,128)(2,1)S(1)} %get-tuple-element.49.half_ref), channel_id=1, source_target_pairs={{0,2},{2,0},{1,3},{3,1},{4,6},{6,4},{5,7},{7,5},{8,10},{10,8},{9,1... | collective-permute-start | bytes 786440 | tf_op jit(solution)/shard_map/ppermute | solution.py:528
  16.1 4.2 %collective-permute-start.5 = (bf16[16,4,256]{2,1,0:T(4,128)(2,1)S(1)}, bf16[16,4,256]{2,1,0:T(4,128)(2,1)S(1)}, u32[]{:S(2)}, u32[]{:S(2)}) collective-permute-start(bf16[16,4,256]{2,1,0:T(4,128)(2,1)S(1)} %collective-permute-done.4.refs_2_), channel_id=1, source_target_pairs={{0,4},{4,0},{8,12},{12,8},{1,5},{5,1},{9,13},{13,9},{2,6},{6,2},{1... | collective-permute-start | bytes 98312 | tf_op jit(solution)/shard_map/ppermute | solution.py:528
  17.2 3.1 %copy-start = (bf16[1,1,16,4,256]{4,3,2,1,0:T(4,128)(2,1)S(1)}, bf16[1,1,16,4,256]{4,3,2,1,0:T(4,128)(2,1)}, u32[]{:S(2)}) copy-start(bf16[1,1,16,4,256]{4,3,2,1,0:T(4,128)(2,1)} %param.7) | copy-start | bytes 98308
  21.2 1.6 %collective-permute-start.8 = (bf16[256,384]{1,0:T(8,128)(2,1)S(1)}, bf16[256,384]{1,0:T(8,128)(2,1)S(1)}, u32[]{:S(2)}, u32[]{:S(2)}) collective-permute-start(bf16[256,384]{1,0:T(8,128)(2,1)S(1)} %get-tuple-element.51.mine_ref), channel_id=1, source_target_pairs={{0,1},{1,0},{2,3},{3,2},{4,5},{5,4},{6,7},{7,6},{8,9},{9,8},{10,11... | collective-permute-start | bytes 589832 | tf_op jit(solution)/shard_map/ppermute | solution.py:528
  21.2 4.9 %collective-permute-start.9 = (bf16[256,128]{1,0:T(8,128)(2,1)S(1)}, bf16[256,128]{1,0:T(8,128)(2,1)S(1)}, u32[]{:S(2)}, u32[]{:S(2)}) collective-permute-start(bf16[256,128]{1,0:T(8,128)(2,1)S(1)} %get-tuple-element.50), channel_id=1, source_target_pairs={{0,2},{2,0},{1,3},{3,1},{4,6},{6,4},{5,7},{7,5},{8,10},{10,8},{9,1... | collective-permute-start | bytes 196616 | tf_op jit(solution)/shard_map/ppermute | solution.py:528
  28.3 2.5 %collective-permute-start.10 = (bf16[2688,128]{1,0:T(8,128)(2,1)S(1)}, bf16[2688,128]{1,0:T(8,128)(2,1)S(1)}, u32[]{:S(2)}, u32[]{:S(2)}) collective-permute-start(bf16[2688,128]{1,0:T(8,128)(2,1)S(1)} %get-tuple-element.61.one_ref), channel_id=1, source_target_pairs={{0,1},{1,0},{2,3},{3,2},{4,5},{5,4},{6,7},{7,6},{8,9},{9,8},{10,11... | collective-permute-start | bytes 2064392 | tf_op jit(solution)/shard_map/ppermute | solution.py:528
  29.2 1.7 %collective-permute-start.11 = (bf16[768,128]{1,0:T(8,128)(2,1)S(1)}, bf16[768,128]{1,0:T(8,128)(2,1)S(1)}, u32[]{:S(2)}, u32[]{:S(2)}) collective-permute-start(bf16[768,128]{1,0:T(8,128)(2,1)S(1)} %more.1.two_ref), channel_id=1, source_target_pairs={{0,1},{1,0},{2,3},{3,2},{4,5},{5,4},{6,7},{7,6},{8,9},{9,8},{10,11... | collective-permute-start | bytes 589832 | tf_op jit(solution)/shard_map/ppermute | solution.py:528
